TPU v7x, 32 devices: a whole 2x2x4 slice. The times are simulated.
32 devices in a mesh: gx: 8 (over y, x, core), vert: 4 (over z).
Axes of the slice: x: 2, y: 2, z: 4, core: 2. Of those that a mesh axis runs over, the one named last changes fastest.
Arguments:
- distribution: float32 [2, 96, 96, 1024], P(None, 'vert', None, 'gx'), may hold values from 0 to 4, as said below
- wall_type: int32 [2, 64], P(None, 'gx'), may hold values from 0 to 2
- wall_temp_index: int32 [2, 64], P(None, 'gx'), may hold values from 0 to 1
- wall_temps: float32 [2], replicated, may hold values from 0.5 to 2
- accommodation: int32 [3], replicated, may hold values from 0 to 50
Outputs:
- advanced: float32 [2, 96, 96, 1024], P(None, 'vert', None, 'gx')
Inputs may be any that keep to these rules, and one draw needn't show every extreme that they name: `distribution`: nonnegative phase-space densities.
All inputs are finite; a program needn't handle non-finite values.
Results may differ from a plain program's by a relative error of at most 0.0003.
Values sent between devices are 32-bit elements; how exact they have to be, the bound alone decides.
No kernel may reach another device: no remote copies, remote signals or barrier semaphores. Data moves between devices by JAX's collectives and lax.ppermute only.
A program may use at most 128 MiB of HBM per device.

v0:
```python
import functools
import math

import jax
import jax.numpy as jnp
from jax import lax
from jax.experimental import pallas as pl
from jax.experimental.pallas import tpu as pltpu
from jax.sharding import PartitionSpec as P


Y = 16
ITERS = 4
NTEMP = 2
NTYPE = 3
SUB = 8
LANES = 128
ROWS = 16
PART_X = 16
PART_K = LANES // PART_X
FIELDS = 9
KERNEL_VMEM = 16 * 1024 * 1024
highest = lax.Precision.HIGHEST

vmax_speed = 4.5
courant = 0.5
diffusivity_ratio = 2.0 / 3.0
relaxation_multiplier = 2.5
shear_exponent = 0.19
time_increment = courant / vmax_speed


class Sizes:
    def __init__(self, band, nx, cells, vert):
        assert cells == SUB * Y and nx % (2 * PART_X) == 0
        self.band, self.nx, self.cells, self.vert = band, nx, cells, vert
        self.nv = band * vert
        self.xg = nx // PART_X
        self.kg = -(-band // PART_K)
        self.tiles = self.xg * self.kg
        self.half = self.tiles // 2
        self.state_rows = 2 * self.tiles * cells
        self.side_rows = 2 * self.half * Y * 2 + 2 * SUB
        self.mirror_blocks = 4 * self.tiles
        self.weight = 2.0 * vmax_speed / nx * (2.0 * vmax_speed / self.nv)

    def base(self, f, t):
        return (f * self.tiles + t) * self.cells

    def side_base(self, f, t):
        return SUB + (f * self.half + t % self.half) * 2 * Y

    def mirror_index(self, d, f, t):
        return (d * 2 + f) * self.tiles + t


def node_speed(index, number):
    return vmax_speed * (2.0 * index.astype(jnp.float32) + 1.0 - number) / number


def row_speed(sz, vert_index, offset):
    lower = vert_index // 2 * sz.band + offset
    return node_speed(jnp.where(vert_index % 2 == 0, lower, sz.nv - 1 - lower), sz.nv)


def beam_weights(speed):
    s = jnp.abs(speed) * time_increment
    return -1.5 * s + 0.5 * s * s, 2.0 * s - s * s, -0.5 * s + 0.5 * s * s


def lane():
    return lax.broadcasted_iota(jnp.int32, (SUB, LANES), 1)


def sub():
    return lax.broadcasted_iota(jnp.int32, (SUB, LANES), 0)


def x_speed(sz, group):
    return node_speed(group * PART_X + lane() % PART_X, sz.nx)


def y_speed(sz, vert_index, group):
    return row_speed(sz, vert_index, group * PART_K + lane() // PART_X)


def inside(sz, group):
    if (group + 1) * PART_K <= sz.band:
        return None
    return group * PART_K + lane() // PART_X < sz.band


def masked(mask, value):
    return value if mask is None else jnp.where(mask, value, 0.0)


def real_row(parity, step):
    return jnp.where(parity == 0, Y - 1 - step, step)


def block(start):
    return pl.ds(pl.multiple_of(start, SUB), SUB)


def add_columns(vy, g, h, sums):
    p = vy * g
    q = vy * p
    r = vy * (q + h)
    new = (g, p, q, r, h)
    return new if sums is None else tuple(a + b for a, b in zip(sums, new))


def add_group(vx, sums, totals):
    t0, t1, t2, t3, u0 = sums
    a = vx * t0
    b = vx * a
    c = vx * t1
    new = (t0, a, t1, b, c, t2, u0, vx * (b + t2 + u0), vx * c + t3)
    return new if totals is None else tuple(x + y for x, y in zip(totals, new))


def put_sums(sums_ref, y, totals):
    for m, total in enumerate(totals):
        sums_ref[m, block(y * SUB), :] = total


def send(sz, vert_index, state, sums_ref, mirror, packet, right, left):
    rows = []
    for m in range(FIELDS):
        rows.append(jnp.sum(sums_ref[m].T, axis=0, keepdims=True) * sz.weight)
    n, mx, my, pxx, pxy, pyy, extra, tx, ty = rows
    even = vert_index % 2 == 0
    zero = jnp.zeros_like(n)
    rows = [n, mx, my, pxx + pyy + extra, pxx, pxy, pyy, tx, ty]
    rows += [jnp.where(even, -my, zero), jnp.where(even, zero, my)]
    rows += [zero] * (ROWS - len(rows))
    for r, value in enumerate(rows):
        packet[r : r + 1, :] = value
        mirror[sz.mirror_blocks + r // SUB, r % SUB : r % SUB + 1, :] = value
    for f in range(2):
        for t in range(sz.tiles):
            base = sz.base(f, t)
            for d in range(2):
                mirror[sz.mirror_index(d, f, t)] = state[pl.ds(base + (Y - 1 - d) * SUB, SUB), :]
            positive = t >= sz.half
            out, first = (right, SUB - 2) if positive else (left, 0)
            side = sz.side_base(f, t)
            for c in range(2):
                for part in range(0, Y, SUB):
                    edge = state[pl.ds(base + part * SUB + first + c, SUB, stride=SUB), :]
                    out[pl.ds(side + 2 * part + c, SUB, stride=2), :] = edge
    pad = jnp.zeros((SUB, LANES), jnp.float32)
    for out in (right, left):
        out[0:SUB, :] = pad
        out[sz.side_rows - SUB : sz.side_rows, :] = pad


def wall_fields(sz, face, type_ref, index_ref, temps_ref, acc_ref, wall):
    column = sub()
    kind = jnp.zeros_like(column)
    entry = jnp.zeros_like(column)
    for x in range(SUB):
        kind = jnp.where(column == x, type_ref[face, x], kind)
        entry = jnp.where(column == x, index_ref[face, x], entry)
    percent = jnp.zeros_like(column)
    for t in range(NTYPE):
        percent = jnp.where(kind == t, acc_ref[t], percent)
    alpha = percent.astype(jnp.float32) / 100.0
    heat = jnp.ones((SUB, LANES), jnp.float32)
    denom = jnp.ones((SUB, LANES), jnp.float32)

    def grid(number):
        index = lax.broadcasted_iota(jnp.int32, (1, -(-number // LANES) * LANES), 1)
        return node_speed(index, number), index < number

    vx, in_x = grid(sz.nx)
    vy, in_y = grid(sz.nv)
    for t in range(NTEMP):
        temp = jnp.full((1, 1), temps_ref[t], jnp.float32)
        along = jnp.sum(jnp.where(in_x, jnp.exp(-vx * vx / temp), 0.0), axis=1, keepdims=True)
        across = jnp.sum(
            jnp.where(in_y, jnp.maximum(vy, 0.0) * jnp.exp(-vy * vy / temp), 0.0),
            axis=1,
            keepdims=True,
        )
        inward = sz.weight * along * across / (math.pi * temp)
        heat = jnp.where(entry == t, temp, heat)
        denom = jnp.where(entry == t, inward, denom)
    wall[0] = alpha / (denom * (math.pi * heat))
    wall[1] = 1.0 - alpha
    wall[2] = heat


def first_kernel(
    sz, given, type_ref, index_ref, temps_ref, acc_ref,
    state, mirror, packet, right, left, wall, sums_ref, turn,
):
    vert_index = lax.axis_index("vert")
    parity = vert_index % 2
    wall_fields(sz, 1 - parity, type_ref, index_ref, temps_ref, acc_ref, wall)
    for f in range(2):
        for xg in range(sz.xg):
            for kg in range(sz.kg):
                parts = []
                for k in range(kg * PART_K, (kg + 1) * PART_K):
                    if k < sz.band:
                        parts.append(given[f, k, xg * PART_X : (xg + 1) * PART_X, :])
                    else:
                        parts.append(jnp.zeros((PART_X, sz.cells), jnp.float32))
                turned = jnp.concatenate(parts, axis=0).T
                t = xg * sz.kg + kg
                slot = t % 2
                for x in range(SUB):
                    for part in range(0, Y, SUB):
                        piece = turned[x * Y + part : x * Y + part + SUB, :]
                        turn[slot, pl.ds(part * SUB + x, SUB, stride=SUB), :] = piece
                base = sz.base(f, t)
                for step in range(Y):
                    y = real_row(parity, step)
                    state[pl.ds(base + step * SUB, SUB), :] = turn[slot, block(y * SUB), :]

    def step_body(step, carry):
        totals = None
        for xg in range(sz.xg):
            sums = None
            for kg in range(sz.kg):
                g, h = [state[block(sz.base(f, xg * sz.kg + kg) + step * SUB), :] for f in range(2)]
                sums = add_columns(y_speed(sz, vert_index, kg), g, h, sums)
            totals = add_group(x_speed(sz, xg), sums, totals)
        put_sums(sums_ref, real_row(parity, step), totals)
        return carry

    lax.fori_loop(0, Y, step_body, 0)
    send(sz, vert_index, state, sums_ref, mirror, packet, right, left)


def fields_of(parity, tot):
    def row(r):
        return tot[r // SUB][r % SUB : r % SUB + 1, :]

    n, mx, my, energy, pxx, pxy, pyy, tx, ty = [row(r) for r in range(9)]
    inv_n = 1.0 / n
    ux, uy = mx * inv_n, my * inv_n
    usq = ux * ux + uy * uy
    theta = 2.0 / 3.0 * (energy * inv_n - usq)
    along = ux * mx + uy * my
    qx = tx - 2.0 * (ux * pxx + uy * pxy) + usq * mx - ux * energy + 2.0 * ux * along - ux * usq * n
    qy = ty - 2.0 * (ux * pxy + uy * pyy) + usq * my - uy * energy + 2.0 * uy * along - uy * usq * n
    inv_t = 1.0 / theta
    rate = (time_increment * relaxation_multiplier) * n * jnp.exp(shear_exponent * jnp.log(theta))
    amount = rate * n * inv_t * (1.0 / math.pi)
    scale = (1.0 - diffusivity_ratio) * 0.8 * inv_n * inv_t * inv_t
    flux = jnp.where(parity == 0, row(10), row(9))
    return [ux, uy, inv_t, amount, scale * qx, scale * qy, 0.5 * theta, rate, flux]


def step_kernel(sz, last, *refs):
    refs = list(refs)
    state, mirror_in, right_in, left_in, packet_in, wall = refs[:6]
    others = refs[6 : 6 + sz.vert - 2]
    rest = refs[6 + sz.vert - 2 :]
    if last:
        (final, spread, ghosts, xw, yw, out, turn) = rest
    else:
        (out, mirror, packet, right, left, spread, ghosts, xw, yw, sums_ref) = rest
    vert_index = lax.axis_index("vert")
    parity = vert_index % 2

    tot = [packet_in[SUB * b : SUB * b + SUB, :] + mirror_in[sz.mirror_blocks + b] for b in range(2)]
    for other in others:
        tot = [tot[b] + other[SUB * b : SUB * b + SUB, :] for b in range(2)]
    rows = fields_of(parity, tot)
    index = lax.broadcasted_iota(jnp.int32, (ROWS, LANES), 0)
    table = jnp.zeros((ROWS, sz.cells), jnp.float32)
    for r, value in enumerate(rows):
        table = jnp.where(index == r, value, table)
    for r in range(FIELDS):
        pick = (index == r).astype(jnp.float32)
        spread[r] = lax.dot_general(
            table, pick, (((0,), (0,)), ((), ())),
            precision=highest, preferred_element_type=jnp.float32,
        )

    for xg in range(sz.xg):
        speed = x_speed(sz, xg)
        for r, value in enumerate((speed,) + beam_weights(speed)):
            xw[4 * xg + r] = value
    for kg in range(sz.kg):
        speed = y_speed(sz, vert_index, kg)
        for r, value in enumerate((speed,) + beam_weights(speed)):
            yw[4 * kg + r] = value

    inv_heat = 1.0 / wall[2]
    half_heat = 0.5 * wall[2]
    keep = wall[1]
    emitted = spread[FIELDS - 1, block(real_row(parity, 0) * SUB), :] * wall[0]
    wall_y = []
    for kg in range(sz.kg):
        vy = yw[4 * kg]
        wall_y.append(masked(inside(sz, kg), emitted * jnp.exp(-vy * vy * inv_heat)))
    for xg in range(sz.xg):
        vx = xw[4 * xg]
        wall_x = jnp.exp(-vx * vx * inv_heat)
        for kg in range(sz.kg):
            diffuse = wall_x * wall_y[kg]
            t = xg * sz.kg + kg
            for f in range(2):
                add = half_heat * diffuse if f else diffuse
                for d in range(2):
                    at = sz.mirror_index(d, f, t)
                    ghosts[at] = keep * mirror_in[at] + add

    column = sub()

    def advance(step, upstream):
        y = real_row(parity, step)
        ux, uy, inv_t, amount, px, py, half_theta, rate = [
            spread[r, block(y * SUB), :] for r in range(FIELDS - 1)
        ]
        along_y = []
        for kg in range(sz.kg):
            cy = yw[4 * kg] - uy
            cy_sq = cy * cy * inv_t
            along_y.append((masked(inside(sz, kg), amount * jnp.exp(-cy_sq)), py * cy, cy_sq - 2.0))
        totals = None
        for xg in range(sz.xg):
            vx = xw[4 * xg]
            cx = vx - ux
            cx_sq = cx * cx * inv_t
            ex = jnp.exp(-cx_sq)
            pxs = px * cx
            x0 = (1.0 + xw[4 * xg + 1]) - rate
            x1, x2 = xw[4 * xg + 2], xw[4 * xg + 3]
            sums = None
            for kg in range(sz.kg):
                t = xg * sz.kg + kg
                positive = t >= sz.half
                ey, pys, cys = along_y[kg]
                maxwell = ex * ey
                p = pxs + pys
                sg = maxwell * (1.0 + p * (cx_sq + cys))
                sh = half_theta * (sg + p * maxwell)
                c0 = x0 + yw[4 * kg + 1]
                y1, y2 = yw[4 * kg + 2], yw[4 * kg + 3]
                values = []
                for f, source in ((0, sg), (1, sh)):
                    at = sz.base(f, t) + step * SUB
                    side = sz.side_base(f, t) + 2 * step
                    v = state[block(at), :]
                    if positive:
                        one = jnp.where(column < 1, right_in[pl.ds(side + 1, SUB), :], state[pl.ds(at - 1, SUB), :])
                        two = jnp.where(column < 2, right_in[pl.ds(side, SUB), :], state[pl.ds(at - 2, SUB), :])
                    else:
                        one = jnp.where(
                            column >= SUB - 1, left_in[pl.ds(side - (SUB - 1), SUB), :], state[pl.ds(at + 1, SUB), :]
                        )
                        two = jnp.where(
                            column >= SUB - 2, left_in[pl.ds(side - (SUB - 2), SUB), :], state[pl.ds(at + 2, SUB), :]
                        )
                    near, far = upstream(f, t, at)
                    moved = (v * c0 + source) + (x1 * one + x2 * two) + (y1 * near + y2 * far)
                    out[block(at), :] = moved
                    values.append(moved)
                if not last:
                    sums = add_columns(yw[4 * kg], values[0], values[1], sums)
            if not last:
                totals = add_group(vx, sums, totals)
        if not last:
            put_sums(sums_ref, y, totals)

    def ghost(d, f, t):
        return ghosts[sz.mirror_index(d, f, t)]

    advance(0, lambda f, t, at: (ghost(0, f, t), ghost(1, f, t)))
    advance(1, lambda f, t, at: (state[block(at - SUB), :], ghost(0, f, t)))

    def body(step, carry):
        advance(step, lambda f, t, at: (state[block(at - SUB), :], state[block(at - 2 * SUB), :]))
        return carry

    lax.fori_loop(2, Y, body, 0)
    if not last:
        send(sz, vert_index, out, sums_ref, mirror, packet, right, left)
        return
    for f in range(2):
        for xg in range(sz.xg):
            for kg in range(sz.kg):
                t = xg * sz.kg + kg
                slot = t % 2
                base = sz.base(f, t)
                for step in range(Y):
                    y = real_row(parity, step)
                    turn[slot, block(y * SUB), :] = out[pl.ds(base + step * SUB, SUB), :]
                parts = []
                for x in range(SUB):
                    for part in range(0, Y, SUB):
                        parts.append(turn[slot, pl.ds(part * SUB + x, SUB, stride=SUB), :])
                turned = jnp.concatenate(parts, axis=0).T
                for k in range(kg * PART_K, min((kg + 1) * PART_K, sz.band)):
                    row = (k - kg * PART_K) * PART_X
                    final[f, k, xg * PART_X : (xg + 1) * PART_X, :] = turned[row : row + PART_X, :]


def shapes(sz):
    f32 = jnp.float32
    side = jax.ShapeDtypeStruct((sz.side_rows, LANES), f32)
    return (
        jax.ShapeDtypeStruct((sz.state_rows, LANES), f32),
        jax.ShapeDtypeStruct((sz.mirror_blocks + 2, SUB, LANES), f32),
        jax.ShapeDtypeStruct((ROWS, sz.cells), f32),
        side,
        side,
    )


def on_device(distribution, wall_type, wall_temp_index, wall_temps, accommodation):
    _, band, nx, cells = distribution.shape
    vert = lax.axis_size("vert")
    columns = lax.axis_size("gx")
    sz = Sizes(band, nx, cells, vert)
    vmem = pl.BlockSpec(memory_space=pltpu.VMEM)
    smem = pl.BlockSpec(memory_space=pltpu.SMEM)
    final_shape = jax.ShapeDtypeStruct(distribution.shape, jnp.float32)
    bytes_moved = 2 * distribution.size * 4
    sums_scratch = pltpu.VMEM((FIELDS, sz.cells, LANES), jnp.float32)
    turn_scratch = pltpu.VMEM((2, sz.cells, LANES), jnp.float32)
    step_scratch = [
        pltpu.VMEM((FIELDS, sz.cells, LANES), jnp.float32),
        pltpu.VMEM((sz.mirror_blocks, SUB, LANES), jnp.float32),
        pltpu.VMEM((4 * sz.xg, SUB, LANES), jnp.float32),
        pltpu.VMEM((4 * sz.kg, SUB, LANES), jnp.float32),
    ]
    state, mirror, packet, right, left, wall = pl.pallas_call(
        functools.partial(first_kernel, sz),
        out_shape=shapes(sz) + (jax.ShapeDtypeStruct((3, SUB, LANES), jnp.float32),),
        in_specs=[vmem] + [smem] * 4,
        out_specs=(vmem,) * 6,
        scratch_shapes=[sums_scratch, turn_scratch],
        cost_estimate=pl.CostEstimate(
            flops=10 * distribution.size, bytes_accessed=bytes_moved, transcendentals=0
        ),
        compiler_params=pltpu.CompilerParams(vmem_limit_bytes=KERNEL_VMEM),
        name="first",
    )(distribution, wall_type, wall_temp_index, wall_temps, accommodation)
    ring = [(i, (i + 1) % columns) for i in range(columns)]
    back = [(j, i) for i, j in ring]
    for iteration in range(ITERS):
        last = iteration == ITERS - 1
        mirror_in = lax.ppermute(mirror, "vert", [(s, s ^ 1) for s in range(vert)])
        right_in = lax.ppermute(right, "gx", ring)
        left_in = lax.ppermute(left, "gx", back)
        others = []
        for mask in range(vert - 1, 1, -1):
            others.append(lax.ppermute(packet, "vert", [(s, s ^ mask) for s in range(vert)]))
        if last:
            scratch = step_scratch + [pltpu.VMEM((sz.state_rows, LANES), jnp.float32), turn_scratch]
        else:
            scratch = step_scratch + [sums_scratch]
        result = pl.pallas_call(
            functools.partial(step_kernel, sz, last),
            out_shape=(final_shape,) if last else shapes(sz),
            in_specs=[vmem] * (6 + len(others)),
            out_specs=(vmem,) if last else (vmem,) * 5,
            scratch_shapes=scratch,
            cost_estimate=pl.CostEstimate(
                flops=40 * distribution.size, bytes_accessed=bytes_moved, transcendentals=0
            ),
            compiler_params=pltpu.CompilerParams(vmem_limit_bytes=KERNEL_VMEM),
            name="last" if last else "step",
        )(state, mirror_in, right_in, left_in, packet, wall, *others)
        if last:
            (state,) = result
        else:
            state, mirror, packet, right, left = result
    return state


def solution(mesh):
    placed = (P(None, "vert", None, "gx"), P(None, "gx"), P(None, "gx"), P(), P())
    return jax.shard_map(
        on_device,
        mesh=mesh,
        in_specs=placed,
        out_specs=P(None, "vert", None, "gx"),
        check_vma=False,
    )
```

profile of v0, /device:TPU:0, one launch (start us, length us, event | category | flops | bytes accessed | tf_op | source)
XLA Modules:
  0.0 69.2 jit_solution(6769247448388569384)
XLA Ops:
  0.0 0.0 copy-start
  0.0 1.7 %copy-done = f32[2,24,96,128]{3,2,1,0:T(8,128)S(1)} copy-done((f32[2,24,96,128]{3,2,1,0:T(8,128)S(1)}, f32[2,24,96,128]{3,2,1,0:T(8,128)}, u32[]{:S(2)}) %copy-start) | copy-done | bytes 2359320
  1.7 0.0 copy-start.1
  1.7 0.7 copy-done.1
  2.3 0.0 copy-start.2
  2.3 0.7 copy-done.2
  3.0 0.0 copy-start.3
  3.0 0.7 copy-done.3
  3.7 0.0 copy-start.4
  3.7 0.7 copy-done.4
  4.3 2.7 %first.1 = (f32[4608,128]{1,0:T(8,128)S(1)}, f32[74,8,128]{2,1,0:T(8,128)S(1)}, f32[16,128]{1,0:T(8,128)S(1)}, f32[592,128]{1,0:T(8,128)S(1)}, f32[592,128]{1,0:T(8,128)S(1)}, /*index=5*/f32[3,8,128]{2,1,0:T(8,128)S(1)}) custom-call(f32[2,24,96,128]{3,2,1,0:T(8,128)S(1)} %copy-done, s32[2,8]{1,0:T(2,128)S(1)} %copy-done.1, s32[2,8]{1,0:T(2,128)S(1)} %copy-done.2, ...), custom_call_target="tpu_custom_call" | custom-call | flops 5898240 | bytes 4718592 | tf_op jit(solution)/shard_map/first/pallas_call | solution.py:433
  7.0 3.1 %collective-permute-start = (f32[74,8,128]{2,1,0:T(8,128)S(1)}, f32[74,8,128]{2,1,0:T(8,128)S(1)}, u32[]{:S(2)}, u32[]{:S(2)}) collective-permute-start(f32[74,8,128]{2,1,0:T(8,128)S(1)} %get-tuple-element.27), channel_id=1, source_target_pairs={{0,1},{1,0},{2,3},{3,2},{4,5},{5,4},{6,7},{7,6},{8,9},{9,8},{10,11... | collective-permute-start | bytes 909320 | tf_op jit(solution)/shard_map/ppermute | solution.py:449
  10.2 0.0 collective-permute-start.1
  10.2 2.6 %collective-permute-start.2 = (f32[592,128]{1,0:T(8,128)S(1)}, f32[592,128]{1,0:T(8,128)S(1)}, u32[]{:S(2)}, u32[]{:S(2)}) collective-permute-start(f32[592,128]{1,0:T(8,128)S(1)} %get-tuple-element.29), channel_id=1, source_target_pairs={{4,0},{8,4},{12,8},{16,12},{20,16},{24,20},{28,24},{0,28},{5,1},{9... | collective-permute-start | bytes 909320 | tf_op jit(solution)/shard_map/ppermute | solution.py:451
  12.8 2.6 %collective-permute-start.4 = (f32[16,128]{1,0:T(8,128)S(1)}, f32[16,128]{1,0:T(8,128)S(1)}, u32[]{:S(2)}, u32[]{:S(2)}) collective-permute-start(f32[16,128]{1,0:T(8,128)S(1)} %get-tuple-element.30.refs_4_), channel_id=1, source_target_pairs={{0,2},{1,3},{2,0},{3,1},{4,6},{5,7},{6,4},{7,5},{8,10},{9,11},{10,... | collective-permute-start | bytes 24584 | tf_op jit(solution)/shard_map/ppermute | solution.py:454
  15.4 0.0 collective-permute-start.3
  15.4 2.1 %collective-permute-done.4.refs_7_ = f32[16,128]{1,0:T(8,128)S(1)} collective-permute-done((f32[16,128]{1,0:T(8,128)S(1)}, f32[16,128]{1,0:T(8,128)S(1)}, u32[]{:S(2)}, u32[]{:S(2)}) %collective-permute-start.4) | collective-permute-done | bytes 8224 | tf_op jit(solution)/shard_map/ppermute | solution.py:454
  17.5 3.4 %collective-permute-done.3.refs_6_ = f32[16,128]{1,0:T(8,128)S(1)} collective-permute-done((f32[16,128]{1,0:T(8,128)S(1)}, f32[16,128]{1,0:T(8,128)S(1)}, u32[]{:S(2)}, u32[]{:S(2)}) %collective-permute-start.3) | collective-permute-done | bytes 8224 | tf_op jit(solution)/shard_map/ppermute | solution.py:454
  20.8 0.0 collective-permute-done.refs_1_
  20.9 0.0 collective-permute-done.1.refs_2_
  20.9 0.0 collective-permute-done.2.refs_3_
  20.9 3.6 %step.3 = (f32[4608,128]{1,0:T(8,128)S(1)}, f32[74,8,128]{2,1,0:T(8,128)S(1)}, f32[16,128]{1,0:T(8,128)S(1)}, f32[592,128]{1,0:T(8,128)S(1)}, f32[592,128]{1,0:T(8,128)S(1)}) custom-call(f32[4608,128]{1,0:T(8,128)S(1)} %get-tuple-element.26.refs_0_, f32[74,8,128]{2,1,0:T(8,128)S(1)} %collective-permute-done.refs_1_, ...), custom_call_target="tpu_custom_call" | custom-call | flops 23592960 | bytes 4718592 | tf_op jit(solution)/shard_map/step/pallas_call | solution.py:459
  24.4 0.1 collective-permute-start.5
  24.5 0.1 collective-permute-start.6
  24.6 2.6 %collective-permute-start.7 = (f32[592,128]{1,0:T(8,128)S(1)}, f32[592,128]{1,0:T(8,128)S(1)}, u32[]{:S(2)}, u32[]{:S(2)}) collective-permute-start(f32[592,128]{1,0:T(8,128)S(1)} %get-tuple-element.35), channel_id=1, source_target_pairs={{4,0},{8,4},{12,8},{16,12},{20,16},{24,20},{28,24},{0,28},{5,1},{9... | collective-permute-start | bytes 909320 | tf_op jit(solution)/shard_map/ppermute | solution.py:451
  27.2 1.1 %collective-permute-start.9 = (f32[16,128]{1,0:T(8,128)S(1)}, f32[16,128]{1,0:T(8,128)S(1)}, u32[]{:S(2)}, u32[]{:S(2)}) collective-permute-start(f32[16,128]{1,0:T(8,128)S(1)} %get-tuple-element.36.refs_4_), channel_id=1, source_target_pairs={{0,2},{1,3},{2,0},{3,1},{4,6},{5,7},{6,4},{7,5},{8,10},{9,11},{10,... | collective-permute-start | bytes 24584 | tf_op jit(solution)/shard_map/ppermute | solution.py:454
  28.3 3.2 %collective-permute-start.8 = (f32[16,128]{1,0:T(8,128)S(1)}, f32[16,128]{1,0:T(8,128)S(1)}, u32[]{:S(2)}, u32[]{:S(2)}) collective-permute-start(f32[16,128]{1,0:T(8,128)S(1)} %get-tuple-element.36.refs_4_), channel_id=1, source_target_pairs={{0,3},{1,2},{2,1},{3,0},{4,7},{5,6},{6,5},{7,4},{8,11},{9,10},{10,... | collective-permute-start | bytes 24584 | tf_op jit(solution)/shard_map/ppermute | solution.py:454
  31.5 0.3 collective-permute-done.9.refs_7_
  31.9 2.2 %collective-permute-done.8.refs_6_ = f32[16,128]{1,0:T(8,128)S(1)} collective-permute-done((f32[16,128]{1,0:T(8,128)S(1)}, f32[16,128]{1,0:T(8,128)S(1)}, u32[]{:S(2)}, u32[]{:S(2)}) %collective-permute-start.8) | collective-permute-done | bytes 8224 | tf_op jit(solution)/shard_map/ppermute | solution.py:454
  34.0 0.0 collective-permute-done.5.refs_1_
  34.0 0.0 collective-permute-done.6.refs_2_
  34.0 0.0 collective-permute-done.7.refs_3_
  34.0 3.6 %step.4 = (f32[4608,128]{1,0:T(8,128)S(1)}, f32[74,8,128]{2,1,0:T(8,128)S(1)}, f32[16,128]{1,0:T(8,128)S(1)}, f32[592,128]{1,0:T(8,128)S(1)}, f32[592,128]{1,0:T(8,128)S(1)}) custom-call(f32[4608,128]{1,0:T(8,128)S(1)} %get-tuple-element.32.refs_0_, f32[74,8,128]{2,1,0:T(8,128)S(1)} %collective-permute-done.5.refs_1_, ...), custom_call_target="tpu_custom_call" | custom-call | flops 23592960 | bytes 4718592 | tf_op jit(solution)/shard_map/step/pallas_call | solution.py:459
  37.6 2.0 %collective-permute-start.10 = (f32[74,8,128]{2,1,0:T(8,128)S(1)}, f32[74,8,128]{2,1,0:T(8,128)S(1)}, u32[]{:S(2)}, u32[]{:S(2)}) collective-permute-start(f32[74,8,128]{2,1,0:T(8,128)S(1)} %get-tuple-element.38), channel_id=1, source_target_pairs={{0,1},{1,0},{2,3},{3,2},{4,5},{5,4},{6,7},{7,6},{8,9},{9,8},{10,11... | collective-permute-start | bytes 909320 | tf_op jit(solution)/shard_map/ppermute | solution.py:449
  39.6 0.4 collective-permute-start.11
  40.0 2.2 %collective-permute-start.12 = (f32[592,128]{1,0:T(8,128)S(1)}, f32[592,128]{1,0:T(8,128)S(1)}, u32[]{:S(2)}, u32[]{:S(2)}) collective-permute-start(f32[592,128]{1,0:T(8,128)S(1)} %get-tuple-element.40), channel_id=1, source_target_pairs={{4,0},{8,4},{12,8},{16,12},{20,16},{24,20},{28,24},{0,28},{5,1},{9... | collective-permute-start | bytes 909320 | tf_op jit(solution)/shard_map/ppermute | solution.py:451
  42.2 1.6 %collective-permute-start.14 = (f32[16,128]{1,0:T(8,128)S(1)}, f32[16,128]{1,0:T(8,128)S(1)}, u32[]{:S(2)}, u32[]{:S(2)}) collective-permute-start(f32[16,128]{1,0:T(8,128)S(1)} %get-tuple-element.41.refs_4_), channel_id=1, source_target_pairs={{0,2},{1,3},{2,0},{3,1},{4,6},{5,7},{6,4},{7,5},{8,10},{9,11},{10,... | collective-permute-start | bytes 24584 | tf_op jit(solution)/shard_map/ppermute | solution.py:454
  43.8 0.9 %collective-permute-start.13 = (f32[16,128]{1,0:T(8,128)S(1)}, f32[16,128]{1,0:T(8,128)S(1)}, u32[]{:S(2)}, u32[]{:S(2)}) collective-permute-start(f32[16,128]{1,0:T(8,128)S(1)} %get-tuple-element.41.refs_4_), channel_id=1, source_target_pairs={{0,3},{1,2},{2,1},{3,0},{4,7},{5,6},{6,5},{7,4},{8,11},{9,10},{10,... | collective-permute-start | bytes 24584 | tf_op jit(solution)/shard_map/ppermute | solution.py:454
  44.7 2.4 %collective-permute-done.14.refs_7_ = f32[16,128]{1,0:T(8,128)S(1)} collective-permute-done((f32[16,128]{1,0:T(8,128)S(1)}, f32[16,128]{1,0:T(8,128)S(1)}, u32[]{:S(2)}, u32[]{:S(2)}) %collective-permute-start.14) | collective-permute-done | bytes 8224 | tf_op jit(solution)/shard_map/ppermute | solution.py:454
  47.1 2.1 %collective-permute-done.13.refs_6_ = f32[16,128]{1,0:T(8,128)S(1)} collective-permute-done((f32[16,128]{1,0:T(8,128)S(1)}, f32[16,128]{1,0:T(8,128)S(1)}, u32[]{:S(2)}, u32[]{:S(2)}) %collective-permute-start.13) | collective-permute-done | bytes 8224 | tf_op jit(solution)/shard_map/ppermute | solution.py:454
  49.3 0.0 collective-permute-done.10.refs_1_
  49.3 0.6 collective-permute-done.11.refs_2_
  49.9 0.0 collective-permute-done.12.refs_3_
  49.9 3.5 %step.5 = (f32[4608,128]{1,0:T(8,128)S(1)}, f32[74,8,128]{2,1,0:T(8,128)S(1)}, f32[16,128]{1,0:T(8,128)S(1)}, f32[592,128]{1,0:T(8,128)S(1)}, f32[592,128]{1,0:T(8,128)S(1)}) custom-call(f32[4608,128]{1,0:T(8,128)S(1)} %get-tuple-element.37.refs_0_, f32[74,8,128]{2,1,0:T(8,128)S(1)} %collective-permute-done.10.refs_1_, ...), custom_call_target="tpu_custom_call" | custom-call | flops 23592960 | bytes 4718592 | tf_op jit(solution)/shard_map/step/pallas_call | solution.py:459
  53.4 0.1 collective-permute-start.15
  53.5 0.4 collective-permute-start.16
  53.9 2.3 %collective-permute-start.17 = (f32[592,128]{1,0:T(8,128)S(1)}, f32[592,128]{1,0:T(8,128)S(1)}, u32[]{:S(2)}, u32[]{:S(2)}) collective-permute-start(f32[592,128]{1,0:T(8,128)S(1)} %get-tuple-element.45), channel_id=1, source_target_pairs={{4,0},{8,4},{12,8},{16,12},{20,16},{24,20},{28,24},{0,28},{5,1},{9... | collective-permute-start | bytes 909320 | tf_op jit(solution)/shard_map/ppermute | solution.py:451
  56.2 2.1 %collective-permute-start.19 = (f32[16,128]{1,0:T(8,128)S(1)}, f32[16,128]{1,0:T(8,128)S(1)}, u32[]{:S(2)}, u32[]{:S(2)}) collective-permute-start(f32[16,128]{1,0:T(8,128)S(1)} %get-tuple-element.46.refs_4_), channel_id=1, source_target_pairs={{0,2},{1,3},{2,0},{3,1},{4,6},{5,7},{6,4},{7,5},{8,10},{9,11},{10,... | collective-permute-start | bytes 24584 | tf_op jit(solution)/shard_map/ppermute | solution.py:454
  58.3 2.2 %collective-permute-start.18 = (f32[16,128]{1,0:T(8,128)S(1)}, f32[16,128]{1,0:T(8,128)S(1)}, u32[]{:S(2)}, u32[]{:S(2)}) collective-permute-start(f32[16,128]{1,0:T(8,128)S(1)} %get-tuple-element.46.refs_4_), channel_id=1, source_target_pairs={{0,3},{1,2},{2,1},{3,0},{4,7},{5,6},{6,5},{7,4},{8,11},{9,10},{10,... | collective-permute-start | bytes 24584 | tf_op jit(solution)/shard_map/ppermute | solution.py:454
  60.5 0.5 collective-permute-done.19.refs_7_
  61.0 2.7 %collective-permute-done.18.refs_6_ = f32[16,128]{1,0:T(8,128)S(1)} collective-permute-done((f32[16,128]{1,0:T(8,128)S(1)}, f32[16,128]{1,0:T(8,128)S(1)}, u32[]{:S(2)}, u32[]{:S(2)}) %collective-permute-start.18) | collective-permute-done | bytes 8224 | tf_op jit(solution)/shard_map/ppermute | solution.py:454
  63.8 0.0 collective-permute-done.15.refs_1_
  63.8 0.0 collective-permute-done.16.refs_2_
  63.8 0.0 collective-permute-done.17.refs_3_
  63.8 5.4 %last.1 = f32[2,24,96,128]{3,2,1,0:T(8,128)} custom-call(f32[4608,128]{1,0:T(8,128)S(1)} %get-tuple-element.42.refs_0_, f32[74,8,128]{2,1,0:T(8,128)S(1)} %collective-permute-done.15.refs_1_, f32[592,128]{1,0:T(8,128)S(1)} %collective-permute-done.16.refs_2_, f32[592,128]{1,0:T(8,128)S(1)} %collective-permute-done.17.refs_3_, ...), custom_call_target="tpu_custom_call" | custom-call | flops 23592960 | bytes 4718592 | tf_op jit(solution)/shard_map/last/pallas_call | solution.py:459
Async XLA Ops:
  0.0 1.7 %copy-start = (f32[2,24,96,128]{3,2,1,0:T(8,128)S(1)}, f32[2,24,96,128]{3,2,1,0:T(8,128)}, u32[]{:S(2)}) copy-start(f32[2,24,96,128]{3,2,1,0:T(8,128)} %given.1) | copy-start | bytes 7077892
  1.7 0.7 copy-start.1
  2.3 0.7 copy-start.2
  3.0 0.7 copy-start.3
  3.7 0.7 copy-start.4
  7.0 13.8 %collective-permute-start = (f32[74,8,128]{2,1,0:T(8,128)S(1)}, f32[74,8,128]{2,1,0:T(8,128)S(1)}, u32[]{:S(2)}, u32[]{:S(2)}) collective-permute-start(f32[74,8,128]{2,1,0:T(8,128)S(1)} %get-tuple-element.27), channel_id=1, source_target_pairs={{0,1},{1,0},{2,3},{3,2},{4,5},{5,4},{6,7},{7,6},{8,9},{9,8},{10,11... | collective-permute-start | bytes 909320 | tf_op jit(solution)/shard_map/ppermute | solution.py:449
  10.2 10.7 %collective-permute-start.1 = (f32[592,128]{1,0:T(8,128)S(1)}, f32[592,128]{1,0:T(8,128)S(1)}, u32[]{:S(2)}, u32[]{:S(2)}) collective-permute-start(f32[592,128]{1,0:T(8,128)S(1)} %get-tuple-element.28), channel_id=1, source_target_pairs={{0,4},{4,8},{8,12},{12,16},{16,20},{20,24},{24,28},{28,0},{1,5},{5... | collective-permute-start | bytes 909320 | tf_op jit(solution)/shard_map/ppermute | solution.py:450
  10.2 10.7 %collective-permute-start.2 = (f32[592,128]{1,0:T(8,128)S(1)}, f32[592,128]{1,0:T(8,128)S(1)}, u32[]{:S(2)}, u32[]{:S(2)}) collective-permute-start(f32[592,128]{1,0:T(8,128)S(1)} %get-tuple-element.29), channel_id=1, source_target_pairs={{4,0},{8,4},{12,8},{16,12},{20,16},{24,20},{28,24},{0,28},{5,1},{9... | collective-permute-start | bytes 909320 | tf_op jit(solution)/shard_map/ppermute | solution.py:451
  12.8 4.7 %collective-permute-start.4 = (f32[16,128]{1,0:T(8,128)S(1)}, f32[16,128]{1,0:T(8,128)S(1)}, u32[]{:S(2)}, u32[]{:S(2)}) collective-permute-start(f32[16,128]{1,0:T(8,128)S(1)} %get-tuple-element.30.refs_4_), channel_id=1, source_target_pairs={{0,2},{1,3},{2,0},{3,1},{4,6},{5,7},{6,4},{7,5},{8,10},{9,11},{10,... | collective-permute-start | bytes 24584 | tf_op jit(solution)/shard_map/ppermute | solution.py:454
  15.4 5.4 %collective-permute-start.3 = (f32[16,128]{1,0:T(8,128)S(1)}, f32[16,128]{1,0:T(8,128)S(1)}, u32[]{:S(2)}, u32[]{:S(2)}) collective-permute-start(f32[16,128]{1,0:T(8,128)S(1)} %get-tuple-element.30.refs_4_), channel_id=1, source_target_pairs={{0,3},{1,2},{2,1},{3,0},{4,7},{5,6},{6,5},{7,4},{8,11},{9,10},{10,... | collective-permute-start | bytes 24584 | tf_op jit(solution)/shard_map/ppermute | solution.py:454
  24.4 9.6 %collective-permute-start.5 = (f32[74,8,128]{2,1,0:T(8,128)S(1)}, f32[74,8,128]{2,1,0:T(8,128)S(1)}, u32[]{:S(2)}, u32[]{:S(2)}) collective-permute-start(f32[74,8,128]{2,1,0:T(8,128)S(1)} %get-tuple-element.33), channel_id=1, source_target_pairs={{0,1},{1,0},{2,3},{3,2},{4,5},{5,4},{6,7},{7,6},{8,9},{9,8},{10,11... | collective-permute-start | bytes 909320 | tf_op jit(solution)/shard_map/ppermute | solution.py:449
  24.5 9.5 %collective-permute-start.6 = (f32[592,128]{1,0:T(8,128)S(1)}, f32[592,128]{1,0:T(8,128)S(1)}, u32[]{:S(2)}, u32[]{:S(2)}) collective-permute-start(f32[592,128]{1,0:T(8,128)S(1)} %get-tuple-element.34), channel_id=1, source_target_pairs={{0,4},{4,8},{8,12},{12,16},{16,20},{20,24},{24,28},{28,0},{1,5},{5... | collective-permute-start | bytes 909320 | tf_op jit(solution)/shard_map/ppermute | solution.py:450
  24.6 9.5 %collective-permute-start.7 = (f32[592,128]{1,0:T(8,128)S(1)}, f32[592,128]{1,0:T(8,128)S(1)}, u32[]{:S(2)}, u32[]{:S(2)}) collective-permute-start(f32[592,128]{1,0:T(8,128)S(1)} %get-tuple-element.35), channel_id=1, source_target_pairs={{4,0},{8,4},{12,8},{16,12},{20,16},{24,20},{28,24},{0,28},{5,1},{9... | collective-permute-start | bytes 909320 | tf_op jit(solution)/shard_map/ppermute | solution.py:451
  27.2 4.7 %collective-permute-start.9 = (f32[16,128]{1,0:T(8,128)S(1)}, f32[16,128]{1,0:T(8,128)S(1)}, u32[]{:S(2)}, u32[]{:S(2)}) collective-permute-start(f32[16,128]{1,0:T(8,128)S(1)} %get-tuple-element.36.refs_4_), channel_id=1, source_target_pairs={{0,2},{1,3},{2,0},{3,1},{4,6},{5,7},{6,4},{7,5},{8,10},{9,11},{10,... | collective-permute-start | bytes 24584 | tf_op jit(solution)/shard_map/ppermute | solution.py:454
  28.3 5.7 %collective-permute-start.8 = (f32[16,128]{1,0:T(8,128)S(1)}, f32[16,128]{1,0:T(8,128)S(1)}, u32[]{:S(2)}, u32[]{:S(2)}) collective-permute-start(f32[16,128]{1,0:T(8,128)S(1)} %get-tuple-element.36.refs_4_), channel_id=1, source_target_pairs={{0,3},{1,2},{2,1},{3,0},{4,7},{5,6},{6,5},{7,4},{8,11},{9,10},{10,... | collective-permute-start | bytes 24584 | tf_op jit(solution)/shard_map/ppermute | solution.py:454
  37.6 11.7 %collective-permute-start.10 = (f32[74,8,128]{2,1,0:T(8,128)S(1)}, f32[74,8,128]{2,1,0:T(8,128)S(1)}, u32[]{:S(2)}, u32[]{:S(2)}) collective-permute-start(f32[74,8,128]{2,1,0:T(8,128)S(1)} %get-tuple-element.38), channel_id=1, source_target_pairs={{0,1},{1,0},{2,3},{3,2},{4,5},{5,4},{6,7},{7,6},{8,9},{9,8},{10,11... | collective-permute-start | bytes 909320 | tf_op jit(solution)/shard_map/ppermute | solution.py:449
  39.6 10.3 %collective-permute-start.11 = (f32[592,128]{1,0:T(8,128)S(1)}, f32[592,128]{1,0:T(8,128)S(1)}, u32[]{:S(2)}, u32[]{:S(2)}) collective-permute-start(f32[592,128]{1,0:T(8,128)S(1)} %get-tuple-element.39), channel_id=1, source_target_pairs={{0,4},{4,8},{8,12},{12,16},{16,20},{20,24},{24,28},{28,0},{1,5},{5... | collective-permute-start | bytes 909320 | tf_op jit(solution)/shard_map/ppermute | solution.py:450
  40.0 9.9 %collective-permute-start.12 = (f32[592,128]{1,0:T(8,128)S(1)}, f32[592,128]{1,0:T(8,128)S(1)}, u32[]{:S(2)}, u32[]{:S(2)}) collective-permute-start(f32[592,128]{1,0:T(8,128)S(1)} %get-tuple-element.40), channel_id=1, source_target_pairs={{4,0},{8,4},{12,8},{16,12},{20,16},{24,20},{28,24},{0,28},{5,1},{9... | collective-permute-start | bytes 909320 | tf_op jit(solution)/shard_map/ppermute | solution.py:451
  42.2 4.9 %collective-permute-start.14 = (f32[16,128]{1,0:T(8,128)S(1)}, f32[16,128]{1,0:T(8,128)S(1)}, u32[]{:S(2)}, u32[]{:S(2)}) collective-permute-start(f32[16,128]{1,0:T(8,128)S(1)} %get-tuple-element.41.refs_4_), channel_id=1, source_target_pairs={{0,2},{1,3},{2,0},{3,1},{4,6},{5,7},{6,4},{7,5},{8,10},{9,11},{10,... | collective-permute-start | bytes 24584 | tf_op jit(solution)/shard_map/ppermute | solution.py:454
  43.8 5.4 %collective-permute-start.13 = (f32[16,128]{1,0:T(8,128)S(1)}, f32[16,128]{1,0:T(8,128)S(1)}, u32[]{:S(2)}, u32[]{:S(2)}) collective-permute-start(f32[16,128]{1,0:T(8,128)S(1)} %get-tuple-element.41.refs_4_), channel_id=1, source_target_pairs={{0,3},{1,2},{2,1},{3,0},{4,7},{5,6},{6,5},{7,4},{8,11},{9,10},{10,... | collective-permute-start | bytes 24584 | tf_op jit(solution)/shard_map/ppermute | solution.py:454
  53.4 10.3 %collective-permute-start.15 = (f32[74,8,128]{2,1,0:T(8,128)S(1)}, f32[74,8,128]{2,1,0:T(8,128)S(1)}, u32[]{:S(2)}, u32[]{:S(2)}) collective-permute-start(f32[74,8,128]{2,1,0:T(8,128)S(1)} %get-tuple-element.43), channel_id=1, source_target_pairs={{0,1},{1,0},{2,3},{3,2},{4,5},{5,4},{6,7},{7,6},{8,9},{9,8},{10,11... | collective-permute-start | bytes 909320 | tf_op jit(solution)/shard_map/ppermute | solution.py:449
  53.5 10.3 %collective-permute-start.16 = (f32[592,128]{1,0:T(8,128)S(1)}, f32[592,128]{1,0:T(8,128)S(1)}, u32[]{:S(2)}, u32[]{:S(2)}) collective-permute-start(f32[592,128]{1,0:T(8,128)S(1)} %get-tuple-element.44), channel_id=1, source_target_pairs={{0,4},{4,8},{8,12},{12,16},{16,20},{20,24},{24,28},{28,0},{1,5},{5... | collective-permute-start | bytes 909320 | tf_op jit(solution)/shard_map/ppermute | solution.py:450
  53.9 9.9 %collective-permute-start.17 = (f32[592,128]{1,0:T(8,128)S(1)}, f32[592,128]{1,0:T(8,128)S(1)}, u32[]{:S(2)}, u32[]{:S(2)}) collective-permute-start(f32[592,128]{1,0:T(8,128)S(1)} %get-tuple-element.45), channel_id=1, source_target_pairs={{4,0},{8,4},{12,8},{16,12},{20,16},{24,20},{28,24},{0,28},{5,1},{9... | collective-permute-start | bytes 909320 | tf_op jit(solution)/shard_map/ppermute | solution.py:451
  56.2 4.8 %collective-permute-start.19 = (f32[16,128]{1,0:T(8,128)S(1)}, f32[16,128]{1,0:T(8,128)S(1)}, u32[]{:S(2)}, u32[]{:S(2)}) collective-permute-start(f32[16,128]{1,0:T(8,128)S(1)} %get-tuple-element.46.refs_4_), channel_id=1, source_target_pairs={{0,2},{1,3},{2,0},{3,1},{4,6},{5,7},{6,4},{7,5},{8,10},{9,11},{10,... | collective-permute-start | bytes 24584 | tf_op jit(solution)/shard_map/ppermute | solution.py:454
  58.3 5.4 %collective-permute-start.18 = (f32[16,128]{1,0:T(8,128)S(1)}, f32[16,128]{1,0:T(8,128)S(1)}, u32[]{:S(2)}, u32[]{:S(2)}) collective-permute-start(f32[16,128]{1,0:T(8,128)S(1)} %get-tuple-element.46.refs_4_), channel_id=1, source_target_pairs={{0,3},{1,2},{2,1},{3,0},{4,7},{5,6},{6,5},{7,4},{8,11},{9,10},{10,... | collective-permute-start | bytes 24584 | tf_op jit(solution)/shard_map/ppermute | solution.py:454
where the time goes:
time: 69.4 us; the launch traced here: 69.2 us
  starting transfers between devices  29.6 us (43%)
  Pallas kernels  18.8 us (27%)
  waiting for transfers between devices  16.4 us (24%)
  local copies, waits for them, and re-layouts  4.33 us (6%)
    pallas_call x4, Pallas kernels, on_device(): pl.pallas_call(functools.partial(step_kernel, sz, last), out_shape=(final...  16.1 us
    ppermute x8, waiting for transfers between devices, on_device(): lax.ppermute(packet, 'vert', [(s, s ^ mask) for s in range(vert)])  15.7 us
    ppermute x8, starting transfers between devices, on_device(): lax.ppermute(packet, 'vert', [(s, s ^ mask) for s in range(vert)])  13.7 us
    ppermute x4, starting transfers between devices, on_device(): left_in = lax.ppermute(left, 'gx', back)  9.85 us
    ppermute x4, starting transfers between devices, on_device(): mirror_in = lax.ppermute(mirror, 'vert', [(s, s ^ 1) for s in range(vert)])  5.24 us
    unnamed x10, local copies, waits for them, and re-layouts  4.33 us
    pallas_call x1, Pallas kernels, on_device(): pl.pallas_call(functools.partial(first_kernel, sz), out_shape=shapes(sz)...  2.7 us
  transfers between devices with their start and end apart: 20, of which 9 were waited for; matrix products, arithmetic and copies ran while one was open for 0% of the time, Pallas kernels for 0%

commit v1 on v0

--- a/solution.py
+++ b/solution.py
@@ -20,6 +20,7 @@
 PART_K = LANES // PART_X
 FIELDS = 9
 KERNEL_VMEM = 16 * 1024 * 1024
+ALL_VMEM = 64 * 1024 * 1024
 highest = lax.Precision.HIGHEST
 
 vmax_speed = 4.5
@@ -155,7 +156,8 @@
         out[sz.side_rows - SUB : sz.side_rows, :] = pad
 
 
-def wall_fields(sz, face, type_ref, index_ref, temps_ref, acc_ref, wall):
+def wall_kernel(sz, type_ref, index_ref, temps_ref, acc_ref, wall):
+    face = 1 - lax.axis_index("vert") % 2
     column = sub()
     kind = jnp.zeros_like(column)
     entry = jnp.zeros_like(column)
@@ -191,16 +193,23 @@
     wall[2] = heat
 
 
-def first_kernel(
-    sz, given, type_ref, index_ref, temps_ref, acc_ref,
-    state, mirror, packet, right, left, wall, sums_ref, turn,
-):
+def chunk_copy(sz, source, target, sems, f, kg):
+    rows = pl.ds(kg * PART_K, min(PART_K, sz.band - kg * PART_K))
+    return pltpu.make_async_copy(
+        source.at[f, rows], target.at[f, rows], sems.at[f * sz.kg + kg]
+    )
+
+
+def first_kernel(sz, argument, state, mirror, packet, right, left, sums_ref, turn, given, sems):
     vert_index = lax.axis_index("vert")
     parity = vert_index % 2
-    wall_fields(sz, 1 - parity, type_ref, index_ref, temps_ref, acc_ref, wall)
     for f in range(2):
-        for xg in range(sz.xg):
-            for kg in range(sz.kg):
+        for kg in range(sz.kg):
+            chunk_copy(sz, argument, given, sems, f, kg).start()
+    for f in range(2):
+        for kg in range(sz.kg):
+            chunk_copy(sz, argument, given, sems, f, kg).wait()
+            for xg in range(sz.xg):
                 parts = []
                 for k in range(kg * PART_K, (kg + 1) * PART_K):
                     if k < sz.band:
@@ -209,7 +218,7 @@
                         parts.append(jnp.zeros((PART_X, sz.cells), jnp.float32))
                 turned = jnp.concatenate(parts, axis=0).T
                 t = xg * sz.kg + kg
-                slot = t % 2
+                slot = xg % 2
                 for x in range(SUB):
                     for part in range(0, Y, SUB):
                         piece = turned[x * Y + part : x * Y + part + SUB, :]
@@ -260,7 +269,7 @@
     others = refs[6 : 6 + sz.vert - 2]
     rest = refs[6 + sz.vert - 2 :]
     if last:
-        (final, spread, ghosts, xw, yw, out, turn) = rest
+        (result, spread, ghosts, xw, yw, out, turn, final, sems) = rest
     else:
         (out, mirror, packet, right, left, spread, ghosts, xw, yw, sums_ref) = rest
     vert_index = lax.axis_index("vert")
@@ -383,10 +392,10 @@
         send(sz, vert_index, out, sums_ref, mirror, packet, right, left)
         return
     for f in range(2):
-        for xg in range(sz.xg):
-            for kg in range(sz.kg):
+        for kg in range(sz.kg):
+            for xg in range(sz.xg):
                 t = xg * sz.kg + kg
-                slot = t % 2
+                slot = xg % 2
                 base = sz.base(f, t)
                 for step in range(Y):
                     y = real_row(parity, step)
@@ -399,6 +408,10 @@
                 for k in range(kg * PART_K, min((kg + 1) * PART_K, sz.band)):
                     row = (k - kg * PART_K) * PART_X
                     final[f, k, xg * PART_X : (xg + 1) * PART_X, :] = turned[row : row + PART_X, :]
+            chunk_copy(sz, final, result, sems, f, kg).start()
+    for f in range(2):
+        for kg in range(sz.kg):
+            chunk_copy(sz, final, result, sems, f, kg).wait()
 
 
 def shapes(sz):
@@ -420,6 +433,7 @@
     sz = Sizes(band, nx, cells, vert)
     vmem = pl.BlockSpec(memory_space=pltpu.VMEM)
     smem = pl.BlockSpec(memory_space=pltpu.SMEM)
+    hbm = pl.BlockSpec(memory_space=pltpu.HBM)
     final_shape = jax.ShapeDtypeStruct(distribution.shape, jnp.float32)
     bytes_moved = 2 * distribution.size * 4
     sums_scratch = pltpu.VMEM((FIELDS, sz.cells, LANES), jnp.float32)
@@ -430,18 +444,31 @@
         pltpu.VMEM((4 * sz.xg, SUB, LANES), jnp.float32),
         pltpu.VMEM((4 * sz.kg, SUB, LANES), jnp.float32),
     ]
-    state, mirror, packet, right, left, wall = pl.pallas_call(
+    first_vmem = ALL_VMEM - 26 * distribution.size
+    stage = [
+        pltpu.VMEM(distribution.shape, jnp.float32),
+        pltpu.SemaphoreType.DMA((2 * sz.kg,)),
+    ]
+    state, mirror, packet, right, left = pl.pallas_call(
         functools.partial(first_kernel, sz),
-        out_shape=shapes(sz) + (jax.ShapeDtypeStruct((3, SUB, LANES), jnp.float32),),
-        in_specs=[vmem] + [smem] * 4,
-        out_specs=(vmem,) * 6,
-        scratch_shapes=[sums_scratch, turn_scratch],
+        out_shape=shapes(sz),
+        in_specs=[hbm],
+        out_specs=(vmem,) * 5,
+        scratch_shapes=[sums_scratch, turn_scratch] + stage,
         cost_estimate=pl.CostEstimate(
             flops=10 * distribution.size, bytes_accessed=bytes_moved, transcendentals=0
         ),
+        compiler_params=pltpu.CompilerParams(vmem_limit_bytes=first_vmem),
+        name="first",
+    )(distribution)
+    wall = pl.pallas_call(
+        functools.partial(wall_kernel, sz),
+        out_shape=jax.ShapeDtypeStruct((3, SUB, LANES), jnp.float32),
+        in_specs=[smem] * 4,
+        out_specs=vmem,
         compiler_params=pltpu.CompilerParams(vmem_limit_bytes=KERNEL_VMEM),
-        name="first",
-    )(distribution, wall_type, wall_temp_index, wall_temps, accommodation)
+        name="walls",
+    )(wall_type, wall_temp_index, wall_temps, accommodation)
     ring = [(i, (i + 1) % columns) for i in range(columns)]
     back = [(j, i) for i, j in ring]
     for iteration in range(ITERS):
@@ -453,14 +480,14 @@
         for mask in range(vert - 1, 1, -1):
             others.append(lax.ppermute(packet, "vert", [(s, s ^ mask) for s in range(vert)]))
         if last:
-            scratch = step_scratch + [pltpu.VMEM((sz.state_rows, LANES), jnp.float32), turn_scratch]
+            scratch = step_scratch + [pltpu.VMEM((sz.state_rows, LANES), jnp.float32), turn_scratch] + stage
         else:
             scratch = step_scratch + [sums_scratch]
         result = pl.pallas_call(
             functools.partial(step_kernel, sz, last),
             out_shape=(final_shape,) if last else shapes(sz),
             in_specs=[vmem] * (6 + len(others)),
-            out_specs=(vmem,) if last else (vmem,) * 5,
+            out_specs=(hbm,) if last else (vmem,) * 5,
             scratch_shapes=scratch,
             cost_estimate=pl.CostEstimate(
                 flops=40 * distribution.size, bytes_accessed=bytes_moved, transcendentals=0

time: 69.4 us -> 65.3 us (0.941)
  local copies, waits for them, and re-layouts: 4.33 us -> 0.01 us
  Pallas kernels: 18.8 us -> 19.7 us
  waiting for transfers between devices: 16.4 us -> 15.7 us
    unnamed x10 -> x8, local copies, waits for them, and re-layouts: 4.33 us -> 0.01 us
    pallas_call x1 -> x2, Pallas kernels: 2.7 us -> 4.26 us  [the longest x1 3.58 us: on_device(): pl.pallas_call(functools.partial(first_kernel, sz), out_shape=shapes(sz),...]
    ppermute x8, waiting for transfers between devices: 15.7 us -> 15 us  [on_device(): lax.ppermute(packet, 'vert', [(s, s ^ mask) for s in range(vert)])]
  transfers between devices with their start and end apart: 20 -> 20, of which waited for: 9 -> 9; matrix products, arithmetic and copies ran while one was open for 0% -> 0% of each run, Pallas kernels for 0% -> 1%
where the time goes in v1:
time: 65.3 us; the launch traced here: 65.1 us
  starting transfers between devices  29.6 us (45%)
  Pallas kernels  19.7 us (30%)
  waiting for transfers between devices  15.7 us (24%)
    pallas_call x4, Pallas kernels, on_device(): pl.pallas_call(functools.partial(step_kernel, sz, last), out_shape=(final...  15.5 us
    ppermute x8, waiting for transfers between devices, on_device(): lax.ppermute(packet, 'vert', [(s, s ^ mask) for s in range(vert)])  15 us
    ppermute x8, starting transfers between devices, on_device(): lax.ppermute(packet, 'vert', [(s, s ^ mask) for s in range(vert)])  13.7 us
    ppermute x4, starting transfers between devices, on_device(): left_in = lax.ppermute(left, 'gx', back)  9.84 us
    ppermute x4, starting transfers between devices, on_device(): mirror_in = lax.ppermute(mirror, 'vert', [(s, s ^ 1) for s in range(vert)])  5.2 us
    pallas_call x1, Pallas kernels, on_device(): pl.pallas_call(functools.partial(first_kernel, sz), out_shape=shapes(sz),...  3.58 us
  transfers between devices with their start and end apart: 20, of which 9 were waited for; matrix products, arithmetic and copies ran while one was open for 0% of the time, Pallas kernels for 1%

profile of v1, /device:TPU:0, one launch (start us, length us, event | category | flops | bytes accessed | tf_op | source)
XLA Modules:
  0.0 65.1 jit_solution(8457380756946685945)
XLA Ops:
  0.0 0.0 copy-start.3
  0.0 0.0 copy-start.2
  0.0 0.0 copy-start.1
  0.0 0.0 copy-start
  0.0 3.6 %first.1 = (f32[4608,128]{1,0:T(8,128)S(1)}, f32[74,8,128]{2,1,0:T(8,128)S(1)}, f32[16,128]{1,0:T(8,128)S(1)}, f32[592,128]{1,0:T(8,128)S(1)}, f32[592,128]{1,0:T(8,128)S(1)}) custom-call(f32[2,24,96,128]{3,2,1,0:T(8,128)} %argument.1), custom_call_target="tpu_custom_call" | custom-call | flops 5898240 | bytes 4718592 | tf_op jit(solution)/shard_map/first/pallas_call | solution.py:452
  3.6 3.1 %collective-permute-start = (f32[74,8,128]{2,1,0:T(8,128)S(1)}, f32[74,8,128]{2,1,0:T(8,128)S(1)}, u32[]{:S(2)}, u32[]{:S(2)}) collective-permute-start(f32[74,8,128]{2,1,0:T(8,128)S(1)} %get-tuple-element.26), channel_id=1, source_target_pairs={{0,1},{1,0},{2,3},{3,2},{4,5},{5,4},{6,7},{7,6},{8,9},{9,8},{10,11... | collective-permute-start | bytes 909320 | tf_op jit(solution)/shard_map/ppermute | solution.py:476
  6.7 0.0 collective-permute-start.1
  6.7 2.6 %collective-permute-start.2 = (f32[592,128]{1,0:T(8,128)S(1)}, f32[592,128]{1,0:T(8,128)S(1)}, u32[]{:S(2)}, u32[]{:S(2)}) collective-permute-start(f32[592,128]{1,0:T(8,128)S(1)} %get-tuple-element.28), channel_id=1, source_target_pairs={{4,0},{8,4},{12,8},{16,12},{20,16},{24,20},{28,24},{0,28},{5,1},{9... | collective-permute-start | bytes 909320 | tf_op jit(solution)/shard_map/ppermute | solution.py:478
  9.3 2.6 %collective-permute-start.4 = (f32[16,128]{1,0:T(8,128)S(1)}, f32[16,128]{1,0:T(8,128)S(1)}, u32[]{:S(2)}, u32[]{:S(2)}) collective-permute-start(f32[16,128]{1,0:T(8,128)S(1)} %get-tuple-element.29.refs_4_), channel_id=1, source_target_pairs={{0,2},{1,3},{2,0},{3,1},{4,6},{5,7},{6,4},{7,5},{8,10},{9,11},{10,... | collective-permute-start | bytes 24584 | tf_op jit(solution)/shard_map/ppermute | solution.py:481
  11.9 0.0 collective-permute-start.3
  11.9 0.0 copy-done.3
  11.9 0.0 copy-done.2
  11.9 0.0 copy-done.1
  11.9 0.0 copy-done
  11.9 0.7 %walls.1.refs_5_ = f32[3,8,128]{2,1,0:T(8,128)S(1)} custom-call(s32[2,8]{1,0:T(2,128)S(1)} %copy-done, s32[2,8]{1,0:T(2,128)S(1)} %copy-done.1, f32[2]{0:T(128)S(1)} %copy-done.2, s32[3]{0:T(128)S(1)} %copy-done.3), custom_call_target="tpu_custom_call" | custom-call | tf_op jit(solution)/shard_map/walls/pallas_call | solution.py:464
  12.6 1.4 %collective-permute-done.4.refs_7_ = f32[16,128]{1,0:T(8,128)S(1)} collective-permute-done((f32[16,128]{1,0:T(8,128)S(1)}, f32[16,128]{1,0:T(8,128)S(1)}, u32[]{:S(2)}, u32[]{:S(2)}) %collective-permute-start.4) | collective-permute-done | bytes 8224 | tf_op jit(solution)/shard_map/ppermute | solution.py:481
  14.0 3.4 %collective-permute-done.3.refs_6_ = f32[16,128]{1,0:T(8,128)S(1)} collective-permute-done((f32[16,128]{1,0:T(8,128)S(1)}, f32[16,128]{1,0:T(8,128)S(1)}, u32[]{:S(2)}, u32[]{:S(2)}) %collective-permute-start.3) | collective-permute-done | bytes 8224 | tf_op jit(solution)/shard_map/ppermute | solution.py:481
  17.4 0.0 collective-permute-done.refs_1_
  17.4 0.0 collective-permute-done.1.refs_2_
  17.4 0.0 collective-permute-done.2.refs_3_
  17.4 3.5 %step.3 = (f32[4608,128]{1,0:T(8,128)S(1)}, f32[74,8,128]{2,1,0:T(8,128)S(1)}, f32[16,128]{1,0:T(8,128)S(1)}, f32[592,128]{1,0:T(8,128)S(1)}, f32[592,128]{1,0:T(8,128)S(1)}) custom-call(f32[4608,128]{1,0:T(8,128)S(1)} %get-tuple-element.25.refs_0_, f32[74,8,128]{2,1,0:T(8,128)S(1)} %collective-permute-done.refs_1_, ...), custom_call_target="tpu_custom_call" | custom-call | flops 23592960 | bytes 4718592 | tf_op jit(solution)/shard_map/step/pallas_call | solution.py:486
  20.9 0.1 collective-permute-start.5
  21.0 0.1 collective-permute-start.6
  21.1 2.6 %collective-permute-start.7 = (f32[592,128]{1,0:T(8,128)S(1)}, f32[592,128]{1,0:T(8,128)S(1)}, u32[]{:S(2)}, u32[]{:S(2)}) collective-permute-start(f32[592,128]{1,0:T(8,128)S(1)} %get-tuple-element.33), channel_id=1, source_target_pairs={{4,0},{8,4},{12,8},{16,12},{20,16},{24,20},{28,24},{0,28},{5,1},{9... | collective-permute-start | bytes 909320 | tf_op jit(solution)/shard_map/ppermute | solution.py:478
  23.7 1.1 %collective-permute-start.9 = (f32[16,128]{1,0:T(8,128)S(1)}, f32[16,128]{1,0:T(8,128)S(1)}, u32[]{:S(2)}, u32[]{:S(2)}) collective-permute-start(f32[16,128]{1,0:T(8,128)S(1)} %get-tuple-element.34.refs_4_), channel_id=1, source_target_pairs={{0,2},{1,3},{2,0},{3,1},{4,6},{5,7},{6,4},{7,5},{8,10},{9,11},{10,... | collective-permute-start | bytes 24584 | tf_op jit(solution)/shard_map/ppermute | solution.py:481
  24.8 3.2 %collective-permute-start.8 = (f32[16,128]{1,0:T(8,128)S(1)}, f32[16,128]{1,0:T(8,128)S(1)}, u32[]{:S(2)}, u32[]{:S(2)}) collective-permute-start(f32[16,128]{1,0:T(8,128)S(1)} %get-tuple-element.34.refs_4_), channel_id=1, source_target_pairs={{0,3},{1,2},{2,1},{3,0},{4,7},{5,6},{6,5},{7,4},{8,11},{9,10},{10,... | collective-permute-start | bytes 24584 | tf_op jit(solution)/shard_map/ppermute | solution.py:481
  28.0 0.3 collective-permute-done.9.refs_7_
  28.3 2.2 %collective-permute-done.8.refs_6_ = f32[16,128]{1,0:T(8,128)S(1)} collective-permute-done((f32[16,128]{1,0:T(8,128)S(1)}, f32[16,128]{1,0:T(8,128)S(1)}, u32[]{:S(2)}, u32[]{:S(2)}) %collective-permute-start.8) | collective-permute-done | bytes 8224 | tf_op jit(solution)/shard_map/ppermute | solution.py:481
  30.5 0.0 collective-permute-done.5.refs_1_
  30.5 0.0 collective-permute-done.6.refs_2_
  30.5 0.0 collective-permute-done.7.refs_3_
  30.5 3.6 %step.4 = (f32[4608,128]{1,0:T(8,128)S(1)}, f32[74,8,128]{2,1,0:T(8,128)S(1)}, f32[16,128]{1,0:T(8,128)S(1)}, f32[592,128]{1,0:T(8,128)S(1)}, f32[592,128]{1,0:T(8,128)S(1)}) custom-call(f32[4608,128]{1,0:T(8,128)S(1)} %get-tuple-element.30.refs_0_, f32[74,8,128]{2,1,0:T(8,128)S(1)} %collective-permute-done.5.refs_1_, ...), custom_call_target="tpu_custom_call" | custom-call | flops 23592960 | bytes 4718592 | tf_op jit(solution)/shard_map/step/pallas_call | solution.py:486
  34.1 2.0 %collective-permute-start.10 = (f32[74,8,128]{2,1,0:T(8,128)S(1)}, f32[74,8,128]{2,1,0:T(8,128)S(1)}, u32[]{:S(2)}, u32[]{:S(2)}) collective-permute-start(f32[74,8,128]{2,1,0:T(8,128)S(1)} %get-tuple-element.36), channel_id=1, source_target_pairs={{0,1},{1,0},{2,3},{3,2},{4,5},{5,4},{6,7},{7,6},{8,9},{9,8},{10,11... | collective-permute-start | bytes 909320 | tf_op jit(solution)/shard_map/ppermute | solution.py:476
  36.1 0.4 collective-permute-start.11
  36.5 2.3 %collective-permute-start.12 = (f32[592,128]{1,0:T(8,128)S(1)}, f32[592,128]{1,0:T(8,128)S(1)}, u32[]{:S(2)}, u32[]{:S(2)}) collective-permute-start(f32[592,128]{1,0:T(8,128)S(1)} %get-tuple-element.38), channel_id=1, source_target_pairs={{4,0},{8,4},{12,8},{16,12},{20,16},{24,20},{28,24},{0,28},{5,1},{9... | collective-permute-start | bytes 909320 | tf_op jit(solution)/shard_map/ppermute | solution.py:478
  38.7 1.6 %collective-permute-start.14 = (f32[16,128]{1,0:T(8,128)S(1)}, f32[16,128]{1,0:T(8,128)S(1)}, u32[]{:S(2)}, u32[]{:S(2)}) collective-permute-start(f32[16,128]{1,0:T(8,128)S(1)} %get-tuple-element.39.refs_4_), channel_id=1, source_target_pairs={{0,2},{1,3},{2,0},{3,1},{4,6},{5,7},{6,4},{7,5},{8,10},{9,11},{10,... | collective-permute-start | bytes 24584 | tf_op jit(solution)/shard_map/ppermute | solution.py:481
  40.3 0.9 %collective-permute-start.13 = (f32[16,128]{1,0:T(8,128)S(1)}, f32[16,128]{1,0:T(8,128)S(1)}, u32[]{:S(2)}, u32[]{:S(2)}) collective-permute-start(f32[16,128]{1,0:T(8,128)S(1)} %get-tuple-element.39.refs_4_), channel_id=1, source_target_pairs={{0,3},{1,2},{2,1},{3,0},{4,7},{5,6},{6,5},{7,4},{8,11},{9,10},{10,... | collective-permute-start | bytes 24584 | tf_op jit(solution)/shard_map/ppermute | solution.py:481
  41.2 2.4 %collective-permute-done.14.refs_7_ = f32[16,128]{1,0:T(8,128)S(1)} collective-permute-done((f32[16,128]{1,0:T(8,128)S(1)}, f32[16,128]{1,0:T(8,128)S(1)}, u32[]{:S(2)}, u32[]{:S(2)}) %collective-permute-start.14) | collective-permute-done | bytes 8224 | tf_op jit(solution)/shard_map/ppermute | solution.py:481
  43.6 2.1 %collective-permute-done.13.refs_6_ = f32[16,128]{1,0:T(8,128)S(1)} collective-permute-done((f32[16,128]{1,0:T(8,128)S(1)}, f32[16,128]{1,0:T(8,128)S(1)}, u32[]{:S(2)}, u32[]{:S(2)}) %collective-permute-start.13) | collective-permute-done | bytes 8224 | tf_op jit(solution)/shard_map/ppermute | solution.py:481
  45.8 0.0 collective-permute-done.10.refs_1_
  45.8 0.6 collective-permute-done.11.refs_2_
  46.4 0.0 collective-permute-done.12.refs_3_
  46.4 3.5 %step.5 = (f32[4608,128]{1,0:T(8,128)S(1)}, f32[74,8,128]{2,1,0:T(8,128)S(1)}, f32[16,128]{1,0:T(8,128)S(1)}, f32[592,128]{1,0:T(8,128)S(1)}, f32[592,128]{1,0:T(8,128)S(1)}) custom-call(f32[4608,128]{1,0:T(8,128)S(1)} %get-tuple-element.35.refs_0_, f32[74,8,128]{2,1,0:T(8,128)S(1)} %collective-permute-done.10.refs_1_, ...), custom_call_target="tpu_custom_call" | custom-call | flops 23592960 | bytes 4718592 | tf_op jit(solution)/shard_map/step/pallas_call | solution.py:486
  49.9 0.1 collective-permute-start.15
  50.0 0.4 collective-permute-start.16
  50.4 2.3 %collective-permute-start.17 = (f32[592,128]{1,0:T(8,128)S(1)}, f32[592,128]{1,0:T(8,128)S(1)}, u32[]{:S(2)}, u32[]{:S(2)}) collective-permute-start(f32[592,128]{1,0:T(8,128)S(1)} %get-tuple-element.43), channel_id=1, source_target_pairs={{4,0},{8,4},{12,8},{16,12},{20,16},{24,20},{28,24},{0,28},{5,1},{9... | collective-permute-start | bytes 909320 | tf_op jit(solution)/shard_map/ppermute | solution.py:478
  52.7 2.1 %collective-permute-start.19 = (f32[16,128]{1,0:T(8,128)S(1)}, f32[16,128]{1,0:T(8,128)S(1)}, u32[]{:S(2)}, u32[]{:S(2)}) collective-permute-start(f32[16,128]{1,0:T(8,128)S(1)} %get-tuple-element.44.refs_4_), channel_id=1, source_target_pairs={{0,2},{1,3},{2,0},{3,1},{4,6},{5,7},{6,4},{7,5},{8,10},{9,11},{10,... | collective-permute-start | bytes 24584 | tf_op jit(solution)/shard_map/ppermute | solution.py:481
  54.8 2.2 %collective-permute-start.18 = (f32[16,128]{1,0:T(8,128)S(1)}, f32[16,128]{1,0:T(8,128)S(1)}, u32[]{:S(2)}, u32[]{:S(2)}) collective-permute-start(f32[16,128]{1,0:T(8,128)S(1)} %get-tuple-element.44.refs_4_), channel_id=1, source_target_pairs={{0,3},{1,2},{2,1},{3,0},{4,7},{5,6},{6,5},{7,4},{8,11},{9,10},{10,... | collective-permute-start | bytes 24584 | tf_op jit(solution)/shard_map/ppermute | solution.py:481
  57.0 0.5 collective-permute-done.19.refs_7_
  57.5 2.7 %collective-permute-done.18.refs_6_ = f32[16,128]{1,0:T(8,128)S(1)} collective-permute-done((f32[16,128]{1,0:T(8,128)S(1)}, f32[16,128]{1,0:T(8,128)S(1)}, u32[]{:S(2)}, u32[]{:S(2)}) %collective-permute-start.18) | collective-permute-done | bytes 8224 | tf_op jit(solution)/shard_map/ppermute | solution.py:481
  60.3 0.0 collective-permute-done.15.refs_1_
  60.3 0.0 collective-permute-done.16.refs_2_
  60.3 0.0 collective-permute-done.17.refs_3_
  60.3 4.8 %last.1 = f32[2,24,96,128]{3,2,1,0:T(8,128)} custom-call(f32[4608,128]{1,0:T(8,128)S(1)} %get-tuple-element.40.refs_0_, f32[74,8,128]{2,1,0:T(8,128)S(1)} %collective-permute-done.15.refs_1_, f32[592,128]{1,0:T(8,128)S(1)} %collective-permute-done.16.refs_2_, f32[592,128]{1,0:T(8,128)S(1)} %collective-permute-done.17.refs_3_, ...), custom_call_target="tpu_custom_call" | custom-call | flops 23592960 | bytes 4718592 | tf_op jit(solution)/shard_map/last/pallas_call | solution.py:486
Async XLA Ops:
  0.0 11.9 %copy-start.3 = (s32[3]{0:T(128)S(1)}, s32[3]{0:T(128)}, u32[]{:S(2)}) copy-start(s32[3]{0:T(128)} %acc_ref.1) | copy-start | bytes 40
  0.0 11.9 %copy-start.2 = (f32[2]{0:T(128)S(1)}, f32[2]{0:T(128)}, u32[]{:S(2)}) copy-start(f32[2]{0:T(128)} %temps_ref.1) | copy-start | bytes 28
  0.0 11.9 %copy-start.1 = (s32[2,8]{1,0:T(2,128)S(1)}, s32[2,8]{1,0:T(2,128)}, u32[]{:S(2)}) copy-start(s32[2,8]{1,0:T(2,128)} %index_ref.1) | copy-start | bytes 196
  0.0 11.9 %copy-start = (s32[2,8]{1,0:T(2,128)S(1)}, s32[2,8]{1,0:T(2,128)}, u32[]{:S(2)}) copy-start(s32[2,8]{1,0:T(2,128)} %type_ref.1) | copy-start | bytes 196
  3.6 13.8 %collective-permute-start = (f32[74,8,128]{2,1,0:T(8,128)S(1)}, f32[74,8,128]{2,1,0:T(8,128)S(1)}, u32[]{:S(2)}, u32[]{:S(2)}) collective-permute-start(f32[74,8,128]{2,1,0:T(8,128)S(1)} %get-tuple-element.26), channel_id=1, source_target_pairs={{0,1},{1,0},{2,3},{3,2},{4,5},{5,4},{6,7},{7,6},{8,9},{9,8},{10,11... | collective-permute-start | bytes 909320 | tf_op jit(solution)/shard_map/ppermute | solution.py:476
  6.7 10.7 %collective-permute-start.1 = (f32[592,128]{1,0:T(8,128)S(1)}, f32[592,128]{1,0:T(8,128)S(1)}, u32[]{:S(2)}, u32[]{:S(2)}) collective-permute-start(f32[592,128]{1,0:T(8,128)S(1)} %get-tuple-element.27), channel_id=1, source_target_pairs={{0,4},{4,8},{8,12},{12,16},{16,20},{20,24},{24,28},{28,0},{1,5},{5... | collective-permute-start | bytes 909320 | tf_op jit(solution)/shard_map/ppermute | solution.py:477
  6.7 10.7 %collective-permute-start.2 = (f32[592,128]{1,0:T(8,128)S(1)}, f32[592,128]{1,0:T(8,128)S(1)}, u32[]{:S(2)}, u32[]{:S(2)}) collective-permute-start(f32[592,128]{1,0:T(8,128)S(1)} %get-tuple-element.28), channel_id=1, source_target_pairs={{4,0},{8,4},{12,8},{16,12},{20,16},{24,20},{28,24},{0,28},{5,1},{9... | collective-permute-start | bytes 909320 | tf_op jit(solution)/shard_map/ppermute | solution.py:478
  9.3 4.7 %collective-permute-start.4 = (f32[16,128]{1,0:T(8,128)S(1)}, f32[16,128]{1,0:T(8,128)S(1)}, u32[]{:S(2)}, u32[]{:S(2)}) collective-permute-start(f32[16,128]{1,0:T(8,128)S(1)} %get-tuple-element.29.refs_4_), channel_id=1, source_target_pairs={{0,2},{1,3},{2,0},{3,1},{4,6},{5,7},{6,4},{7,5},{8,10},{9,11},{10,... | collective-permute-start | bytes 24584 | tf_op jit(solution)/shard_map/ppermute | solution.py:481
  11.9 5.4 %collective-permute-start.3 = (f32[16,128]{1,0:T(8,128)S(1)}, f32[16,128]{1,0:T(8,128)S(1)}, u32[]{:S(2)}, u32[]{:S(2)}) collective-permute-start(f32[16,128]{1,0:T(8,128)S(1)} %get-tuple-element.29.refs_4_), channel_id=1, source_target_pairs={{0,3},{1,2},{2,1},{3,0},{4,7},{5,6},{6,5},{7,4},{8,11},{9,10},{10,... | collective-permute-start | bytes 24584 | tf_op jit(solution)/shard_map/ppermute | solution.py:481
  20.9 9.6 %collective-permute-start.5 = (f32[74,8,128]{2,1,0:T(8,128)S(1)}, f32[74,8,128]{2,1,0:T(8,128)S(1)}, u32[]{:S(2)}, u32[]{:S(2)}) collective-permute-start(f32[74,8,128]{2,1,0:T(8,128)S(1)} %get-tuple-element.31), channel_id=1, source_target_pairs={{0,1},{1,0},{2,3},{3,2},{4,5},{5,4},{6,7},{7,6},{8,9},{9,8},{10,11... | collective-permute-start | bytes 909320 | tf_op jit(solution)/shard_map/ppermute | solution.py:476
  21.0 9.5 %collective-permute-start.6 = (f32[592,128]{1,0:T(8,128)S(1)}, f32[592,128]{1,0:T(8,128)S(1)}, u32[]{:S(2)}, u32[]{:S(2)}) collective-permute-start(f32[592,128]{1,0:T(8,128)S(1)} %get-tuple-element.32), channel_id=1, source_target_pairs={{0,4},{4,8},{8,12},{12,16},{16,20},{20,24},{24,28},{28,0},{1,5},{5... | collective-permute-start | bytes 909320 | tf_op jit(solution)/shard_map/ppermute | solution.py:477
  21.1 9.5 %collective-permute-start.7 = (f32[592,128]{1,0:T(8,128)S(1)}, f32[592,128]{1,0:T(8,128)S(1)}, u32[]{:S(2)}, u32[]{:S(2)}) collective-permute-start(f32[592,128]{1,0:T(8,128)S(1)} %get-tuple-element.33), channel_id=1, source_target_pairs={{4,0},{8,4},{12,8},{16,12},{20,16},{24,20},{28,24},{0,28},{5,1},{9... | collective-permute-start | bytes 909320 | tf_op jit(solution)/shard_map/ppermute | solution.py:478
  23.7 4.7 %collective-permute-start.9 = (f32[16,128]{1,0:T(8,128)S(1)}, f32[16,128]{1,0:T(8,128)S(1)}, u32[]{:S(2)}, u32[]{:S(2)}) collective-permute-start(f32[16,128]{1,0:T(8,128)S(1)} %get-tuple-element.34.refs_4_), channel_id=1, source_target_pairs={{0,2},{1,3},{2,0},{3,1},{4,6},{5,7},{6,4},{7,5},{8,10},{9,11},{10,... | collective-permute-start | bytes 24584 | tf_op jit(solution)/shard_map/ppermute | solution.py:481
  24.8 5.7 %collective-permute-start.8 = (f32[16,128]{1,0:T(8,128)S(1)}, f32[16,128]{1,0:T(8,128)S(1)}, u32[]{:S(2)}, u32[]{:S(2)}) collective-permute-start(f32[16,128]{1,0:T(8,128)S(1)} %get-tuple-element.34.refs_4_), channel_id=1, source_target_pairs={{0,3},{1,2},{2,1},{3,0},{4,7},{5,6},{6,5},{7,4},{8,11},{9,10},{10,... | collective-permute-start | bytes 24584 | tf_op jit(solution)/shard_map/ppermute | solution.py:481
  34.1 11.7 %collective-permute-start.10 = (f32[74,8,128]{2,1,0:T(8,128)S(1)}, f32[74,8,128]{2,1,0:T(8,128)S(1)}, u32[]{:S(2)}, u32[]{:S(2)}) collective-permute-start(f32[74,8,128]{2,1,0:T(8,128)S(1)} %get-tuple-element.36), channel_id=1, source_target_pairs={{0,1},{1,0},{2,3},{3,2},{4,5},{5,4},{6,7},{7,6},{8,9},{9,8},{10,11... | collective-permute-start | bytes 909320 | tf_op jit(solution)/shard_map/ppermute | solution.py:476
  36.1 10.3 %collective-permute-start.11 = (f32[592,128]{1,0:T(8,128)S(1)}, f32[592,128]{1,0:T(8,128)S(1)}, u32[]{:S(2)}, u32[]{:S(2)}) collective-permute-start(f32[592,128]{1,0:T(8,128)S(1)} %get-tuple-element.37), channel_id=1, source_target_pairs={{0,4},{4,8},{8,12},{12,16},{16,20},{20,24},{24,28},{28,0},{1,5},{5... | collective-permute-start | bytes 909320 | tf_op jit(solution)/shard_map/ppermute | solution.py:477
  36.5 9.9 %collective-permute-start.12 = (f32[592,128]{1,0:T(8,128)S(1)}, f32[592,128]{1,0:T(8,128)S(1)}, u32[]{:S(2)}, u32[]{:S(2)}) collective-permute-start(f32[592,128]{1,0:T(8,128)S(1)} %get-tuple-element.38), channel_id=1, source_target_pairs={{4,0},{8,4},{12,8},{16,12},{20,16},{24,20},{28,24},{0,28},{5,1},{9... | collective-permute-start | bytes 909320 | tf_op jit(solution)/shard_map/ppermute | solution.py:478
  38.7 4.9 %collective-permute-start.14 = (f32[16,128]{1,0:T(8,128)S(1)}, f32[16,128]{1,0:T(8,128)S(1)}, u32[]{:S(2)}, u32[]{:S(2)}) collective-permute-start(f32[16,128]{1,0:T(8,128)S(1)} %get-tuple-element.39.refs_4_), channel_id=1, source_target_pairs={{0,2},{1,3},{2,0},{3,1},{4,6},{5,7},{6,4},{7,5},{8,10},{9,11},{10,... | collective-permute-start | bytes 24584 | tf_op jit(solution)/shard_map/ppermute | solution.py:481
  40.3 5.4 %collective-permute-start.13 = (f32[16,128]{1,0:T(8,128)S(1)}, f32[16,128]{1,0:T(8,128)S(1)}, u32[]{:S(2)}, u32[]{:S(2)}) collective-permute-start(f32[16,128]{1,0:T(8,128)S(1)} %get-tuple-element.39.refs_4_), channel_id=1, source_target_pairs={{0,3},{1,2},{2,1},{3,0},{4,7},{5,6},{6,5},{7,4},{8,11},{9,10},{10,... | collective-permute-start | bytes 24584 | tf_op jit(solution)/shard_map/ppermute | solution.py:481
  49.9 10.3 %collective-permute-start.15 = (f32[74,8,128]{2,1,0:T(8,128)S(1)}, f32[74,8,128]{2,1,0:T(8,128)S(1)}, u32[]{:S(2)}, u32[]{:S(2)}) collective-permute-start(f32[74,8,128]{2,1,0:T(8,128)S(1)} %get-tuple-element.41), channel_id=1, source_target_pairs={{0,1},{1,0},{2,3},{3,2},{4,5},{5,4},{6,7},{7,6},{8,9},{9,8},{10,11... | collective-permute-start | bytes 909320 | tf_op jit(solution)/shard_map/ppermute | solution.py:476
  50.0 10.3 %collective-permute-start.16 = (f32[592,128]{1,0:T(8,128)S(1)}, f32[592,128]{1,0:T(8,128)S(1)}, u32[]{:S(2)}, u32[]{:S(2)}) collective-permute-start(f32[592,128]{1,0:T(8,128)S(1)} %get-tuple-element.42), channel_id=1, source_target_pairs={{0,4},{4,8},{8,12},{12,16},{16,20},{20,24},{24,28},{28,0},{1,5},{5... | collective-permute-start | bytes 909320 | tf_op jit(solution)/shard_map/ppermute | solution.py:477
  50.4 9.9 %collective-permute-start.17 = (f32[592,128]{1,0:T(8,128)S(1)}, f32[592,128]{1,0:T(8,128)S(1)}, u32[]{:S(2)}, u32[]{:S(2)}) collective-permute-start(f32[592,128]{1,0:T(8,128)S(1)} %get-tuple-element.43), channel_id=1, source_target_pairs={{4,0},{8,4},{12,8},{16,12},{20,16},{24,20},{28,24},{0,28},{5,1},{9... | collective-permute-start | bytes 909320 | tf_op jit(solution)/shard_map/ppermute | solution.py:478
  52.7 4.8 %collective-permute-start.19 = (f32[16,128]{1,0:T(8,128)S(1)}, f32[16,128]{1,0:T(8,128)S(1)}, u32[]{:S(2)}, u32[]{:S(2)}) collective-permute-start(f32[16,128]{1,0:T(8,128)S(1)} %get-tuple-element.44.refs_4_), channel_id=1, source_target_pairs={{0,2},{1,3},{2,0},{3,1},{4,6},{5,7},{6,4},{7,5},{8,10},{9,11},{10,... | collective-permute-start | bytes 24584 | tf_op jit(solution)/shard_map/ppermute | solution.py:481
  54.8 5.4 %collective-permute-start.18 = (f32[16,128]{1,0:T(8,128)S(1)}, f32[16,128]{1,0:T(8,128)S(1)}, u32[]{:S(2)}, u32[]{:S(2)}) collective-permute-start(f32[16,128]{1,0:T(8,128)S(1)} %get-tuple-element.44.refs_4_), channel_id=1, source_target_pairs={{0,3},{1,2},{2,1},{3,0},{4,7},{5,6},{6,5},{7,4},{8,11},{9,10},{10,... | collective-permute-start | bytes 24584 | tf_op jit(solution)/shard_map/ppermute | solution.py:481

commit v2 on v1

--- a/solution.py
+++ b/solution.py
@@ -21,7 +21,6 @@
 FIELDS = 9
 KERNEL_VMEM = 16 * 1024 * 1024
 ALL_VMEM = 64 * 1024 * 1024
-highest = lax.Precision.HIGHEST
 
 vmax_speed = 4.5
 courant = 0.5
@@ -144,19 +143,25 @@
             for d in range(2):
                 mirror[sz.mirror_index(d, f, t)] = state[pl.ds(base + (Y - 1 - d) * SUB, SUB), :]
             positive = t >= sz.half
-            out, first = (right, SUB - 2) if positive else (left, 0)
+            out = right if positive else left
             side = sz.side_base(f, t)
-            for c in range(2):
-                for part in range(0, Y, SUB):
-                    edge = state[pl.ds(base + part * SUB + first + c, SUB, stride=SUB), :]
-                    out[pl.ds(side + 2 * part + c, SUB, stride=2), :] = edge
+            _, x1, x2 = beam_weights(x_speed(sz, t // sz.kg))
+            ends = (SUB - 1, SUB - 2) if positive else (0, 1)
+            for part in range(0, Y, SUB):
+                near, far = [
+                    state[pl.ds(base + part * SUB + c, SUB, stride=SUB), :] for c in ends
+                ]
+                pair = (x1 * near + x2 * far, x2 * near)
+                for c in range(2):
+                    value = pair[c] if positive else pair[1 - c]
+                    out[pl.ds(side + 2 * part + c, SUB, stride=2), :] = value
     pad = jnp.zeros((SUB, LANES), jnp.float32)
     for out in (right, left):
         out[0:SUB, :] = pad
         out[sz.side_rows - SUB : sz.side_rows, :] = pad
 
 
-def wall_kernel(sz, type_ref, index_ref, temps_ref, acc_ref, wall):
+def wall_kernel(sz, type_ref, index_ref, temps_ref, acc_ref, wall, xw, yw, emission):
     face = 1 - lax.axis_index("vert") % 2
     column = sub()
     kind = jnp.zeros_like(column)
@@ -188,9 +193,25 @@
         inward = sz.weight * along * across / (math.pi * temp)
         heat = jnp.where(entry == t, temp, heat)
         denom = jnp.where(entry == t, inward, denom)
-    wall[0] = alpha / (denom * (math.pi * heat))
-    wall[1] = 1.0 - alpha
-    wall[2] = heat
+    wall[0] = 1.0 - alpha
+    emitted = alpha / (denom * (math.pi * heat))
+    vert_index = lax.axis_index("vert")
+    inv_heat = 1.0 / heat
+    wall_y = []
+    for kg in range(sz.kg):
+        vy = y_speed(sz, vert_index, kg)
+        for r, value in enumerate((vy,) + beam_weights(vy)):
+            yw[4 * kg + r] = value
+        wall_y.append(masked(inside(sz, kg), emitted * jnp.exp(-vy * vy * inv_heat)))
+    for xg in range(sz.xg):
+        vx = x_speed(sz, xg)
+        for r, value in enumerate((vx,) + beam_weights(vx)):
+            xw[4 * xg + r] = value
+        wall_x = jnp.exp(-vx * vx * inv_heat)
+        for kg in range(sz.kg):
+            diffuse = wall_x * wall_y[kg]
+            emission[xg * sz.kg + kg] = diffuse
+            emission[sz.tiles + xg * sz.kg + kg] = 0.5 * heat * diffuse
 
 
 def chunk_copy(sz, source, target, sems, f, kg):
@@ -263,65 +284,89 @@
     return [ux, uy, inv_t, amount, scale * qx, scale * qy, 0.5 * theta, rate, flux]
 
 
-def step_kernel(sz, last, *refs):
-    refs = list(refs)
-    state, mirror_in, right_in, left_in, packet_in, wall = refs[:6]
-    others = refs[6 : 6 + sz.vert - 2]
-    rest = refs[6 + sz.vert - 2 :]
-    if last:
-        (result, spread, ghosts, xw, yw, out, turn, final, sems) = rest
-    else:
-        (out, mirror, packet, right, left, spread, ghosts, xw, yw, sums_ref) = rest
-    vert_index = lax.axis_index("vert")
-    parity = vert_index % 2
-
-    tot = [packet_in[SUB * b : SUB * b + SUB, :] + mirror_in[sz.mirror_blocks + b] for b in range(2)]
-    for other in others:
-        tot = [tot[b] + other[SUB * b : SUB * b + SUB, :] for b in range(2)]
-    rows = fields_of(parity, tot)
+def advect_kernel(sz, state, xw, yw, out):
+    column = sub()
+
+    def advance(step, near_at, far_at):
+        for xg in range(sz.xg):
+            x0 = 1.0 + xw[4 * xg + 1]
+            x1, x2 = xw[4 * xg + 2], xw[4 * xg + 3]
+            for kg in range(sz.kg):
+                t = xg * sz.kg + kg
+                c0 = x0 + yw[4 * kg + 1]
+                y1, y2 = yw[4 * kg + 2], yw[4 * kg + 3]
+                for f in range(2):
+                    at = sz.base(f, t) + step * SUB
+                    v = state[block(at), :]
+                    if t >= sz.half:
+                        one = jnp.where(column < 1, 0.0, state[pl.ds(at - 1, SUB), :])
+                        two = jnp.where(column < 2, 0.0, state[pl.ds(at - 2, SUB), :])
+                    else:
+                        one = jnp.where(column >= SUB - 1, 0.0, state[pl.ds(at + 1, SUB), :])
+                        two = jnp.where(column >= SUB - 2, 0.0, state[pl.ds(at + 2, SUB), :])
+                    moved = v * c0 + (x1 * one + x2 * two)
+                    if near_at:
+                        moved = moved + y1 * state[block(at - SUB), :]
+                    if far_at:
+                        moved = moved + y2 * state[block(at - 2 * SUB), :]
+                    out[block(at), :] = moved
+
+    advance(0, False, False)
+    advance(1, True, False)
+
+    def body(step, carry):
+        advance(step, True, True)
+        return carry
+
+    lax.fori_loop(2, Y, body, 0)
+
+
+def spread_fields(sz, rows, spread):
     index = lax.broadcasted_iota(jnp.int32, (ROWS, LANES), 0)
     table = jnp.zeros((ROWS, sz.cells), jnp.float32)
     for r, value in enumerate(rows):
         table = jnp.where(index == r, value, table)
+    parts = []
+    for _ in range(3):
+        part = table.astype(jnp.bfloat16)
+        parts.append(part)
+        table = table - part.astype(jnp.float32)
+    parts = jnp.concatenate(parts, axis=0)
+    index = lax.broadcasted_iota(jnp.int32, (3 * ROWS, LANES), 0) % ROWS
+    picks = [(index == r).astype(jnp.float32).astype(jnp.bfloat16) for r in range(FIELDS)]
+    wide = lax.dot_general(
+        parts, jnp.concatenate(picks, axis=1), (((0,), (0,)), ((), ())),
+        preferred_element_type=jnp.float32,
+    )
     for r in range(FIELDS):
-        pick = (index == r).astype(jnp.float32)
-        spread[r] = lax.dot_general(
-            table, pick, (((0,), (0,)), ((), ())),
-            precision=highest, preferred_element_type=jnp.float32,
-        )
-
-    for xg in range(sz.xg):
-        speed = x_speed(sz, xg)
-        for r, value in enumerate((speed,) + beam_weights(speed)):
-            xw[4 * xg + r] = value
-    for kg in range(sz.kg):
-        speed = y_speed(sz, vert_index, kg)
-        for r, value in enumerate((speed,) + beam_weights(speed)):
-            yw[4 * kg + r] = value
-
-    inv_heat = 1.0 / wall[2]
-    half_heat = 0.5 * wall[2]
-    keep = wall[1]
-    emitted = spread[FIELDS - 1, block(real_row(parity, 0) * SUB), :] * wall[0]
-    wall_y = []
-    for kg in range(sz.kg):
-        vy = yw[4 * kg]
-        wall_y.append(masked(inside(sz, kg), emitted * jnp.exp(-vy * vy * inv_heat)))
-    for xg in range(sz.xg):
-        vx = xw[4 * xg]
-        wall_x = jnp.exp(-vx * vx * inv_heat)
-        for kg in range(sz.kg):
-            diffuse = wall_x * wall_y[kg]
-            t = xg * sz.kg + kg
-            for f in range(2):
-                add = half_heat * diffuse if f else diffuse
-                for d in range(2):
-                    at = sz.mirror_index(d, f, t)
-                    ghosts[at] = keep * mirror_in[at] + add
-
+        spread[r] = wide[:, r * LANES : (r + 1) * LANES]
+
+
+def step_kernel(sz, last, *refs):
+    refs = list(refs)
+    state, inner, mirror_in, right_in, left_in, packet_in, wall, xw, yw, emission = refs[:10]
+    others = refs[10 : 10 + sz.vert - 2]
+    rest = refs[10 + sz.vert - 2 :]
+    if last:
+        (result, spread, out, turn, final, sems) = rest
+    else:
+        (out, mirror, packet, right, left, spread, sums_ref) = rest
+    vert_index = lax.axis_index("vert")
+    parity = vert_index % 2
+
+    tot = [packet_in[SUB * b : SUB * b + SUB, :] + mirror_in[sz.mirror_blocks + b] for b in range(2)]
+    for other in others:
+        tot = [tot[b] + other[SUB * b : SUB * b + SUB, :] for b in range(2)]
+    spread_fields(sz, fields_of(parity, tot), spread)
+
+    keep = wall[0]
+    flux = spread[FIELDS - 1, block(real_row(parity, 0) * SUB), :]
     column = sub()
 
-    def advance(step, upstream):
+    def ghost(d, f, t):
+        return keep * mirror_in[sz.mirror_index(d, f, t)] + flux * emission[f * sz.tiles + t]
+
+    def advance(step, beyond):
         y = real_row(parity, step)
         ux, uy, inv_t, amount, px, py, half_theta, rate = [
             spread[r, block(y * SUB), :] for r in range(FIELDS - 1)
@@ -338,36 +383,26 @@
             cx_sq = cx * cx * inv_t
             ex = jnp.exp(-cx_sq)
             pxs = px * cx
-            x0 = (1.0 + xw[4 * xg + 1]) - rate
-            x1, x2 = xw[4 * xg + 2], xw[4 * xg + 3]
             sums = None
             for kg in range(sz.kg):
                 t = xg * sz.kg + kg
-                positive = t >= sz.half
                 ey, pys, cys = along_y[kg]
                 maxwell = ex * ey
                 p = pxs + pys
                 sg = maxwell * (1.0 + p * (cx_sq + cys))
                 sh = half_theta * (sg + p * maxwell)
-                c0 = x0 + yw[4 * kg + 1]
-                y1, y2 = yw[4 * kg + 2], yw[4 * kg + 3]
                 values = []
                 for f, source in ((0, sg), (1, sh)):
                     at = sz.base(f, t) + step * SUB
                     side = sz.side_base(f, t) + 2 * step
-                    v = state[block(at), :]
-                    if positive:
-                        one = jnp.where(column < 1, right_in[pl.ds(side + 1, SUB), :], state[pl.ds(at - 1, SUB), :])
-                        two = jnp.where(column < 2, right_in[pl.ds(side, SUB), :], state[pl.ds(at - 2, SUB), :])
+                    if t >= sz.half:
+                        edge = jnp.where(column < 2, right_in[pl.ds(side, SUB), :], 0.0)
                     else:
-                        one = jnp.where(
-                            column >= SUB - 1, left_in[pl.ds(side - (SUB - 1), SUB), :], state[pl.ds(at + 1, SUB), :]
-                        )
-                        two = jnp.where(
-                            column >= SUB - 2, left_in[pl.ds(side - (SUB - 2), SUB), :], state[pl.ds(at + 2, SUB), :]
-                        )
-                    near, far = upstream(f, t, at)
-                    moved = (v * c0 + source) + (x1 * one + x2 * two) + (y1 * near + y2 * far)
+                        start = side - (SUB - 2)
+                        edge = jnp.where(column >= SUB - 2, left_in[pl.ds(start, SUB), :], 0.0)
+                    moved = (inner[block(at), :] + edge) + (source - rate * state[block(at), :])
+                    if beyond is not None:
+                        moved = moved + beyond(f, t, yw[4 * kg + 2], yw[4 * kg + 3])
                     out[block(at), :] = moved
                     values.append(moved)
                 if not last:
@@ -377,14 +412,11 @@
         if not last:
             put_sums(sums_ref, y, totals)
 
-    def ghost(d, f, t):
-        return ghosts[sz.mirror_index(d, f, t)]
-
-    advance(0, lambda f, t, at: (ghost(0, f, t), ghost(1, f, t)))
-    advance(1, lambda f, t, at: (state[block(at - SUB), :], ghost(0, f, t)))
+    advance(0, lambda f, t, y1, y2: y1 * ghost(0, f, t) + y2 * ghost(1, f, t))
+    advance(1, lambda f, t, y1, y2: y2 * ghost(0, f, t))
 
     def body(step, carry):
-        advance(step, lambda f, t, at: (state[block(at - SUB), :], state[block(at - 2 * SUB), :]))
+        advance(step, None)
         return carry
 
     lax.fori_loop(2, Y, body, 0)
@@ -438,12 +470,7 @@
     bytes_moved = 2 * distribution.size * 4
     sums_scratch = pltpu.VMEM((FIELDS, sz.cells, LANES), jnp.float32)
     turn_scratch = pltpu.VMEM((2, sz.cells, LANES), jnp.float32)
-    step_scratch = [
-        pltpu.VMEM((FIELDS, sz.cells, LANES), jnp.float32),
-        pltpu.VMEM((sz.mirror_blocks, SUB, LANES), jnp.float32),
-        pltpu.VMEM((4 * sz.xg, SUB, LANES), jnp.float32),
-        pltpu.VMEM((4 * sz.kg, SUB, LANES), jnp.float32),
-    ]
+    step_scratch = [pltpu.VMEM((FIELDS, sz.cells, LANES), jnp.float32)]
     first_vmem = ALL_VMEM - 26 * distribution.size
     stage = [
         pltpu.VMEM(distribution.shape, jnp.float32),
@@ -461,11 +488,14 @@
         compiler_params=pltpu.CompilerParams(vmem_limit_bytes=first_vmem),
         name="first",
     )(distribution)
-    wall = pl.pallas_call(
+    tables = pl.pallas_call(
         functools.partial(wall_kernel, sz),
-        out_shape=jax.ShapeDtypeStruct((3, SUB, LANES), jnp.float32),
+        out_shape=tuple(
+            jax.ShapeDtypeStruct((count, SUB, LANES), jnp.float32)
+            for count in (1, 4 * sz.xg, 4 * sz.kg, 2 * sz.tiles)
+        ),
         in_specs=[smem] * 4,
-        out_specs=vmem,
+        out_specs=(vmem,) * 4,
         compiler_params=pltpu.CompilerParams(vmem_limit_bytes=KERNEL_VMEM),
         name="walls",
     )(wall_type, wall_temp_index, wall_temps, accommodation)
@@ -479,6 +509,17 @@
         others = []
         for mask in range(vert - 1, 1, -1):
             others.append(lax.ppermute(packet, "vert", [(s, s ^ mask) for s in range(vert)]))
+        inner = pl.pallas_call(
+            functools.partial(advect_kernel, sz),
+            out_shape=jax.ShapeDtypeStruct((sz.state_rows, LANES), jnp.float32),
+            in_specs=[vmem] * 3,
+            out_specs=vmem,
+            cost_estimate=pl.CostEstimate(
+                flops=12 * distribution.size, bytes_accessed=bytes_moved, transcendentals=0
+            ),
+            compiler_params=pltpu.CompilerParams(vmem_limit_bytes=KERNEL_VMEM),
+            name="advect",
+        )(state, tables[1], tables[2])
         if last:
             scratch = step_scratch + [pltpu.VMEM((sz.state_rows, LANES), jnp.float32), turn_scratch] + stage
         else:
@@ -486,7 +527,7 @@
         result = pl.pallas_call(
             functools.partial(step_kernel, sz, last),
             out_shape=(final_shape,) if last else shapes(sz),
-            in_specs=[vmem] * (6 + len(others)),
+            in_specs=[vmem] * (10 + len(others)),
             out_specs=(hbm,) if last else (vmem,) * 5,
             scratch_shapes=scratch,
             cost_estimate=pl.CostEstimate(
@@ -494,7 +535,7 @@
             ),
             compiler_params=pltpu.CompilerParams(vmem_limit_bytes=KERNEL_VMEM),
             name="last" if last else "step",
-        )(state, mirror_in, right_in, left_in, packet, wall, *others)
+        )(state, inner, mirror_in, right_in, left_in, packet, *tables, *others)
         if last:
             (state,) = result
         else:

time: 65.3 us -> 60.4 us (0.925)
  waiting for transfers between devices: 15.7 us -> 10.9 us
    pallas_call x4, Pallas kernels: 15.5 us -> 10.6 us  [on_device(): pl.pallas_call(functools.partial(step_kernel, sz, last), out_shape=(final...]
    pallas_call x1 -> x5, Pallas kernels: 0.68 us -> 5.43 us  [the longest x4 4.73 us: on_device(): pl.pallas_call(functools.partial(advect_kernel, sz), out_shape=jax.ShapeD...]
    ppermute x8, waiting for transfers between devices: 15 us -> 10.3 us  [on_device(): lax.ppermute(packet, 'vert', [(s, s ^ mask) for s in range(vert)])]
  transfers between devices with their start and end apart: 20 -> 20, of which waited for: 9 -> 6; matrix products, arithmetic and copies ran while one was open for 0% -> 0% of each run, Pallas kernels for 1% -> 9%
where the time goes in v2:
time: 60.4 us; the launch traced here: 60.3 us
  starting transfers between devices  29.6 us (49%)
  Pallas kernels  19.6 us (32%)
  waiting for transfers between devices  10.9 us (18%)
    ppermute x8, starting transfers between devices, on_device(): lax.ppermute(packet, 'vert', [(s, s ^ mask) for s in range(vert)])  13.7 us
    pallas_call x4, Pallas kernels, on_device(): pl.pallas_call(functools.partial(step_kernel, sz, last), out_shape=(final...  10.6 us
    ppermute x8, waiting for transfers between devices, on_device(): lax.ppermute(packet, 'vert', [(s, s ^ mask) for s in range(vert)])  10.3 us
    ppermute x4, starting transfers between devices, on_device(): left_in = lax.ppermute(left, 'gx', back)  9.8 us
    ppermute x4, starting transfers between devices, on_device(): mirror_in = lax.ppermute(mirror, 'vert', [(s, s ^ 1) for s in range(vert)])  5.19 us
    pallas_call x4, Pallas kernels, on_device(): pl.pallas_call(functools.partial(advect_kernel, sz), out_shape=jax.ShapeD...  4.73 us
    pallas_call x1, Pallas kernels, on_device(): pl.pallas_call(functools.partial(first_kernel, sz), out_shape=shapes(sz),...  3.59 us
  transfers between devices with their start and end apart: 20, of which 6 were waited for; matrix products, arithmetic and copies ran while one was open for 0% of the time, Pallas kernels for 9%

profile of v2, /device:TPU:0, one launch (start us, length us, event | category | flops | bytes accessed | tf_op | source)
XLA Modules:
  0.0 60.3 jit_solution(3767585323284567810)
XLA Ops:
  0.0 0.0 copy-start.3
  0.0 0.0 copy-start.2
  0.0 0.0 copy-start.1
  0.0 0.0 copy-start
  0.0 3.6 %first.1 = (f32[4608,128]{1,0:T(8,128)S(1)}, f32[74,8,128]{2,1,0:T(8,128)S(1)}, f32[16,128]{1,0:T(8,128)S(1)}, f32[592,128]{1,0:T(8,128)S(1)}, f32[592,128]{1,0:T(8,128)S(1)}) custom-call(f32[2,24,96,128]{3,2,1,0:T(8,128)} %argument.1), custom_call_target="tpu_custom_call" | custom-call | flops 5898240 | bytes 4718592 | tf_op jit(solution)/shard_map/first/pallas_call | solution.py:479
  3.6 3.1 %collective-permute-start = (f32[74,8,128]{2,1,0:T(8,128)S(1)}, f32[74,8,128]{2,1,0:T(8,128)S(1)}, u32[]{:S(2)}, u32[]{:S(2)}) collective-permute-start(f32[74,8,128]{2,1,0:T(8,128)S(1)} %get-tuple-element.32), channel_id=1, source_target_pairs={{0,1},{1,0},{2,3},{3,2},{4,5},{5,4},{6,7},{7,6},{8,9},{9,8},{10,11... | collective-permute-start | bytes 909320 | tf_op jit(solution)/shard_map/ppermute | solution.py:506
  6.7 0.0 collective-permute-start.1
  6.7 2.6 %collective-permute-start.2 = (f32[592,128]{1,0:T(8,128)S(1)}, f32[592,128]{1,0:T(8,128)S(1)}, u32[]{:S(2)}, u32[]{:S(2)}) collective-permute-start(f32[592,128]{1,0:T(8,128)S(1)} %get-tuple-element.34), channel_id=1, source_target_pairs={{4,0},{8,4},{12,8},{16,12},{20,16},{24,20},{28,24},{0,28},{5,1},{9... | collective-permute-start | bytes 909320 | tf_op jit(solution)/shard_map/ppermute | solution.py:508
  9.3 2.6 %collective-permute-start.4 = (f32[16,128]{1,0:T(8,128)S(1)}, f32[16,128]{1,0:T(8,128)S(1)}, u32[]{:S(2)}, u32[]{:S(2)}) collective-permute-start(f32[16,128]{1,0:T(8,128)S(1)} %get-tuple-element.35.refs_5_), channel_id=1, source_target_pairs={{0,2},{1,3},{2,0},{3,1},{4,6},{5,7},{6,4},{7,5},{8,10},{9,11},{10,... | collective-permute-start | bytes 24584 | tf_op jit(solution)/shard_map/ppermute | solution.py:511
  11.9 0.0 collective-permute-start.3
  11.9 0.0 copy-done.3
  11.9 0.0 copy-done.2
  11.9 0.0 copy-done.1
  11.9 0.0 copy-done
  11.9 0.7 %walls.1 = (f32[1,8,128]{2,1,0:T(8,128)S(1)}, f32[24,8,128]{2,1,0:T(8,128)S(1)}, f32[12,8,128]{2,1,0:T(8,128)S(1)}, f32[36,8,128]{2,1,0:T(8,128)S(1)}) custom-call(s32[2,8]{1,0:T(2,128)S(1)} %copy-done, s32[2,8]{1,0:T(2,128)S(1)} %copy-done.1, f32[2]{0:T(128)S(1)} %copy-done.2, s32[3]{0:T(128)S(1)} %copy-done.3), custom_call_target="tpu_custom_call" | custom-call | tf_op jit(solution)/shard_map/walls/pallas_call | solution.py:491
  12.7 1.3 %advect.4.refs_1_ = f32[4608,128]{1,0:T(8,128)S(1)} custom-call(f32[4608,128]{1,0:T(8,128)S(1)} %get-tuple-element.29.state.refs_0_, f32[24,8,128]{2,1,0:T(8,128)S(1)} %get-tuple-element.30.xw.refs_7_, f32[12,8,128]{2,1,0:T(8,128)S(1)} %get-tuple-element.31.yw.refs_8_), custom_call_target="tpu_custom_call" | custom-call | flops 7077888 | bytes 4718592 | tf_op jit(solution)/shard_map/advect/pallas_call | solution.py:512
  14.0 0.0 collective-permute-done.4.refs_11_
  14.0 3.4 %collective-permute-done.3.refs_10_ = f32[16,128]{1,0:T(8,128)S(1)} collective-permute-done((f32[16,128]{1,0:T(8,128)S(1)}, f32[16,128]{1,0:T(8,128)S(1)}, u32[]{:S(2)}, u32[]{:S(2)}) %collective-permute-start.3) | collective-permute-done | bytes 8224 | tf_op jit(solution)/shard_map/ppermute | solution.py:511
  17.4 0.0 collective-permute-done.refs_2_
  17.4 0.0 collective-permute-done.1.refs_3_
  17.4 0.0 collective-permute-done.2.refs_4_
  17.4 2.4 %step.3 = (f32[4608,128]{1,0:T(8,128)S(1)}, f32[74,8,128]{2,1,0:T(8,128)S(1)}, f32[16,128]{1,0:T(8,128)S(1)}, f32[592,128]{1,0:T(8,128)S(1)}, f32[592,128]{1,0:T(8,128)S(1)}) custom-call(f32[4608,128]{1,0:T(8,128)S(1)} %get-tuple-element.29.state.refs_0_, f32[4608,128]{1,0:T(8,128)S(1)} %advect.4.refs_1_, f32[74,8,128]{2,1,0:T(8,128)S(1)} %collective-permute-done.refs_2_, ...), custom_call_target="tpu_custom_call" | custom-call | flops 23592960 | bytes 4718592 | tf_op jit(solution)/shard_map/step/pallas_call | solution.py:527
  19.7 0.1 collective-permute-start.5
  19.8 0.1 collective-permute-start.6
  19.9 2.6 %collective-permute-start.7 = (f32[592,128]{1,0:T(8,128)S(1)}, f32[592,128]{1,0:T(8,128)S(1)}, u32[]{:S(2)}, u32[]{:S(2)}) collective-permute-start(f32[592,128]{1,0:T(8,128)S(1)} %get-tuple-element.41), channel_id=1, source_target_pairs={{4,0},{8,4},{12,8},{16,12},{20,16},{24,20},{28,24},{0,28},{5,1},{9... | collective-permute-start | bytes 909320 | tf_op jit(solution)/shard_map/ppermute | solution.py:508
  22.5 1.1 %collective-permute-start.9 = (f32[16,128]{1,0:T(8,128)S(1)}, f32[16,128]{1,0:T(8,128)S(1)}, u32[]{:S(2)}, u32[]{:S(2)}) collective-permute-start(f32[16,128]{1,0:T(8,128)S(1)} %get-tuple-element.42.refs_5_), channel_id=1, source_target_pairs={{0,2},{1,3},{2,0},{3,1},{4,6},{5,7},{6,4},{7,5},{8,10},{9,11},{10,... | collective-permute-start | bytes 24584 | tf_op jit(solution)/shard_map/ppermute | solution.py:511
  23.6 3.2 %collective-permute-start.8 = (f32[16,128]{1,0:T(8,128)S(1)}, f32[16,128]{1,0:T(8,128)S(1)}, u32[]{:S(2)}, u32[]{:S(2)}) collective-permute-start(f32[16,128]{1,0:T(8,128)S(1)} %get-tuple-element.42.refs_5_), channel_id=1, source_target_pairs={{0,3},{1,2},{2,1},{3,0},{4,7},{5,6},{6,5},{7,4},{8,11},{9,10},{10,... | collective-permute-start | bytes 24584 | tf_op jit(solution)/shard_map/ppermute | solution.py:511
  26.8 1.1 %advect.5.refs_1_ = f32[4608,128]{1,0:T(8,128)S(1)} custom-call(f32[4608,128]{1,0:T(8,128)S(1)} %get-tuple-element.38.state.refs_0_, f32[24,8,128]{2,1,0:T(8,128)S(1)} %get-tuple-element.30.xw.refs_7_, f32[12,8,128]{2,1,0:T(8,128)S(1)} %get-tuple-element.31.yw.refs_8_), custom_call_target="tpu_custom_call" | custom-call | flops 7077888 | bytes 4718592 | tf_op jit(solution)/shard_map/advect/pallas_call | solution.py:512
  28.0 0.0 collective-permute-done.9.refs_11_
  28.0 1.3 %collective-permute-done.8.refs_10_ = f32[16,128]{1,0:T(8,128)S(1)} collective-permute-done((f32[16,128]{1,0:T(8,128)S(1)}, f32[16,128]{1,0:T(8,128)S(1)}, u32[]{:S(2)}, u32[]{:S(2)}) %collective-permute-start.8) | collective-permute-done | bytes 8224 | tf_op jit(solution)/shard_map/ppermute | solution.py:511
  29.3 0.0 collective-permute-done.5.refs_2_
  29.4 0.0 collective-permute-done.6.refs_3_
  29.4 0.0 collective-permute-done.7.refs_4_
  29.4 2.4 %step.4 = (f32[4608,128]{1,0:T(8,128)S(1)}, f32[74,8,128]{2,1,0:T(8,128)S(1)}, f32[16,128]{1,0:T(8,128)S(1)}, f32[592,128]{1,0:T(8,128)S(1)}, f32[592,128]{1,0:T(8,128)S(1)}) custom-call(f32[4608,128]{1,0:T(8,128)S(1)} %get-tuple-element.38.state.refs_0_, f32[4608,128]{1,0:T(8,128)S(1)} %advect.5.refs_1_, f32[74,8,128]{2,1,0:T(8,128)S(1)} %collective-permute-done.5.refs_2_, ...), custom_call_target="tpu_custom_call" | custom-call | flops 23592960 | bytes 4718592 | tf_op jit(solution)/shard_map/step/pallas_call | solution.py:527
  31.7 2.0 %collective-permute-start.10 = (f32[74,8,128]{2,1,0:T(8,128)S(1)}, f32[74,8,128]{2,1,0:T(8,128)S(1)}, u32[]{:S(2)}, u32[]{:S(2)}) collective-permute-start(f32[74,8,128]{2,1,0:T(8,128)S(1)} %get-tuple-element.44), channel_id=1, source_target_pairs={{0,1},{1,0},{2,3},{3,2},{4,5},{5,4},{6,7},{7,6},{8,9},{9,8},{10,11... | collective-permute-start | bytes 909320 | tf_op jit(solution)/shard_map/ppermute | solution.py:506
  33.7 0.4 collective-permute-start.11
  34.1 2.2 %collective-permute-start.12 = (f32[592,128]{1,0:T(8,128)S(1)}, f32[592,128]{1,0:T(8,128)S(1)}, u32[]{:S(2)}, u32[]{:S(2)}) collective-permute-start(f32[592,128]{1,0:T(8,128)S(1)} %get-tuple-element.46), channel_id=1, source_target_pairs={{4,0},{8,4},{12,8},{16,12},{20,16},{24,20},{28,24},{0,28},{5,1},{9... | collective-permute-start | bytes 909320 | tf_op jit(solution)/shard_map/ppermute | solution.py:508
  36.3 1.6 %collective-permute-start.14 = (f32[16,128]{1,0:T(8,128)S(1)}, f32[16,128]{1,0:T(8,128)S(1)}, u32[]{:S(2)}, u32[]{:S(2)}) collective-permute-start(f32[16,128]{1,0:T(8,128)S(1)} %get-tuple-element.47.refs_5_), channel_id=1, source_target_pairs={{0,2},{1,3},{2,0},{3,1},{4,6},{5,7},{6,4},{7,5},{8,10},{9,11},{10,... | collective-permute-start | bytes 24584 | tf_op jit(solution)/shard_map/ppermute | solution.py:511
  37.9 0.9 %collective-permute-start.13 = (f32[16,128]{1,0:T(8,128)S(1)}, f32[16,128]{1,0:T(8,128)S(1)}, u32[]{:S(2)}, u32[]{:S(2)}) collective-permute-start(f32[16,128]{1,0:T(8,128)S(1)} %get-tuple-element.47.refs_5_), channel_id=1, source_target_pairs={{0,3},{1,2},{2,1},{3,0},{4,7},{5,6},{6,5},{7,4},{8,11},{9,10},{10,... | collective-permute-start | bytes 24584 | tf_op jit(solution)/shard_map/ppermute | solution.py:511
  38.8 1.1 %advect.6.refs_1_ = f32[4608,128]{1,0:T(8,128)S(1)} custom-call(f32[4608,128]{1,0:T(8,128)S(1)} %get-tuple-element.43.state.refs_0_, f32[24,8,128]{2,1,0:T(8,128)S(1)} %get-tuple-element.30.xw.refs_7_, f32[12,8,128]{2,1,0:T(8,128)S(1)} %get-tuple-element.31.yw.refs_8_), custom_call_target="tpu_custom_call" | custom-call | flops 7077888 | bytes 4718592 | tf_op jit(solution)/shard_map/advect/pallas_call | solution.py:512
  40.0 1.3 %collective-permute-done.14.refs_11_ = f32[16,128]{1,0:T(8,128)S(1)} collective-permute-done((f32[16,128]{1,0:T(8,128)S(1)}, f32[16,128]{1,0:T(8,128)S(1)}, u32[]{:S(2)}, u32[]{:S(2)}) %collective-permute-start.14) | collective-permute-done | bytes 8224 | tf_op jit(solution)/shard_map/ppermute | solution.py:511
  41.3 2.1 %collective-permute-done.13.refs_10_ = f32[16,128]{1,0:T(8,128)S(1)} collective-permute-done((f32[16,128]{1,0:T(8,128)S(1)}, f32[16,128]{1,0:T(8,128)S(1)}, u32[]{:S(2)}, u32[]{:S(2)}) %collective-permute-start.13) | collective-permute-done | bytes 8224 | tf_op jit(solution)/shard_map/ppermute | solution.py:511
  43.4 0.0 collective-permute-done.10.refs_2_
  43.4 0.6 collective-permute-done.11.refs_3_
  44.0 0.0 collective-permute-done.12.refs_4_
  44.0 2.3 %step.5 = (f32[4608,128]{1,0:T(8,128)S(1)}, f32[74,8,128]{2,1,0:T(8,128)S(1)}, f32[16,128]{1,0:T(8,128)S(1)}, f32[592,128]{1,0:T(8,128)S(1)}, f32[592,128]{1,0:T(8,128)S(1)}) custom-call(f32[4608,128]{1,0:T(8,128)S(1)} %get-tuple-element.43.state.refs_0_, f32[4608,128]{1,0:T(8,128)S(1)} %advect.6.refs_1_, f32[74,8,128]{2,1,0:T(8,128)S(1)} %collective-permute-done.10.refs_2_, ...), custom_call_target="tpu_custom_call" | custom-call | flops 23592960 | bytes 4718592 | tf_op jit(solution)/shard_map/step/pallas_call | solution.py:527
  46.4 0.1 collective-permute-start.15
  46.4 0.4 collective-permute-start.16
  46.8 2.3 %collective-permute-start.17 = (f32[592,128]{1,0:T(8,128)S(1)}, f32[592,128]{1,0:T(8,128)S(1)}, u32[]{:S(2)}, u32[]{:S(2)}) collective-permute-start(f32[592,128]{1,0:T(8,128)S(1)} %get-tuple-element.51), channel_id=1, source_target_pairs={{4,0},{8,4},{12,8},{16,12},{20,16},{24,20},{28,24},{0,28},{5,1},{9... | collective-permute-start | bytes 909320 | tf_op jit(solution)/shard_map/ppermute | solution.py:508
  49.1 2.1 %collective-permute-start.19 = (f32[16,128]{1,0:T(8,128)S(1)}, f32[16,128]{1,0:T(8,128)S(1)}, u32[]{:S(2)}, u32[]{:S(2)}) collective-permute-start(f32[16,128]{1,0:T(8,128)S(1)} %get-tuple-element.52.refs_5_), channel_id=1, source_target_pairs={{0,2},{1,3},{2,0},{3,1},{4,6},{5,7},{6,4},{7,5},{8,10},{9,11},{10,... | collective-permute-start | bytes 24584 | tf_op jit(solution)/shard_map/ppermute | solution.py:511
  51.3 2.2 %collective-permute-start.18 = (f32[16,128]{1,0:T(8,128)S(1)}, f32[16,128]{1,0:T(8,128)S(1)}, u32[]{:S(2)}, u32[]{:S(2)}) collective-permute-start(f32[16,128]{1,0:T(8,128)S(1)} %get-tuple-element.52.refs_5_), channel_id=1, source_target_pairs={{0,3},{1,2},{2,1},{3,0},{4,7},{5,6},{6,5},{7,4},{8,11},{9,10},{10,... | collective-permute-start | bytes 24584 | tf_op jit(solution)/shard_map/ppermute | solution.py:511
  53.5 1.1 %advect.7.refs_1_ = f32[4608,128]{1,0:T(8,128)S(1)} custom-call(f32[4608,128]{1,0:T(8,128)S(1)} %get-tuple-element.48.state.refs_0_, f32[24,8,128]{2,1,0:T(8,128)S(1)} %get-tuple-element.30.xw.refs_7_, f32[12,8,128]{2,1,0:T(8,128)S(1)} %get-tuple-element.31.yw.refs_8_), custom_call_target="tpu_custom_call" | custom-call | flops 7077888 | bytes 4718592 | tf_op jit(solution)/shard_map/advect/pallas_call | solution.py:512
  54.6 0.0 collective-permute-done.19.refs_11_
  54.6 2.1 %collective-permute-done.18.refs_10_ = f32[16,128]{1,0:T(8,128)S(1)} collective-permute-done((f32[16,128]{1,0:T(8,128)S(1)}, f32[16,128]{1,0:T(8,128)S(1)}, u32[]{:S(2)}, u32[]{:S(2)}) %collective-permute-start.18) | collective-permute-done | bytes 8224 | tf_op jit(solution)/shard_map/ppermute | solution.py:511
  56.7 0.0 collective-permute-done.15.refs_2_
  56.7 0.0 collective-permute-done.16.refs_3_
  56.7 0.0 collective-permute-done.17.refs_4_
  56.7 3.5 %last.1 = f32[2,24,96,128]{3,2,1,0:T(8,128)} custom-call(f32[4608,128]{1,0:T(8,128)S(1)} %get-tuple-element.48.state.refs_0_, f32[4608,128]{1,0:T(8,128)S(1)} %advect.7.refs_1_, f32[74,8,128]{2,1,0:T(8,128)S(1)} %collective-permute-done.15.refs_2_, f32[592,128]{1,0:T(8,128)S(1)} %collective-permute-done.16.refs_3_, ...), custom_call_target="tpu_custom_call" | custom-call | flops 23592960 | bytes 4718592 | tf_op jit(solution)/shard_map/last/pallas_call | solution.py:527
Async XLA Ops:
  0.0 11.9 %copy-start.3 = (s32[3]{0:T(128)S(1)}, s32[3]{0:T(128)}, u32[]{:S(2)}) copy-start(s32[3]{0:T(128)} %acc_ref.1) | copy-start | bytes 40
  0.0 11.9 %copy-start.2 = (f32[2]{0:T(128)S(1)}, f32[2]{0:T(128)}, u32[]{:S(2)}) copy-start(f32[2]{0:T(128)} %temps_ref.1) | copy-start | bytes 28
  0.0 11.9 %copy-start.1 = (s32[2,8]{1,0:T(2,128)S(1)}, s32[2,8]{1,0:T(2,128)}, u32[]{:S(2)}) copy-start(s32[2,8]{1,0:T(2,128)} %index_ref.1) | copy-start | bytes 196
  0.0 11.9 %copy-start = (s32[2,8]{1,0:T(2,128)S(1)}, s32[2,8]{1,0:T(2,128)}, u32[]{:S(2)}) copy-start(s32[2,8]{1,0:T(2,128)} %type_ref.1) | copy-start | bytes 196
  3.6 13.8 %collective-permute-start = (f32[74,8,128]{2,1,0:T(8,128)S(1)}, f32[74,8,128]{2,1,0:T(8,128)S(1)}, u32[]{:S(2)}, u32[]{:S(2)}) collective-permute-start(f32[74,8,128]{2,1,0:T(8,128)S(1)} %get-tuple-element.32), channel_id=1, source_target_pairs={{0,1},{1,0},{2,3},{3,2},{4,5},{5,4},{6,7},{7,6},{8,9},{9,8},{10,11... | collective-permute-start | bytes 909320 | tf_op jit(solution)/shard_map/ppermute | solution.py:506
  6.7 10.7 %collective-permute-start.1 = (f32[592,128]{1,0:T(8,128)S(1)}, f32[592,128]{1,0:T(8,128)S(1)}, u32[]{:S(2)}, u32[]{:S(2)}) collective-permute-start(f32[592,128]{1,0:T(8,128)S(1)} %get-tuple-element.33), channel_id=1, source_target_pairs={{0,4},{4,8},{8,12},{12,16},{16,20},{20,24},{24,28},{28,0},{1,5},{5... | collective-permute-start | bytes 909320 | tf_op jit(solution)/shard_map/ppermute | solution.py:507
  6.7 10.7 %collective-permute-start.2 = (f32[592,128]{1,0:T(8,128)S(1)}, f32[592,128]{1,0:T(8,128)S(1)}, u32[]{:S(2)}, u32[]{:S(2)}) collective-permute-start(f32[592,128]{1,0:T(8,128)S(1)} %get-tuple-element.34), channel_id=1, source_target_pairs={{4,0},{8,4},{12,8},{16,12},{20,16},{24,20},{28,24},{0,28},{5,1},{9... | collective-permute-start | bytes 909320 | tf_op jit(solution)/shard_map/ppermute | solution.py:508
  9.3 4.7 %collective-permute-start.4 = (f32[16,128]{1,0:T(8,128)S(1)}, f32[16,128]{1,0:T(8,128)S(1)}, u32[]{:S(2)}, u32[]{:S(2)}) collective-permute-start(f32[16,128]{1,0:T(8,128)S(1)} %get-tuple-element.35.refs_5_), channel_id=1, source_target_pairs={{0,2},{1,3},{2,0},{3,1},{4,6},{5,7},{6,4},{7,5},{8,10},{9,11},{10,... | collective-permute-start | bytes 24584 | tf_op jit(solution)/shard_map/ppermute | solution.py:511
  11.9 5.4 %collective-permute-start.3 = (f32[16,128]{1,0:T(8,128)S(1)}, f32[16,128]{1,0:T(8,128)S(1)}, u32[]{:S(2)}, u32[]{:S(2)}) collective-permute-start(f32[16,128]{1,0:T(8,128)S(1)} %get-tuple-element.35.refs_5_), channel_id=1, source_target_pairs={{0,3},{1,2},{2,1},{3,0},{4,7},{5,6},{6,5},{7,4},{8,11},{9,10},{10,... | collective-permute-start | bytes 24584 | tf_op jit(solution)/shard_map/ppermute | solution.py:511
  19.7 9.6 %collective-permute-start.5 = (f32[74,8,128]{2,1,0:T(8,128)S(1)}, f32[74,8,128]{2,1,0:T(8,128)S(1)}, u32[]{:S(2)}, u32[]{:S(2)}) collective-permute-start(f32[74,8,128]{2,1,0:T(8,128)S(1)} %get-tuple-element.39), channel_id=1, source_target_pairs={{0,1},{1,0},{2,3},{3,2},{4,5},{5,4},{6,7},{7,6},{8,9},{9,8},{10,11... | collective-permute-start | bytes 909320 | tf_op jit(solution)/shard_map/ppermute | solution.py:506
  19.8 9.5 %collective-permute-start.6 = (f32[592,128]{1,0:T(8,128)S(1)}, f32[592,128]{1,0:T(8,128)S(1)}, u32[]{:S(2)}, u32[]{:S(2)}) collective-permute-start(f32[592,128]{1,0:T(8,128)S(1)} %get-tuple-element.40), channel_id=1, source_target_pairs={{0,4},{4,8},{8,12},{12,16},{16,20},{20,24},{24,28},{28,0},{1,5},{5... | collective-permute-start | bytes 909320 | tf_op jit(solution)/shard_map/ppermute | solution.py:507
  19.9 9.5 %collective-permute-start.7 = (f32[592,128]{1,0:T(8,128)S(1)}, f32[592,128]{1,0:T(8,128)S(1)}, u32[]{:S(2)}, u32[]{:S(2)}) collective-permute-start(f32[592,128]{1,0:T(8,128)S(1)} %get-tuple-element.41), channel_id=1, source_target_pairs={{4,0},{8,4},{12,8},{16,12},{20,16},{24,20},{28,24},{0,28},{5,1},{9... | collective-permute-start | bytes 909320 | tf_op jit(solution)/shard_map/ppermute | solution.py:508
  22.5 5.5 %collective-permute-start.9 = (f32[16,128]{1,0:T(8,128)S(1)}, f32[16,128]{1,0:T(8,128)S(1)}, u32[]{:S(2)}, u32[]{:S(2)}) collective-permute-start(f32[16,128]{1,0:T(8,128)S(1)} %get-tuple-element.42.refs_5_), channel_id=1, source_target_pairs={{0,2},{1,3},{2,0},{3,1},{4,6},{5,7},{6,4},{7,5},{8,10},{9,11},{10,... | collective-permute-start | bytes 24584 | tf_op jit(solution)/shard_map/ppermute | solution.py:511
  23.6 5.7 %collective-permute-start.8 = (f32[16,128]{1,0:T(8,128)S(1)}, f32[16,128]{1,0:T(8,128)S(1)}, u32[]{:S(2)}, u32[]{:S(2)}) collective-permute-start(f32[16,128]{1,0:T(8,128)S(1)} %get-tuple-element.42.refs_5_), channel_id=1, source_target_pairs={{0,3},{1,2},{2,1},{3,0},{4,7},{5,6},{6,5},{7,4},{8,11},{9,10},{10,... | collective-permute-start | bytes 24584 | tf_op jit(solution)/shard_map/ppermute | solution.py:511
  31.7 11.7 %collective-permute-start.10 = (f32[74,8,128]{2,1,0:T(8,128)S(1)}, f32[74,8,128]{2,1,0:T(8,128)S(1)}, u32[]{:S(2)}, u32[]{:S(2)}) collective-permute-start(f32[74,8,128]{2,1,0:T(8,128)S(1)} %get-tuple-element.44), channel_id=1, source_target_pairs={{0,1},{1,0},{2,3},{3,2},{4,5},{5,4},{6,7},{7,6},{8,9},{9,8},{10,11... | collective-permute-start | bytes 909320 | tf_op jit(solution)/shard_map/ppermute | solution.py:506
  33.7 10.3 %collective-permute-start.11 = (f32[592,128]{1,0:T(8,128)S(1)}, f32[592,128]{1,0:T(8,128)S(1)}, u32[]{:S(2)}, u32[]{:S(2)}) collective-permute-start(f32[592,128]{1,0:T(8,128)S(1)} %get-tuple-element.45), channel_id=1, source_target_pairs={{0,4},{4,8},{8,12},{12,16},{16,20},{20,24},{24,28},{28,0},{1,5},{5... | collective-permute-start | bytes 909320 | tf_op jit(solution)/shard_map/ppermute | solution.py:507
  34.1 9.9 %collective-permute-start.12 = (f32[592,128]{1,0:T(8,128)S(1)}, f32[592,128]{1,0:T(8,128)S(1)}, u32[]{:S(2)}, u32[]{:S(2)}) collective-permute-start(f32[592,128]{1,0:T(8,128)S(1)} %get-tuple-element.46), channel_id=1, source_target_pairs={{4,0},{8,4},{12,8},{16,12},{20,16},{24,20},{28,24},{0,28},{5,1},{9... | collective-permute-start | bytes 909320 | tf_op jit(solution)/shard_map/ppermute | solution.py:508
  36.3 4.9 %collective-permute-start.14 = (f32[16,128]{1,0:T(8,128)S(1)}, f32[16,128]{1,0:T(8,128)S(1)}, u32[]{:S(2)}, u32[]{:S(2)}) collective-permute-start(f32[16,128]{1,0:T(8,128)S(1)} %get-tuple-element.47.refs_5_), channel_id=1, source_target_pairs={{0,2},{1,3},{2,0},{3,1},{4,6},{5,7},{6,4},{7,5},{8,10},{9,11},{10,... | collective-permute-start | bytes 24584 | tf_op jit(solution)/shard_map/ppermute | solution.py:511
  37.9 5.4 %collective-permute-start.13 = (f32[16,128]{1,0:T(8,128)S(1)}, f32[16,128]{1,0:T(8,128)S(1)}, u32[]{:S(2)}, u32[]{:S(2)}) collective-permute-start(f32[16,128]{1,0:T(8,128)S(1)} %get-tuple-element.47.refs_5_), channel_id=1, source_target_pairs={{0,3},{1,2},{2,1},{3,0},{4,7},{5,6},{6,5},{7,4},{8,11},{9,10},{10,... | collective-permute-start | bytes 24584 | tf_op jit(solution)/shard_map/ppermute | solution.py:511
  46.4 10.4 %collective-permute-start.15 = (f32[74,8,128]{2,1,0:T(8,128)S(1)}, f32[74,8,128]{2,1,0:T(8,128)S(1)}, u32[]{:S(2)}, u32[]{:S(2)}) collective-permute-start(f32[74,8,128]{2,1,0:T(8,128)S(1)} %get-tuple-element.49), channel_id=1, source_target_pairs={{0,1},{1,0},{2,3},{3,2},{4,5},{5,4},{6,7},{7,6},{8,9},{9,8},{10,11... | collective-permute-start | bytes 909320 | tf_op jit(solution)/shard_map/ppermute | solution.py:506
  46.4 10.3 %collective-permute-start.16 = (f32[592,128]{1,0:T(8,128)S(1)}, f32[592,128]{1,0:T(8,128)S(1)}, u32[]{:S(2)}, u32[]{:S(2)}) collective-permute-start(f32[592,128]{1,0:T(8,128)S(1)} %get-tuple-element.50), channel_id=1, source_target_pairs={{0,4},{4,8},{8,12},{12,16},{16,20},{20,24},{24,28},{28,0},{1,5},{5... | collective-permute-start | bytes 909320 | tf_op jit(solution)/shard_map/ppermute | solution.py:507
  46.8 9.9 %collective-permute-start.17 = (f32[592,128]{1,0:T(8,128)S(1)}, f32[592,128]{1,0:T(8,128)S(1)}, u32[]{:S(2)}, u32[]{:S(2)}) collective-permute-start(f32[592,128]{1,0:T(8,128)S(1)} %get-tuple-element.51), channel_id=1, source_target_pairs={{4,0},{8,4},{12,8},{16,12},{20,16},{24,20},{28,24},{0,28},{5,1},{9... | collective-permute-start | bytes 909320 | tf_op jit(solution)/shard_map/ppermute | solution.py:508
  49.1 5.5 %collective-permute-start.19 = (f32[16,128]{1,0:T(8,128)S(1)}, f32[16,128]{1,0:T(8,128)S(1)}, u32[]{:S(2)}, u32[]{:S(2)}) collective-permute-start(f32[16,128]{1,0:T(8,128)S(1)} %get-tuple-element.52.refs_5_), channel_id=1, source_target_pairs={{0,2},{1,3},{2,0},{3,1},{4,6},{5,7},{6,4},{7,5},{8,10},{9,11},{10,... | collective-permute-start | bytes 24584 | tf_op jit(solution)/shard_map/ppermute | solution.py:511
  51.3 5.4 %collective-permute-start.18 = (f32[16,128]{1,0:T(8,128)S(1)}, f32[16,128]{1,0:T(8,128)S(1)}, u32[]{:S(2)}, u32[]{:S(2)}) collective-permute-start(f32[16,128]{1,0:T(8,128)S(1)} %get-tuple-element.52.refs_5_), channel_id=1, source_target_pairs={{0,3},{1,2},{2,1},{3,0},{4,7},{5,6},{6,5},{7,4},{8,11},{9,10},{10,... | collective-permute-start | bytes 24584 | tf_op jit(solution)/shard_map/ppermute | solution.py:511

commit v3 on v2

--- a/solution.py
+++ b/solution.py
@@ -214,23 +214,25 @@
             emission[sz.tiles + xg * sz.kg + kg] = 0.5 * heat * diffuse
 
 
-def chunk_copy(sz, source, target, sems, f, kg):
-    rows = pl.ds(kg * PART_K, min(PART_K, sz.band - kg * PART_K))
+def group_copy(sz, source, target, sems, f, xg):
+    speeds = pl.ds(xg * PART_X, PART_X)
     return pltpu.make_async_copy(
-        source.at[f, rows], target.at[f, rows], sems.at[f * sz.kg + kg]
+        source.at[f, :, speeds], target.at[f, :, speeds], sems.at[f * sz.xg + xg]
     )
 
 
-def first_kernel(sz, argument, state, mirror, packet, right, left, sums_ref, turn, given, sems):
+def first_kernel(sz, argument, state, mirror, packet, right, left, sums_ref, turn_a, turn_b, given, sems):
     vert_index = lax.axis_index("vert")
     parity = vert_index % 2
-    for f in range(2):
+    for xg in range(sz.xg):
+        for f in range(2):
+            group_copy(sz, argument, given, sems, f, xg).start()
+    for xg in range(sz.xg):
+        turn = turn_b if xg % 2 else turn_a
+        for f in range(2):
+            group_copy(sz, argument, given, sems, f, xg).wait()
         for kg in range(sz.kg):
-            chunk_copy(sz, argument, given, sems, f, kg).start()
-    for f in range(2):
-        for kg in range(sz.kg):
-            chunk_copy(sz, argument, given, sems, f, kg).wait()
-            for xg in range(sz.xg):
+            for f in range(2):
                 parts = []
                 for k in range(kg * PART_K, (kg + 1) * PART_K):
                     if k < sz.band:
@@ -238,29 +240,24 @@
                     else:
                         parts.append(jnp.zeros((PART_X, sz.cells), jnp.float32))
                 turned = jnp.concatenate(parts, axis=0).T
-                t = xg * sz.kg + kg
-                slot = xg % 2
+                slot = 2 * kg + f
                 for x in range(SUB):
                     for part in range(0, Y, SUB):
                         piece = turned[x * Y + part : x * Y + part + SUB, :]
                         turn[slot, pl.ds(part * SUB + x, SUB, stride=SUB), :] = piece
-                base = sz.base(f, t)
-                for step in range(Y):
-                    y = real_row(parity, step)
-                    state[pl.ds(base + step * SUB, SUB), :] = turn[slot, block(y * SUB), :]
-
-    def step_body(step, carry):
-        totals = None
-        for xg in range(sz.xg):
+        vx = x_speed(sz, xg)
+        for step in range(Y):
+            y = real_row(parity, step)
             sums = None
             for kg in range(sz.kg):
-                g, h = [state[block(sz.base(f, xg * sz.kg + kg) + step * SUB), :] for f in range(2)]
+                g, h = [turn[2 * kg + f, block(y * SUB), :] for f in range(2)]
+                for f, value in enumerate((g, h)):
+                    state[pl.ds(sz.base(f, xg * sz.kg + kg) + step * SUB, SUB), :] = value
                 sums = add_columns(y_speed(sz, vert_index, kg), g, h, sums)
-            totals = add_group(x_speed(sz, xg), sums, totals)
-        put_sums(sums_ref, real_row(parity, step), totals)
-        return carry
-
-    lax.fori_loop(0, Y, step_body, 0)
+            for m, total in enumerate(add_group(vx, sums, None)):
+                if xg:
+                    total = total + sums_ref[m, block(y * SUB), :]
+                sums_ref[m, block(y * SUB), :] = total
     send(sz, vert_index, state, sums_ref, mirror, packet, right, left)
 
 
@@ -342,108 +339,155 @@
         spread[r] = wide[:, r * LANES : (r + 1) * LANES]
 
 
-def step_kernel(sz, last, *refs):
-    refs = list(refs)
-    state, inner, mirror_in, right_in, left_in, packet_in, wall, xw, yw, emission = refs[:10]
-    others = refs[10 : 10 + sz.vert - 2]
-    rest = refs[10 + sz.vert - 2 :]
-    if last:
-        (result, spread, out, turn, final, sems) = rest
-    else:
-        (out, mirror, packet, right, left, spread, sums_ref) = rest
-    vert_index = lax.axis_index("vert")
-    parity = vert_index % 2
-
+def received(sz, parity, mirror_in, packet_in, others, spread):
     tot = [packet_in[SUB * b : SUB * b + SUB, :] + mirror_in[sz.mirror_blocks + b] for b in range(2)]
     for other in others:
         tot = [tot[b] + other[SUB * b : SUB * b + SUB, :] for b in range(2)]
     spread_fields(sz, fields_of(parity, tot), spread)
 
-    keep = wall[0]
+
+def side_edge(sz, right_in, left_in, f, t, step):
+    column = sub()
+    side = sz.side_base(f, t) + 2 * step
+    if t >= sz.half:
+        return jnp.where(column < 2, right_in[pl.ds(side, SUB), :], 0.0)
+    start = side - (SUB - 2)
+    return jnp.where(column >= SUB - 2, left_in[pl.ds(start, SUB), :], 0.0)
+
+
+def field_rows(spread, y):
+    return [spread[r, block(y * SUB), :] for r in range(FIELDS - 1)]
+
+
+def part_y(sz, yw, kg, uy, inv_t, amount, py):
+    cy = yw[4 * kg] - uy
+    cy_sq = cy * cy * inv_t
+    return masked(inside(sz, kg), amount * jnp.exp(-cy_sq)), py * cy, cy_sq - 2.0
+
+
+def part_x(vx, ux, inv_t, px):
+    cx = vx - ux
+    cx_sq = cx * cx * inv_t
+    return jnp.exp(-cx_sq), px * cx, cx_sq
+
+
+def target(along_x, along_y, half_theta):
+    ex, pxs, cx_sq = along_x
+    ey, pys, cys = along_y
+    maxwell = ex * ey
+    p = pxs + pys
+    sg = maxwell * (1.0 + p * (cx_sq + cys))
+    return sg, half_theta * (sg + p * maxwell)
+
+
+def wall_part(sz, mirror_in, wall, emission, flux, yw):
+    def ghost(d, f, t):
+        return wall[0] * mirror_in[sz.mirror_index(d, f, t)] + flux * emission[f * sz.tiles + t]
+
+    def beyond(step, f, t):
+        kg = t % sz.kg
+        y1, y2 = yw[4 * kg + 2], yw[4 * kg + 3]
+        if step == 0:
+            return y1 * ghost(0, f, t) + y2 * ghost(1, f, t)
+        return y2 * ghost(0, f, t)
+
+    return beyond
+
+
+def step_kernel(sz, *refs):
+    state, inner, mirror_in, right_in, left_in, packet_in, wall, xw, yw, emission = refs[:10]
+    others = refs[10 : 10 + sz.vert - 2]
+    out, mirror, packet, right, left, spread, sums_ref = refs[10 + sz.vert - 2 :]
+    vert_index = lax.axis_index("vert")
+    parity = vert_index % 2
+    received(sz, parity, mirror_in, packet_in, others, spread)
     flux = spread[FIELDS - 1, block(real_row(parity, 0) * SUB), :]
-    column = sub()
-
-    def ghost(d, f, t):
-        return keep * mirror_in[sz.mirror_index(d, f, t)] + flux * emission[f * sz.tiles + t]
-
-    def advance(step, beyond):
+    beyond = wall_part(sz, mirror_in, wall, emission, flux, yw)
+
+    def advance(step, near_wall):
         y = real_row(parity, step)
-        ux, uy, inv_t, amount, px, py, half_theta, rate = [
-            spread[r, block(y * SUB), :] for r in range(FIELDS - 1)
-        ]
-        along_y = []
-        for kg in range(sz.kg):
-            cy = yw[4 * kg] - uy
-            cy_sq = cy * cy * inv_t
-            along_y.append((masked(inside(sz, kg), amount * jnp.exp(-cy_sq)), py * cy, cy_sq - 2.0))
+        ux, uy, inv_t, amount, px, py, half_theta, rate = field_rows(spread, y)
+        along_y = [part_y(sz, yw, kg, uy, inv_t, amount, py) for kg in range(sz.kg)]
         totals = None
         for xg in range(sz.xg):
             vx = xw[4 * xg]
-            cx = vx - ux
-            cx_sq = cx * cx * inv_t
-            ex = jnp.exp(-cx_sq)
-            pxs = px * cx
+            along_x = part_x(vx, ux, inv_t, px)
             sums = None
             for kg in range(sz.kg):
                 t = xg * sz.kg + kg
-                ey, pys, cys = along_y[kg]
-                maxwell = ex * ey
-                p = pxs + pys
-                sg = maxwell * (1.0 + p * (cx_sq + cys))
-                sh = half_theta * (sg + p * maxwell)
                 values = []
-                for f, source in ((0, sg), (1, sh)):
+                for f, source in enumerate(target(along_x, along_y[kg], half_theta)):
                     at = sz.base(f, t) + step * SUB
-                    side = sz.side_base(f, t) + 2 * step
-                    if t >= sz.half:
-                        edge = jnp.where(column < 2, right_in[pl.ds(side, SUB), :], 0.0)
-                    else:
-                        start = side - (SUB - 2)
-                        edge = jnp.where(column >= SUB - 2, left_in[pl.ds(start, SUB), :], 0.0)
+                    edge = side_edge(sz, right_in, left_in, f, t, step)
                     moved = (inner[block(at), :] + edge) + (source - rate * state[block(at), :])
-                    if beyond is not None:
-                        moved = moved + beyond(f, t, yw[4 * kg + 2], yw[4 * kg + 3])
+                    if near_wall:
+                        moved = moved + beyond(step, f, t)
                     out[block(at), :] = moved
                     values.append(moved)
-                if not last:
-                    sums = add_columns(yw[4 * kg], values[0], values[1], sums)
-            if not last:
-                totals = add_group(vx, sums, totals)
-        if not last:
-            put_sums(sums_ref, y, totals)
-
-    advance(0, lambda f, t, y1, y2: y1 * ghost(0, f, t) + y2 * ghost(1, f, t))
-    advance(1, lambda f, t, y1, y2: y2 * ghost(0, f, t))
+                sums = add_columns(yw[4 * kg], values[0], values[1], sums)
+            totals = add_group(vx, sums, totals)
+        put_sums(sums_ref, y, totals)
+
+    advance(0, True)
+    advance(1, True)
 
     def body(step, carry):
-        advance(step, None)
+        advance(step, False)
         return carry
 
     lax.fori_loop(2, Y, body, 0)
-    if not last:
-        send(sz, vert_index, out, sums_ref, mirror, packet, right, left)
-        return
-    for f in range(2):
+    send(sz, vert_index, out, sums_ref, mirror, packet, right, left)
+
+
+def last_kernel(sz, *refs):
+    state, inner, mirror_in, right_in, left_in, packet_in, wall, xw, yw, emission = refs[:10]
+    others = refs[10 : 10 + sz.vert - 2]
+    result, spread, along, turn_a, turn_b, final, sems = refs[10 + sz.vert - 2 :]
+    parity = lax.axis_index("vert") % 2
+    received(sz, parity, mirror_in, packet_in, others, spread)
+    flux = spread[FIELDS - 1, block(real_row(parity, 0) * SUB), :]
+    beyond = wall_part(sz, mirror_in, wall, emission, flux, yw)
+
+    def prepare(step, carry):
+        _, uy, inv_t, amount, _, py, _, _ = field_rows(spread, real_row(parity, step))
         for kg in range(sz.kg):
-            for xg in range(sz.xg):
+            for r, value in enumerate(part_y(sz, yw, kg, uy, inv_t, amount, py)):
+                along[3 * kg + r, block(step * SUB), :] = value
+        return carry
+
+    lax.fori_loop(0, Y, prepare, 0)
+    for xg in range(sz.xg):
+        turn = turn_b if xg % 2 else turn_a
+        vx = xw[4 * xg]
+        for step in range(Y):
+            y = real_row(parity, step)
+            rows = pl.ds(step * SUB, SUB)
+            ux, _, inv_t, _, px, _, half_theta, rate = field_rows(spread, y)
+            along_x = part_x(vx, ux, inv_t, px)
+            for kg in range(sz.kg):
                 t = xg * sz.kg + kg
-                slot = xg % 2
-                base = sz.base(f, t)
-                for step in range(Y):
-                    y = real_row(parity, step)
-                    turn[slot, block(y * SUB), :] = out[pl.ds(base + step * SUB, SUB), :]
+                along_y = [along[3 * kg + r, rows, :] for r in range(3)]
+                for f, source in enumerate(target(along_x, along_y, half_theta)):
+                    at = pl.ds(sz.base(f, t) + step * SUB, SUB)
+                    edge = side_edge(sz, right_in, left_in, f, t, step)
+                    moved = (inner[at, :] + edge) + (source - rate * state[at, :])
+                    if step < 2:
+                        moved = moved + beyond(step, f, t)
+                    turn[2 * kg + f, block(y * SUB), :] = moved
+        for f in range(2):
+            for kg in range(sz.kg):
                 parts = []
                 for x in range(SUB):
                     for part in range(0, Y, SUB):
-                        parts.append(turn[slot, pl.ds(part * SUB + x, SUB, stride=SUB), :])
+                        parts.append(turn[2 * kg + f, pl.ds(part * SUB + x, SUB, stride=SUB), :])
                 turned = jnp.concatenate(parts, axis=0).T
                 for k in range(kg * PART_K, min((kg + 1) * PART_K, sz.band)):
                     row = (k - kg * PART_K) * PART_X
                     final[f, k, xg * PART_X : (xg + 1) * PART_X, :] = turned[row : row + PART_X, :]
-            chunk_copy(sz, final, result, sems, f, kg).start()
-    for f in range(2):
-        for kg in range(sz.kg):
-            chunk_copy(sz, final, result, sems, f, kg).wait()
+            group_copy(sz, final, result, sems, f, xg).start()
+    for xg in range(sz.xg):
+        for f in range(2):
+            group_copy(sz, final, result, sems, f, xg).wait()
 
 
 def shapes(sz):
@@ -469,19 +513,19 @@
     final_shape = jax.ShapeDtypeStruct(distribution.shape, jnp.float32)
     bytes_moved = 2 * distribution.size * 4
     sums_scratch = pltpu.VMEM((FIELDS, sz.cells, LANES), jnp.float32)
-    turn_scratch = pltpu.VMEM((2, sz.cells, LANES), jnp.float32)
+    turn_scratch = [pltpu.VMEM((2 * sz.kg, sz.cells, LANES), jnp.float32)] * 2
     step_scratch = [pltpu.VMEM((FIELDS, sz.cells, LANES), jnp.float32)]
     first_vmem = ALL_VMEM - 26 * distribution.size
     stage = [
         pltpu.VMEM(distribution.shape, jnp.float32),
-        pltpu.SemaphoreType.DMA((2 * sz.kg,)),
+        pltpu.SemaphoreType.DMA((2 * sz.xg,)),
     ]
     state, mirror, packet, right, left = pl.pallas_call(
         functools.partial(first_kernel, sz),
         out_shape=shapes(sz),
         in_specs=[hbm],
         out_specs=(vmem,) * 5,
-        scratch_shapes=[sums_scratch, turn_scratch] + stage,
+        scratch_shapes=[sums_scratch] + turn_scratch + stage,
         cost_estimate=pl.CostEstimate(
             flops=10 * distribution.size, bytes_accessed=bytes_moved, transcendentals=0
         ),
@@ -521,11 +565,12 @@
             name="advect",
         )(state, tables[1], tables[2])
         if last:
-            scratch = step_scratch + [pltpu.VMEM((sz.state_rows, LANES), jnp.float32), turn_scratch] + stage
+            along = pltpu.VMEM((3 * sz.kg, sz.cells, LANES), jnp.float32)
+            scratch = step_scratch + [along] + turn_scratch + stage
         else:
             scratch = step_scratch + [sums_scratch]
         result = pl.pallas_call(
-            functools.partial(step_kernel, sz, last),
+            functools.partial(last_kernel if last else step_kernel, sz),
             out_shape=(final_shape,) if last else shapes(sz),
             in_specs=[vmem] * (10 + len(others)),
             out_specs=(hbm,) if last else (vmem,) * 5,

time: 60.4 us -> 61 us (level)
  no operation moved by 1% of the time
where the time goes in v3:
time: 61 us; the launch traced here: 60.8 us
  starting transfers between devices  29.6 us (49%)
  Pallas kernels  20.1 us (33%)
  waiting for transfers between devices  10.9 us (18%)
    ppermute x8, starting transfers between devices, on_device(): lax.ppermute(packet, 'vert', [(s, s ^ mask) for s in range(vert)])  13.7 us
    pallas_call x4, Pallas kernels, on_device(): pl.pallas_call(functools.partial(last_kernel if last else step_kernel, sz...  10.7 us
    ppermute x8, waiting for transfers between devices, on_device(): lax.ppermute(packet, 'vert', [(s, s ^ mask) for s in range(vert)])  10.3 us
    ppermute x4, starting transfers between devices, on_device(): left_in = lax.ppermute(left, 'gx', back)  9.82 us
    ppermute x4, starting transfers between devices, on_device(): mirror_in = lax.ppermute(mirror, 'vert', [(s, s ^ 1) for s in range(vert)])  5.23 us
    pallas_call x4, Pallas kernels, on_device(): pl.pallas_call(functools.partial(advect_kernel, sz), out_shape=jax.ShapeD...  4.73 us
    pallas_call x1, Pallas kernels, on_device(): pl.pallas_call(functools.partial(first_kernel, sz), out_shape=shapes(sz),...  4 us
  transfers between devices with their start and end apart: 20, of which 6 were waited for; matrix products, arithmetic and copies ran while one was open for 0% of the time, Pallas kernels for 9%

profile of v3, /device:TPU:0, one launch (start us, length us, event | category | flops | bytes accessed | tf_op | source)
XLA Modules:
  0.0 60.8 jit_solution(7160544001396440442)
XLA Ops:
  0.0 0.0 copy-start.3
  0.0 0.0 copy-start.2
  0.0 0.0 copy-start.1
  0.0 0.0 copy-start
  0.0 4.0 %first.1 = (f32[4608,128]{1,0:T(8,128)S(1)}, f32[74,8,128]{2,1,0:T(8,128)S(1)}, f32[16,128]{1,0:T(8,128)S(1)}, f32[592,128]{1,0:T(8,128)S(1)}, f32[592,128]{1,0:T(8,128)S(1)}) custom-call(f32[2,24,96,128]{3,2,1,0:T(8,128)} %argument.1), custom_call_target="tpu_custom_call" | custom-call | flops 5898240 | bytes 4718592 | tf_op jit(solution)/shard_map/first/pallas_call | solution.py:523
  4.0 3.1 %collective-permute-start = (f32[74,8,128]{2,1,0:T(8,128)S(1)}, f32[74,8,128]{2,1,0:T(8,128)S(1)}, u32[]{:S(2)}, u32[]{:S(2)}) collective-permute-start(f32[74,8,128]{2,1,0:T(8,128)S(1)} %get-tuple-element.32), channel_id=1, source_target_pairs={{0,1},{1,0},{2,3},{3,2},{4,5},{5,4},{6,7},{7,6},{8,9},{9,8},{10,11... | collective-permute-start | bytes 909320 | tf_op jit(solution)/shard_map/ppermute | solution.py:550
  7.1 0.0 collective-permute-start.1
  7.1 2.6 %collective-permute-start.2 = (f32[592,128]{1,0:T(8,128)S(1)}, f32[592,128]{1,0:T(8,128)S(1)}, u32[]{:S(2)}, u32[]{:S(2)}) collective-permute-start(f32[592,128]{1,0:T(8,128)S(1)} %get-tuple-element.34), channel_id=1, source_target_pairs={{4,0},{8,4},{12,8},{16,12},{20,16},{24,20},{28,24},{0,28},{5,1},{9... | collective-permute-start | bytes 909320 | tf_op jit(solution)/shard_map/ppermute | solution.py:552
  9.8 2.6 %collective-permute-start.4 = (f32[16,128]{1,0:T(8,128)S(1)}, f32[16,128]{1,0:T(8,128)S(1)}, u32[]{:S(2)}, u32[]{:S(2)}) collective-permute-start(f32[16,128]{1,0:T(8,128)S(1)} %get-tuple-element.35.refs_5_), channel_id=1, source_target_pairs={{0,2},{1,3},{2,0},{3,1},{4,6},{5,7},{6,4},{7,5},{8,10},{9,11},{10,... | collective-permute-start | bytes 24584 | tf_op jit(solution)/shard_map/ppermute | solution.py:555
  12.3 0.0 collective-permute-start.3
  12.3 0.0 copy-done.3
  12.4 0.0 copy-done.2
  12.4 0.0 copy-done.1
  12.4 0.0 copy-done
  12.4 0.7 %walls.1 = (f32[1,8,128]{2,1,0:T(8,128)S(1)}, f32[24,8,128]{2,1,0:T(8,128)S(1)}, f32[12,8,128]{2,1,0:T(8,128)S(1)}, f32[36,8,128]{2,1,0:T(8,128)S(1)}) custom-call(s32[2,8]{1,0:T(2,128)S(1)} %copy-done, s32[2,8]{1,0:T(2,128)S(1)} %copy-done.1, f32[2]{0:T(128)S(1)} %copy-done.2, s32[3]{0:T(128)S(1)} %copy-done.3), custom_call_target="tpu_custom_call" | custom-call | tf_op jit(solution)/shard_map/walls/pallas_call | solution.py:535
  13.1 1.3 %advect.4.refs_1_ = f32[4608,128]{1,0:T(8,128)S(1)} custom-call(f32[4608,128]{1,0:T(8,128)S(1)} %get-tuple-element.29.state.refs_0_, f32[24,8,128]{2,1,0:T(8,128)S(1)} %get-tuple-element.30.xw.refs_7_, f32[12,8,128]{2,1,0:T(8,128)S(1)} %get-tuple-element.31.yw.refs_8_), custom_call_target="tpu_custom_call" | custom-call | flops 7077888 | bytes 4718592 | tf_op jit(solution)/shard_map/advect/pallas_call | solution.py:556
  14.4 0.0 collective-permute-done.4.refs_11_
  14.4 3.4 %collective-permute-done.3.refs_10_ = f32[16,128]{1,0:T(8,128)S(1)} collective-permute-done((f32[16,128]{1,0:T(8,128)S(1)}, f32[16,128]{1,0:T(8,128)S(1)}, u32[]{:S(2)}, u32[]{:S(2)}) %collective-permute-start.3) | collective-permute-done | bytes 8224 | tf_op jit(solution)/shard_map/ppermute | solution.py:555
  17.8 0.0 collective-permute-done.refs_2_
  17.8 0.0 collective-permute-done.1.refs_3_
  17.8 0.0 collective-permute-done.2.refs_4_
  17.8 2.4 %step.3 = (f32[4608,128]{1,0:T(8,128)S(1)}, f32[74,8,128]{2,1,0:T(8,128)S(1)}, f32[16,128]{1,0:T(8,128)S(1)}, f32[592,128]{1,0:T(8,128)S(1)}, f32[592,128]{1,0:T(8,128)S(1)}) custom-call(f32[4608,128]{1,0:T(8,128)S(1)} %get-tuple-element.29.state.refs_0_, f32[4608,128]{1,0:T(8,128)S(1)} %advect.4.refs_1_, f32[74,8,128]{2,1,0:T(8,128)S(1)} %collective-permute-done.refs_2_, ...), custom_call_target="tpu_custom_call" | custom-call | flops 23592960 | bytes 4718592 | tf_op jit(solution)/shard_map/step/pallas_call | solution.py:572
  20.2 0.1 collective-permute-start.5
  20.3 0.1 collective-permute-start.6
  20.3 2.6 %collective-permute-start.7 = (f32[592,128]{1,0:T(8,128)S(1)}, f32[592,128]{1,0:T(8,128)S(1)}, u32[]{:S(2)}, u32[]{:S(2)}) collective-permute-start(f32[592,128]{1,0:T(8,128)S(1)} %get-tuple-element.41), channel_id=1, source_target_pairs={{4,0},{8,4},{12,8},{16,12},{20,16},{24,20},{28,24},{0,28},{5,1},{9... | collective-permute-start | bytes 909320 | tf_op jit(solution)/shard_map/ppermute | solution.py:552
  23.0 1.1 %collective-permute-start.9 = (f32[16,128]{1,0:T(8,128)S(1)}, f32[16,128]{1,0:T(8,128)S(1)}, u32[]{:S(2)}, u32[]{:S(2)}) collective-permute-start(f32[16,128]{1,0:T(8,128)S(1)} %get-tuple-element.42.refs_5_), channel_id=1, source_target_pairs={{0,2},{1,3},{2,0},{3,1},{4,6},{5,7},{6,4},{7,5},{8,10},{9,11},{10,... | collective-permute-start | bytes 24584 | tf_op jit(solution)/shard_map/ppermute | solution.py:555
  24.1 3.2 %collective-permute-start.8 = (f32[16,128]{1,0:T(8,128)S(1)}, f32[16,128]{1,0:T(8,128)S(1)}, u32[]{:S(2)}, u32[]{:S(2)}) collective-permute-start(f32[16,128]{1,0:T(8,128)S(1)} %get-tuple-element.42.refs_5_), channel_id=1, source_target_pairs={{0,3},{1,2},{2,1},{3,0},{4,7},{5,6},{6,5},{7,4},{8,11},{9,10},{10,... | collective-permute-start | bytes 24584 | tf_op jit(solution)/shard_map/ppermute | solution.py:555
  27.3 1.1 %advect.5.refs_1_ = f32[4608,128]{1,0:T(8,128)S(1)} custom-call(f32[4608,128]{1,0:T(8,128)S(1)} %get-tuple-element.38.state.refs_0_, f32[24,8,128]{2,1,0:T(8,128)S(1)} %get-tuple-element.30.xw.refs_7_, f32[12,8,128]{2,1,0:T(8,128)S(1)} %get-tuple-element.31.yw.refs_8_), custom_call_target="tpu_custom_call" | custom-call | flops 7077888 | bytes 4718592 | tf_op jit(solution)/shard_map/advect/pallas_call | solution.py:556
  28.4 0.0 collective-permute-done.9.refs_11_
  28.4 1.3 %collective-permute-done.8.refs_10_ = f32[16,128]{1,0:T(8,128)S(1)} collective-permute-done((f32[16,128]{1,0:T(8,128)S(1)}, f32[16,128]{1,0:T(8,128)S(1)}, u32[]{:S(2)}, u32[]{:S(2)}) %collective-permute-start.8) | collective-permute-done | bytes 8224 | tf_op jit(solution)/shard_map/ppermute | solution.py:555
  29.8 0.0 collective-permute-done.5.refs_2_
  29.8 0.0 collective-permute-done.6.refs_3_
  29.8 0.0 collective-permute-done.7.refs_4_
  29.8 2.4 %step.4 = (f32[4608,128]{1,0:T(8,128)S(1)}, f32[74,8,128]{2,1,0:T(8,128)S(1)}, f32[16,128]{1,0:T(8,128)S(1)}, f32[592,128]{1,0:T(8,128)S(1)}, f32[592,128]{1,0:T(8,128)S(1)}) custom-call(f32[4608,128]{1,0:T(8,128)S(1)} %get-tuple-element.38.state.refs_0_, f32[4608,128]{1,0:T(8,128)S(1)} %advect.5.refs_1_, f32[74,8,128]{2,1,0:T(8,128)S(1)} %collective-permute-done.5.refs_2_, ...), custom_call_target="tpu_custom_call" | custom-call | flops 23592960 | bytes 4718592 | tf_op jit(solution)/shard_map/step/pallas_call | solution.py:572
  32.1 2.0 %collective-permute-start.10 = (f32[74,8,128]{2,1,0:T(8,128)S(1)}, f32[74,8,128]{2,1,0:T(8,128)S(1)}, u32[]{:S(2)}, u32[]{:S(2)}) collective-permute-start(f32[74,8,128]{2,1,0:T(8,128)S(1)} %get-tuple-element.44), channel_id=1, source_target_pairs={{0,1},{1,0},{2,3},{3,2},{4,5},{5,4},{6,7},{7,6},{8,9},{9,8},{10,11... | collective-permute-start | bytes 909320 | tf_op jit(solution)/shard_map/ppermute | solution.py:550
  34.1 0.4 collective-permute-start.11
  34.5 2.2 %collective-permute-start.12 = (f32[592,128]{1,0:T(8,128)S(1)}, f32[592,128]{1,0:T(8,128)S(1)}, u32[]{:S(2)}, u32[]{:S(2)}) collective-permute-start(f32[592,128]{1,0:T(8,128)S(1)} %get-tuple-element.46), channel_id=1, source_target_pairs={{4,0},{8,4},{12,8},{16,12},{20,16},{24,20},{28,24},{0,28},{5,1},{9... | collective-permute-start | bytes 909320 | tf_op jit(solution)/shard_map/ppermute | solution.py:552
  36.8 1.6 %collective-permute-start.14 = (f32[16,128]{1,0:T(8,128)S(1)}, f32[16,128]{1,0:T(8,128)S(1)}, u32[]{:S(2)}, u32[]{:S(2)}) collective-permute-start(f32[16,128]{1,0:T(8,128)S(1)} %get-tuple-element.47.refs_5_), channel_id=1, source_target_pairs={{0,2},{1,3},{2,0},{3,1},{4,6},{5,7},{6,4},{7,5},{8,10},{9,11},{10,... | collective-permute-start | bytes 24584 | tf_op jit(solution)/shard_map/ppermute | solution.py:555
  38.4 0.9 %collective-permute-start.13 = (f32[16,128]{1,0:T(8,128)S(1)}, f32[16,128]{1,0:T(8,128)S(1)}, u32[]{:S(2)}, u32[]{:S(2)}) collective-permute-start(f32[16,128]{1,0:T(8,128)S(1)} %get-tuple-element.47.refs_5_), channel_id=1, source_target_pairs={{0,3},{1,2},{2,1},{3,0},{4,7},{5,6},{6,5},{7,4},{8,11},{9,10},{10,... | collective-permute-start | bytes 24584 | tf_op jit(solution)/shard_map/ppermute | solution.py:555
  39.2 1.1 %advect.6.refs_1_ = f32[4608,128]{1,0:T(8,128)S(1)} custom-call(f32[4608,128]{1,0:T(8,128)S(1)} %get-tuple-element.43.state.refs_0_, f32[24,8,128]{2,1,0:T(8,128)S(1)} %get-tuple-element.30.xw.refs_7_, f32[12,8,128]{2,1,0:T(8,128)S(1)} %get-tuple-element.31.yw.refs_8_), custom_call_target="tpu_custom_call" | custom-call | flops 7077888 | bytes 4718592 | tf_op jit(solution)/shard_map/advect/pallas_call | solution.py:556
  40.4 1.3 %collective-permute-done.14.refs_11_ = f32[16,128]{1,0:T(8,128)S(1)} collective-permute-done((f32[16,128]{1,0:T(8,128)S(1)}, f32[16,128]{1,0:T(8,128)S(1)}, u32[]{:S(2)}, u32[]{:S(2)}) %collective-permute-start.14) | collective-permute-done | bytes 8224 | tf_op jit(solution)/shard_map/ppermute | solution.py:555
  41.7 2.1 %collective-permute-done.13.refs_10_ = f32[16,128]{1,0:T(8,128)S(1)} collective-permute-done((f32[16,128]{1,0:T(8,128)S(1)}, f32[16,128]{1,0:T(8,128)S(1)}, u32[]{:S(2)}, u32[]{:S(2)}) %collective-permute-start.13) | collective-permute-done | bytes 8224 | tf_op jit(solution)/shard_map/ppermute | solution.py:555
  43.8 0.0 collective-permute-done.10.refs_2_
  43.8 0.6 %collective-permute-done.11.refs_3_ = f32[592,128]{1,0:T(8,128)S(1)} collective-permute-done((f32[592,128]{1,0:T(8,128)S(1)}, f32[592,128]{1,0:T(8,128)S(1)}, u32[]{:S(2)}, u32[]{:S(2)}) %collective-permute-start.11) | collective-permute-done | bytes 303136 | tf_op jit(solution)/shard_map/ppermute | solution.py:551
  44.4 0.0 collective-permute-done.12.refs_4_
  44.4 2.4 %step.5 = (f32[4608,128]{1,0:T(8,128)S(1)}, f32[74,8,128]{2,1,0:T(8,128)S(1)}, f32[16,128]{1,0:T(8,128)S(1)}, f32[592,128]{1,0:T(8,128)S(1)}, f32[592,128]{1,0:T(8,128)S(1)}) custom-call(f32[4608,128]{1,0:T(8,128)S(1)} %get-tuple-element.43.state.refs_0_, f32[4608,128]{1,0:T(8,128)S(1)} %advect.6.refs_1_, f32[74,8,128]{2,1,0:T(8,128)S(1)} %collective-permute-done.10.refs_2_, ...), custom_call_target="tpu_custom_call" | custom-call | flops 23592960 | bytes 4718592 | tf_op jit(solution)/shard_map/step/pallas_call | solution.py:572
  46.8 0.1 collective-permute-start.15
  46.9 0.4 collective-permute-start.16
  47.3 2.3 %collective-permute-start.17 = (f32[592,128]{1,0:T(8,128)S(1)}, f32[592,128]{1,0:T(8,128)S(1)}, u32[]{:S(2)}, u32[]{:S(2)}) collective-permute-start(f32[592,128]{1,0:T(8,128)S(1)} %get-tuple-element.51), channel_id=1, source_target_pairs={{4,0},{8,4},{12,8},{16,12},{20,16},{24,20},{28,24},{0,28},{5,1},{9... | collective-permute-start | bytes 909320 | tf_op jit(solution)/shard_map/ppermute | solution.py:552
  49.6 2.1 %collective-permute-start.19 = (f32[16,128]{1,0:T(8,128)S(1)}, f32[16,128]{1,0:T(8,128)S(1)}, u32[]{:S(2)}, u32[]{:S(2)}) collective-permute-start(f32[16,128]{1,0:T(8,128)S(1)} %get-tuple-element.52.refs_5_), channel_id=1, source_target_pairs={{0,2},{1,3},{2,0},{3,1},{4,6},{5,7},{6,4},{7,5},{8,10},{9,11},{10,... | collective-permute-start | bytes 24584 | tf_op jit(solution)/shard_map/ppermute | solution.py:555
  51.7 2.2 %collective-permute-start.18 = (f32[16,128]{1,0:T(8,128)S(1)}, f32[16,128]{1,0:T(8,128)S(1)}, u32[]{:S(2)}, u32[]{:S(2)}) collective-permute-start(f32[16,128]{1,0:T(8,128)S(1)} %get-tuple-element.52.refs_5_), channel_id=1, source_target_pairs={{0,3},{1,2},{2,1},{3,0},{4,7},{5,6},{6,5},{7,4},{8,11},{9,10},{10,... | collective-permute-start | bytes 24584 | tf_op jit(solution)/shard_map/ppermute | solution.py:555
  53.9 1.1 %advect.7.refs_1_ = f32[4608,128]{1,0:T(8,128)S(1)} custom-call(f32[4608,128]{1,0:T(8,128)S(1)} %get-tuple-element.48.state.refs_0_, f32[24,8,128]{2,1,0:T(8,128)S(1)} %get-tuple-element.30.xw.refs_7_, f32[12,8,128]{2,1,0:T(8,128)S(1)} %get-tuple-element.31.yw.refs_8_), custom_call_target="tpu_custom_call" | custom-call | flops 7077888 | bytes 4718592 | tf_op jit(solution)/shard_map/advect/pallas_call | solution.py:556
  55.1 0.0 collective-permute-done.19.refs_11_
  55.1 2.1 %collective-permute-done.18.refs_10_ = f32[16,128]{1,0:T(8,128)S(1)} collective-permute-done((f32[16,128]{1,0:T(8,128)S(1)}, f32[16,128]{1,0:T(8,128)S(1)}, u32[]{:S(2)}, u32[]{:S(2)}) %collective-permute-start.18) | collective-permute-done | bytes 8224 | tf_op jit(solution)/shard_map/ppermute | solution.py:555
  57.2 0.0 collective-permute-done.15.refs_2_
  57.2 0.0 collective-permute-done.16.refs_3_
  57.2 0.0 collective-permute-done.17.refs_4_
  57.2 3.6 %last.1 = f32[2,24,96,128]{3,2,1,0:T(8,128)} custom-call(f32[4608,128]{1,0:T(8,128)S(1)} %get-tuple-element.48.state.refs_0_, f32[4608,128]{1,0:T(8,128)S(1)} %advect.7.refs_1_, f32[74,8,128]{2,1,0:T(8,128)S(1)} %collective-permute-done.15.refs_2_, f32[592,128]{1,0:T(8,128)S(1)} %collective-permute-done.16.refs_3_, ...), custom_call_target="tpu_custom_call" | custom-call | flops 23592960 | bytes 4718592 | tf_op jit(solution)/shard_map/last/pallas_call | solution.py:572
Async XLA Ops:
  0.0 12.4 %copy-start.3 = (s32[3]{0:T(128)S(1)}, s32[3]{0:T(128)}, u32[]{:S(2)}) copy-start(s32[3]{0:T(128)} %acc_ref.1) | copy-start | bytes 40
  0.0 12.4 %copy-start.2 = (f32[2]{0:T(128)S(1)}, f32[2]{0:T(128)}, u32[]{:S(2)}) copy-start(f32[2]{0:T(128)} %temps_ref.1) | copy-start | bytes 28
  0.0 12.4 %copy-start.1 = (s32[2,8]{1,0:T(2,128)S(1)}, s32[2,8]{1,0:T(2,128)}, u32[]{:S(2)}) copy-start(s32[2,8]{1,0:T(2,128)} %index_ref.1) | copy-start | bytes 196
  0.0 12.4 %copy-start = (s32[2,8]{1,0:T(2,128)S(1)}, s32[2,8]{1,0:T(2,128)}, u32[]{:S(2)}) copy-start(s32[2,8]{1,0:T(2,128)} %type_ref.1) | copy-start | bytes 196
  4.0 13.8 %collective-permute-start = (f32[74,8,128]{2,1,0:T(8,128)S(1)}, f32[74,8,128]{2,1,0:T(8,128)S(1)}, u32[]{:S(2)}, u32[]{:S(2)}) collective-permute-start(f32[74,8,128]{2,1,0:T(8,128)S(1)} %get-tuple-element.32), channel_id=1, source_target_pairs={{0,1},{1,0},{2,3},{3,2},{4,5},{5,4},{6,7},{7,6},{8,9},{9,8},{10,11... | collective-permute-start | bytes 909320 | tf_op jit(solution)/shard_map/ppermute | solution.py:550
  7.1 10.7 %collective-permute-start.1 = (f32[592,128]{1,0:T(8,128)S(1)}, f32[592,128]{1,0:T(8,128)S(1)}, u32[]{:S(2)}, u32[]{:S(2)}) collective-permute-start(f32[592,128]{1,0:T(8,128)S(1)} %get-tuple-element.33), channel_id=1, source_target_pairs={{0,4},{4,8},{8,12},{12,16},{16,20},{20,24},{24,28},{28,0},{1,5},{5... | collective-permute-start | bytes 909320 | tf_op jit(solution)/shard_map/ppermute | solution.py:551
  7.1 10.7 %collective-permute-start.2 = (f32[592,128]{1,0:T(8,128)S(1)}, f32[592,128]{1,0:T(8,128)S(1)}, u32[]{:S(2)}, u32[]{:S(2)}) collective-permute-start(f32[592,128]{1,0:T(8,128)S(1)} %get-tuple-element.34), channel_id=1, source_target_pairs={{4,0},{8,4},{12,8},{16,12},{20,16},{24,20},{28,24},{0,28},{5,1},{9... | collective-permute-start | bytes 909320 | tf_op jit(solution)/shard_map/ppermute | solution.py:552
  9.8 4.7 %collective-permute-start.4 = (f32[16,128]{1,0:T(8,128)S(1)}, f32[16,128]{1,0:T(8,128)S(1)}, u32[]{:S(2)}, u32[]{:S(2)}) collective-permute-start(f32[16,128]{1,0:T(8,128)S(1)} %get-tuple-element.35.refs_5_), channel_id=1, source_target_pairs={{0,2},{1,3},{2,0},{3,1},{4,6},{5,7},{6,4},{7,5},{8,10},{9,11},{10,... | collective-permute-start | bytes 24584 | tf_op jit(solution)/shard_map/ppermute | solution.py:555
  12.3 5.4 %collective-permute-start.3 = (f32[16,128]{1,0:T(8,128)S(1)}, f32[16,128]{1,0:T(8,128)S(1)}, u32[]{:S(2)}, u32[]{:S(2)}) collective-permute-start(f32[16,128]{1,0:T(8,128)S(1)} %get-tuple-element.35.refs_5_), channel_id=1, source_target_pairs={{0,3},{1,2},{2,1},{3,0},{4,7},{5,6},{6,5},{7,4},{8,11},{9,10},{10,... | collective-permute-start | bytes 24584 | tf_op jit(solution)/shard_map/ppermute | solution.py:555
  20.2 9.6 %collective-permute-start.5 = (f32[74,8,128]{2,1,0:T(8,128)S(1)}, f32[74,8,128]{2,1,0:T(8,128)S(1)}, u32[]{:S(2)}, u32[]{:S(2)}) collective-permute-start(f32[74,8,128]{2,1,0:T(8,128)S(1)} %get-tuple-element.39), channel_id=1, source_target_pairs={{0,1},{1,0},{2,3},{3,2},{4,5},{5,4},{6,7},{7,6},{8,9},{9,8},{10,11... | collective-permute-start | bytes 909320 | tf_op jit(solution)/shard_map/ppermute | solution.py:550
  20.3 9.5 %collective-permute-start.6 = (f32[592,128]{1,0:T(8,128)S(1)}, f32[592,128]{1,0:T(8,128)S(1)}, u32[]{:S(2)}, u32[]{:S(2)}) collective-permute-start(f32[592,128]{1,0:T(8,128)S(1)} %get-tuple-element.40), channel_id=1, source_target_pairs={{0,4},{4,8},{8,12},{12,16},{16,20},{20,24},{24,28},{28,0},{1,5},{5... | collective-permute-start | bytes 909320 | tf_op jit(solution)/shard_map/ppermute | solution.py:551
  20.3 9.5 %collective-permute-start.7 = (f32[592,128]{1,0:T(8,128)S(1)}, f32[592,128]{1,0:T(8,128)S(1)}, u32[]{:S(2)}, u32[]{:S(2)}) collective-permute-start(f32[592,128]{1,0:T(8,128)S(1)} %get-tuple-element.41), channel_id=1, source_target_pairs={{4,0},{8,4},{12,8},{16,12},{20,16},{24,20},{28,24},{0,28},{5,1},{9... | collective-permute-start | bytes 909320 | tf_op jit(solution)/shard_map/ppermute | solution.py:552
  23.0 5.5 %collective-permute-start.9 = (f32[16,128]{1,0:T(8,128)S(1)}, f32[16,128]{1,0:T(8,128)S(1)}, u32[]{:S(2)}, u32[]{:S(2)}) collective-permute-start(f32[16,128]{1,0:T(8,128)S(1)} %get-tuple-element.42.refs_5_), channel_id=1, source_target_pairs={{0,2},{1,3},{2,0},{3,1},{4,6},{5,7},{6,4},{7,5},{8,10},{9,11},{10,... | collective-permute-start | bytes 24584 | tf_op jit(solution)/shard_map/ppermute | solution.py:555
  24.1 5.7 %collective-permute-start.8 = (f32[16,128]{1,0:T(8,128)S(1)}, f32[16,128]{1,0:T(8,128)S(1)}, u32[]{:S(2)}, u32[]{:S(2)}) collective-permute-start(f32[16,128]{1,0:T(8,128)S(1)} %get-tuple-element.42.refs_5_), channel_id=1, source_target_pairs={{0,3},{1,2},{2,1},{3,0},{4,7},{5,6},{6,5},{7,4},{8,11},{9,10},{10,... | collective-permute-start | bytes 24584 | tf_op jit(solution)/shard_map/ppermute | solution.py:555
  32.1 11.7 %collective-permute-start.10 = (f32[74,8,128]{2,1,0:T(8,128)S(1)}, f32[74,8,128]{2,1,0:T(8,128)S(1)}, u32[]{:S(2)}, u32[]{:S(2)}) collective-permute-start(f32[74,8,128]{2,1,0:T(8,128)S(1)} %get-tuple-element.44), channel_id=1, source_target_pairs={{0,1},{1,0},{2,3},{3,2},{4,5},{5,4},{6,7},{7,6},{8,9},{9,8},{10,11... | collective-permute-start | bytes 909320 | tf_op jit(solution)/shard_map/ppermute | solution.py:550
  34.1 10.3 %collective-permute-start.11 = (f32[592,128]{1,0:T(8,128)S(1)}, f32[592,128]{1,0:T(8,128)S(1)}, u32[]{:S(2)}, u32[]{:S(2)}) collective-permute-start(f32[592,128]{1,0:T(8,128)S(1)} %get-tuple-element.45), channel_id=1, source_target_pairs={{0,4},{4,8},{8,12},{12,16},{16,20},{20,24},{24,28},{28,0},{1,5},{5... | collective-permute-start | bytes 909320 | tf_op jit(solution)/shard_map/ppermute | solution.py:551
  34.5 9.9 %collective-permute-start.12 = (f32[592,128]{1,0:T(8,128)S(1)}, f32[592,128]{1,0:T(8,128)S(1)}, u32[]{:S(2)}, u32[]{:S(2)}) collective-permute-start(f32[592,128]{1,0:T(8,128)S(1)} %get-tuple-element.46), channel_id=1, source_target_pairs={{4,0},{8,4},{12,8},{16,12},{20,16},{24,20},{28,24},{0,28},{5,1},{9... | collective-permute-start | bytes 909320 | tf_op jit(solution)/shard_map/ppermute | solution.py:552
  36.8 4.9 %collective-permute-start.14 = (f32[16,128]{1,0:T(8,128)S(1)}, f32[16,128]{1,0:T(8,128)S(1)}, u32[]{:S(2)}, u32[]{:S(2)}) collective-permute-start(f32[16,128]{1,0:T(8,128)S(1)} %get-tuple-element.47.refs_5_), channel_id=1, source_target_pairs={{0,2},{1,3},{2,0},{3,1},{4,6},{5,7},{6,4},{7,5},{8,10},{9,11},{10,... | collective-permute-start | bytes 24584 | tf_op jit(solution)/shard_map/ppermute | solution.py:555
  38.4 5.4 %collective-permute-start.13 = (f32[16,128]{1,0:T(8,128)S(1)}, f32[16,128]{1,0:T(8,128)S(1)}, u32[]{:S(2)}, u32[]{:S(2)}) collective-permute-start(f32[16,128]{1,0:T(8,128)S(1)} %get-tuple-element.47.refs_5_), channel_id=1, source_target_pairs={{0,3},{1,2},{2,1},{3,0},{4,7},{5,6},{6,5},{7,4},{8,11},{9,10},{10,... | collective-permute-start | bytes 24584 | tf_op jit(solution)/shard_map/ppermute | solution.py:555
  46.8 10.4 %collective-permute-start.15 = (f32[74,8,128]{2,1,0:T(8,128)S(1)}, f32[74,8,128]{2,1,0:T(8,128)S(1)}, u32[]{:S(2)}, u32[]{:S(2)}) collective-permute-start(f32[74,8,128]{2,1,0:T(8,128)S(1)} %get-tuple-element.49), channel_id=1, source_target_pairs={{0,1},{1,0},{2,3},{3,2},{4,5},{5,4},{6,7},{7,6},{8,9},{9,8},{10,11... | collective-permute-start | bytes 909320 | tf_op jit(solution)/shard_map/ppermute | solution.py:550
  46.9 10.3 %collective-permute-start.16 = (f32[592,128]{1,0:T(8,128)S(1)}, f32[592,128]{1,0:T(8,128)S(1)}, u32[]{:S(2)}, u32[]{:S(2)}) collective-permute-start(f32[592,128]{1,0:T(8,128)S(1)} %get-tuple-element.50), channel_id=1, source_target_pairs={{0,4},{4,8},{8,12},{12,16},{16,20},{20,24},{24,28},{28,0},{1,5},{5... | collective-permute-start | bytes 909320 | tf_op jit(solution)/shard_map/ppermute | solution.py:551
  47.3 9.9 %collective-permute-start.17 = (f32[592,128]{1,0:T(8,128)S(1)}, f32[592,128]{1,0:T(8,128)S(1)}, u32[]{:S(2)}, u32[]{:S(2)}) collective-permute-start(f32[592,128]{1,0:T(8,128)S(1)} %get-tuple-element.51), channel_id=1, source_target_pairs={{4,0},{8,4},{12,8},{16,12},{20,16},{24,20},{28,24},{0,28},{5,1},{9... | collective-permute-start | bytes 909320 | tf_op jit(solution)/shard_map/ppermute | solution.py:552
  49.6 5.5 %collective-permute-start.19 = (f32[16,128]{1,0:T(8,128)S(1)}, f32[16,128]{1,0:T(8,128)S(1)}, u32[]{:S(2)}, u32[]{:S(2)}) collective-permute-start(f32[16,128]{1,0:T(8,128)S(1)} %get-tuple-element.52.refs_5_), channel_id=1, source_target_pairs={{0,2},{1,3},{2,0},{3,1},{4,6},{5,7},{6,4},{7,5},{8,10},{9,11},{10,... | collective-permute-start | bytes 24584 | tf_op jit(solution)/shard_map/ppermute | solution.py:555
  51.7 5.4 %collective-permute-start.18 = (f32[16,128]{1,0:T(8,128)S(1)}, f32[16,128]{1,0:T(8,128)S(1)}, u32[]{:S(2)}, u32[]{:S(2)}) collective-permute-start(f32[16,128]{1,0:T(8,128)S(1)} %get-tuple-element.52.refs_5_), channel_id=1, source_target_pairs={{0,3},{1,2},{2,1},{3,0},{4,7},{5,6},{6,5},{7,4},{8,11},{9,10},{10,... | collective-permute-start | bytes 24584 | tf_op jit(solution)/shard_map/ppermute | solution.py:555

commit v4 on v3

--- a/solution.py
+++ b/solution.py
@@ -221,6 +221,13 @@
     )
 
 
+def chunk_copy(sz, source, target, sems, f, kg):
+    rows = pl.ds(kg * PART_K, min(PART_K, sz.band - kg * PART_K))
+    return pltpu.make_async_copy(
+        source.at[f, rows], target.at[f, rows], sems.at[f * sz.kg + kg]
+    )
+
+
 def first_kernel(sz, argument, state, mirror, packet, right, left, sums_ref, turn_a, turn_b, given, sems):
     vert_index = lax.axis_index("vert")
     parity = vert_index % 2
@@ -229,8 +236,10 @@
             group_copy(sz, argument, given, sems, f, xg).start()
     for xg in range(sz.xg):
         turn = turn_b if xg % 2 else turn_a
-        for f in range(2):
-            group_copy(sz, argument, given, sems, f, xg).wait()
+        if xg % (sz.xg // 2) == 0:
+            for other in range(xg, xg + sz.xg // 2):
+                for f in range(2):
+                    group_copy(sz, argument, given, sems, f, other).wait()
         for kg in range(sz.kg):
             for f in range(2):
                 parts = []
@@ -449,45 +458,48 @@
     beyond = wall_part(sz, mirror_in, wall, emission, flux, yw)
 
     def prepare(step, carry):
-        _, uy, inv_t, amount, _, py, _, _ = field_rows(spread, real_row(parity, step))
+        rows = block(step * SUB)
+        ux, uy, inv_t, amount, px, py, _, _ = field_rows(spread, real_row(parity, step))
         for kg in range(sz.kg):
             for r, value in enumerate(part_y(sz, yw, kg, uy, inv_t, amount, py)):
-                along[3 * kg + r, block(step * SUB), :] = value
+                along[3 * kg + r, rows, :] = value
+        for xg in range(sz.xg):
+            for r, value in enumerate(part_x(xw[4 * xg], ux, inv_t, px)):
+                along[3 * (sz.kg + xg) + r, rows, :] = value
         return carry
 
     lax.fori_loop(0, Y, prepare, 0)
-    for xg in range(sz.xg):
-        turn = turn_b if xg % 2 else turn_a
-        vx = xw[4 * xg]
-        for step in range(Y):
-            y = real_row(parity, step)
-            rows = pl.ds(step * SUB, SUB)
-            ux, _, inv_t, _, px, _, half_theta, rate = field_rows(spread, y)
-            along_x = part_x(vx, ux, inv_t, px)
-            for kg in range(sz.kg):
-                t = xg * sz.kg + kg
+    for kg in range(sz.kg):
+        for xg in range(sz.xg):
+            turn = turn_b if xg % 2 else turn_a
+            t = xg * sz.kg + kg
+            for step in range(Y):
+                y = real_row(parity, step)
+                rows = pl.ds(step * SUB, SUB)
+                half_theta, rate = [spread[r, block(y * SUB), :] for r in (6, 7)]
                 along_y = [along[3 * kg + r, rows, :] for r in range(3)]
+                along_x = [along[3 * (sz.kg + xg) + r, rows, :] for r in range(3)]
                 for f, source in enumerate(target(along_x, along_y, half_theta)):
                     at = pl.ds(sz.base(f, t) + step * SUB, SUB)
                     edge = side_edge(sz, right_in, left_in, f, t, step)
                     moved = (inner[at, :] + edge) + (source - rate * state[at, :])
                     if step < 2:
                         moved = moved + beyond(step, f, t)
-                    turn[2 * kg + f, block(y * SUB), :] = moved
-        for f in range(2):
-            for kg in range(sz.kg):
+                    turn[f, block(y * SUB), :] = moved
+            for f in range(2):
                 parts = []
                 for x in range(SUB):
                     for part in range(0, Y, SUB):
-                        parts.append(turn[2 * kg + f, pl.ds(part * SUB + x, SUB, stride=SUB), :])
+                        parts.append(turn[f, pl.ds(part * SUB + x, SUB, stride=SUB), :])
                 turned = jnp.concatenate(parts, axis=0).T
                 for k in range(kg * PART_K, min((kg + 1) * PART_K, sz.band)):
                     row = (k - kg * PART_K) * PART_X
                     final[f, k, xg * PART_X : (xg + 1) * PART_X, :] = turned[row : row + PART_X, :]
-            group_copy(sz, final, result, sems, f, xg).start()
-    for xg in range(sz.xg):
         for f in range(2):
-            group_copy(sz, final, result, sems, f, xg).wait()
+            chunk_copy(sz, final, result, sems, f, kg).start()
+    for kg in range(sz.kg):
+        for f in range(2):
+            chunk_copy(sz, final, result, sems, f, kg).wait()
 
 
 def shapes(sz):
@@ -518,7 +530,7 @@
     first_vmem = ALL_VMEM - 26 * distribution.size
     stage = [
         pltpu.VMEM(distribution.shape, jnp.float32),
-        pltpu.SemaphoreType.DMA((2 * sz.xg,)),
+        pltpu.SemaphoreType.DMA((2 * max(sz.xg, sz.kg),)),
     ]
     state, mirror, packet, right, left = pl.pallas_call(
         functools.partial(first_kernel, sz),
@@ -565,7 +577,7 @@
             name="advect",
         )(state, tables[1], tables[2])
         if last:
-            along = pltpu.VMEM((3 * sz.kg, sz.cells, LANES), jnp.float32)
+            along = pltpu.VMEM((3 * (sz.kg + sz.xg), sz.cells, LANES), jnp.float32)
             scratch = step_scratch + [along] + turn_scratch + stage
         else:
             scratch = step_scratch + [sums_scratch]

time: 61 us -> 61 us (level)
  no operation moved by 1% of the time
where the time goes in v4:
time: 61 us; the launch traced here: 60.8 us
  starting transfers between devices  29.6 us (49%)
  Pallas kernels  20.1 us (33%)
  waiting for transfers between devices  10.9 us (18%)
    ppermute x8, starting transfers between devices, on_device(): lax.ppermute(packet, 'vert', [(s, s ^ mask) for s in range(vert)])  13.7 us
    pallas_call x4, Pallas kernels, on_device(): pl.pallas_call(functools.partial(last_kernel if last else step_kernel, sz...  10.8 us
    ppermute x8, waiting for transfers between devices, on_device(): lax.ppermute(packet, 'vert', [(s, s ^ mask) for s in range(vert)])  10.3 us
    ppermute x4, starting transfers between devices, on_device(): left_in = lax.ppermute(left, 'gx', back)  9.85 us
    ppermute x4, starting transfers between devices, on_device(): mirror_in = lax.ppermute(mirror, 'vert', [(s, s ^ 1) for s in range(vert)])  5.23 us
    pallas_call x4, Pallas kernels, on_device(): pl.pallas_call(functools.partial(advect_kernel, sz), out_shape=jax.ShapeD...  4.73 us
    pallas_call x1, Pallas kernels, on_device(): pl.pallas_call(functools.partial(first_kernel, sz), out_shape=shapes(sz),...  3.89 us
  transfers between devices with their start and end apart: 20, of which 6 were waited for; matrix products, arithmetic and copies ran while one was open for 0% of the time, Pallas kernels for 9%

profile of v4, /device:TPU:0, one launch (start us, length us, event | category | flops | bytes accessed | tf_op | source)
XLA Modules:
  0.0 60.8 jit_solution(5902463619831462383)
XLA Ops:
  0.0 0.0 copy-start.3
  0.0 0.0 copy-start.2
  0.0 0.0 copy-start.1
  0.0 0.0 copy-start
  0.0 3.9 %first.1 = (f32[4608,128]{1,0:T(8,128)S(1)}, f32[74,8,128]{2,1,0:T(8,128)S(1)}, f32[16,128]{1,0:T(8,128)S(1)}, f32[592,128]{1,0:T(8,128)S(1)}, f32[592,128]{1,0:T(8,128)S(1)}) custom-call(f32[2,24,96,128]{3,2,1,0:T(8,128)} %argument.1), custom_call_target="tpu_custom_call" | custom-call | flops 5898240 | bytes 4718592 | tf_op jit(solution)/shard_map/first/pallas_call | solution.py:535
  3.9 3.1 %collective-permute-start = (f32[74,8,128]{2,1,0:T(8,128)S(1)}, f32[74,8,128]{2,1,0:T(8,128)S(1)}, u32[]{:S(2)}, u32[]{:S(2)}) collective-permute-start(f32[74,8,128]{2,1,0:T(8,128)S(1)} %get-tuple-element.32), channel_id=1, source_target_pairs={{0,1},{1,0},{2,3},{3,2},{4,5},{5,4},{6,7},{7,6},{8,9},{9,8},{10,11... | collective-permute-start | bytes 909320 | tf_op jit(solution)/shard_map/ppermute | solution.py:562
  7.0 0.0 collective-permute-start.1
  7.0 2.6 %collective-permute-start.2 = (f32[592,128]{1,0:T(8,128)S(1)}, f32[592,128]{1,0:T(8,128)S(1)}, u32[]{:S(2)}, u32[]{:S(2)}) collective-permute-start(f32[592,128]{1,0:T(8,128)S(1)} %get-tuple-element.34), channel_id=1, source_target_pairs={{4,0},{8,4},{12,8},{16,12},{20,16},{24,20},{28,24},{0,28},{5,1},{9... | collective-permute-start | bytes 909320 | tf_op jit(solution)/shard_map/ppermute | solution.py:564
  9.7 2.6 %collective-permute-start.4 = (f32[16,128]{1,0:T(8,128)S(1)}, f32[16,128]{1,0:T(8,128)S(1)}, u32[]{:S(2)}, u32[]{:S(2)}) collective-permute-start(f32[16,128]{1,0:T(8,128)S(1)} %get-tuple-element.35.refs_5_), channel_id=1, source_target_pairs={{0,2},{1,3},{2,0},{3,1},{4,6},{5,7},{6,4},{7,5},{8,10},{9,11},{10,... | collective-permute-start | bytes 24584 | tf_op jit(solution)/shard_map/ppermute | solution.py:567
  12.3 0.0 collective-permute-start.3
  12.3 0.0 copy-done.3
  12.3 0.0 copy-done.2
  12.3 0.0 copy-done.1
  12.3 0.0 copy-done
  12.3 0.7 %walls.1 = (f32[1,8,128]{2,1,0:T(8,128)S(1)}, f32[24,8,128]{2,1,0:T(8,128)S(1)}, f32[12,8,128]{2,1,0:T(8,128)S(1)}, f32[36,8,128]{2,1,0:T(8,128)S(1)}) custom-call(s32[2,8]{1,0:T(2,128)S(1)} %copy-done, s32[2,8]{1,0:T(2,128)S(1)} %copy-done.1, f32[2]{0:T(128)S(1)} %copy-done.2, s32[3]{0:T(128)S(1)} %copy-done.3), custom_call_target="tpu_custom_call" | custom-call | tf_op jit(solution)/shard_map/walls/pallas_call | solution.py:547
  13.0 1.3 %advect.4.refs_1_ = f32[4608,128]{1,0:T(8,128)S(1)} custom-call(f32[4608,128]{1,0:T(8,128)S(1)} %get-tuple-element.29.state.refs_0_, f32[24,8,128]{2,1,0:T(8,128)S(1)} %get-tuple-element.30.xw.refs_7_, f32[12,8,128]{2,1,0:T(8,128)S(1)} %get-tuple-element.31.yw.refs_8_), custom_call_target="tpu_custom_call" | custom-call | flops 7077888 | bytes 4718592 | tf_op jit(solution)/shard_map/advect/pallas_call | solution.py:568
  14.3 0.0 collective-permute-done.4.refs_11_
  14.3 3.4 %collective-permute-done.3.refs_10_ = f32[16,128]{1,0:T(8,128)S(1)} collective-permute-done((f32[16,128]{1,0:T(8,128)S(1)}, f32[16,128]{1,0:T(8,128)S(1)}, u32[]{:S(2)}, u32[]{:S(2)}) %collective-permute-start.3) | collective-permute-done | bytes 8224 | tf_op jit(solution)/shard_map/ppermute | solution.py:567
  17.7 0.0 collective-permute-done.refs_2_
  17.7 0.0 collective-permute-done.1.refs_3_
  17.7 0.0 collective-permute-done.2.refs_4_
  17.7 2.4 %step.3 = (f32[4608,128]{1,0:T(8,128)S(1)}, f32[74,8,128]{2,1,0:T(8,128)S(1)}, f32[16,128]{1,0:T(8,128)S(1)}, f32[592,128]{1,0:T(8,128)S(1)}, f32[592,128]{1,0:T(8,128)S(1)}) custom-call(f32[4608,128]{1,0:T(8,128)S(1)} %get-tuple-element.29.state.refs_0_, f32[4608,128]{1,0:T(8,128)S(1)} %advect.4.refs_1_, f32[74,8,128]{2,1,0:T(8,128)S(1)} %collective-permute-done.refs_2_, ...), custom_call_target="tpu_custom_call" | custom-call | flops 23592960 | bytes 4718592 | tf_op jit(solution)/shard_map/step/pallas_call | solution.py:584
  20.1 0.1 collective-permute-start.5
  20.2 0.1 collective-permute-start.6
  20.2 2.6 %collective-permute-start.7 = (f32[592,128]{1,0:T(8,128)S(1)}, f32[592,128]{1,0:T(8,128)S(1)}, u32[]{:S(2)}, u32[]{:S(2)}) collective-permute-start(f32[592,128]{1,0:T(8,128)S(1)} %get-tuple-element.41), channel_id=1, source_target_pairs={{4,0},{8,4},{12,8},{16,12},{20,16},{24,20},{28,24},{0,28},{5,1},{9... | collective-permute-start | bytes 909320 | tf_op jit(solution)/shard_map/ppermute | solution.py:564
  22.9 1.1 %collective-permute-start.9 = (f32[16,128]{1,0:T(8,128)S(1)}, f32[16,128]{1,0:T(8,128)S(1)}, u32[]{:S(2)}, u32[]{:S(2)}) collective-permute-start(f32[16,128]{1,0:T(8,128)S(1)} %get-tuple-element.42.refs_5_), channel_id=1, source_target_pairs={{0,2},{1,3},{2,0},{3,1},{4,6},{5,7},{6,4},{7,5},{8,10},{9,11},{10,... | collective-permute-start | bytes 24584 | tf_op jit(solution)/shard_map/ppermute | solution.py:567
  24.0 3.2 %collective-permute-start.8 = (f32[16,128]{1,0:T(8,128)S(1)}, f32[16,128]{1,0:T(8,128)S(1)}, u32[]{:S(2)}, u32[]{:S(2)}) collective-permute-start(f32[16,128]{1,0:T(8,128)S(1)} %get-tuple-element.42.refs_5_), channel_id=1, source_target_pairs={{0,3},{1,2},{2,1},{3,0},{4,7},{5,6},{6,5},{7,4},{8,11},{9,10},{10,... | collective-permute-start | bytes 24584 | tf_op jit(solution)/shard_map/ppermute | solution.py:567
  27.2 1.1 %advect.5.refs_1_ = f32[4608,128]{1,0:T(8,128)S(1)} custom-call(f32[4608,128]{1,0:T(8,128)S(1)} %get-tuple-element.38.state.refs_0_, f32[24,8,128]{2,1,0:T(8,128)S(1)} %get-tuple-element.30.xw.refs_7_, f32[12,8,128]{2,1,0:T(8,128)S(1)} %get-tuple-element.31.yw.refs_8_), custom_call_target="tpu_custom_call" | custom-call | flops 7077888 | bytes 4718592 | tf_op jit(solution)/shard_map/advect/pallas_call | solution.py:568
  28.3 0.0 collective-permute-done.9.refs_11_
  28.4 1.3 %collective-permute-done.8.refs_10_ = f32[16,128]{1,0:T(8,128)S(1)} collective-permute-done((f32[16,128]{1,0:T(8,128)S(1)}, f32[16,128]{1,0:T(8,128)S(1)}, u32[]{:S(2)}, u32[]{:S(2)}) %collective-permute-start.8) | collective-permute-done | bytes 8224 | tf_op jit(solution)/shard_map/ppermute | solution.py:567
  29.7 0.0 collective-permute-done.5.refs_2_
  29.7 0.0 collective-permute-done.6.refs_3_
  29.7 0.0 collective-permute-done.7.refs_4_
  29.7 2.4 %step.4 = (f32[4608,128]{1,0:T(8,128)S(1)}, f32[74,8,128]{2,1,0:T(8,128)S(1)}, f32[16,128]{1,0:T(8,128)S(1)}, f32[592,128]{1,0:T(8,128)S(1)}, f32[592,128]{1,0:T(8,128)S(1)}) custom-call(f32[4608,128]{1,0:T(8,128)S(1)} %get-tuple-element.38.state.refs_0_, f32[4608,128]{1,0:T(8,128)S(1)} %advect.5.refs_1_, f32[74,8,128]{2,1,0:T(8,128)S(1)} %collective-permute-done.5.refs_2_, ...), custom_call_target="tpu_custom_call" | custom-call | flops 23592960 | bytes 4718592 | tf_op jit(solution)/shard_map/step/pallas_call | solution.py:584
  32.1 2.0 %collective-permute-start.10 = (f32[74,8,128]{2,1,0:T(8,128)S(1)}, f32[74,8,128]{2,1,0:T(8,128)S(1)}, u32[]{:S(2)}, u32[]{:S(2)}) collective-permute-start(f32[74,8,128]{2,1,0:T(8,128)S(1)} %get-tuple-element.44), channel_id=1, source_target_pairs={{0,1},{1,0},{2,3},{3,2},{4,5},{5,4},{6,7},{7,6},{8,9},{9,8},{10,11... | collective-permute-start | bytes 909320 | tf_op jit(solution)/shard_map/ppermute | solution.py:562
  34.0 0.4 collective-permute-start.11
  34.5 2.2 %collective-permute-start.12 = (f32[592,128]{1,0:T(8,128)S(1)}, f32[592,128]{1,0:T(8,128)S(1)}, u32[]{:S(2)}, u32[]{:S(2)}) collective-permute-start(f32[592,128]{1,0:T(8,128)S(1)} %get-tuple-element.46), channel_id=1, source_target_pairs={{4,0},{8,4},{12,8},{16,12},{20,16},{24,20},{28,24},{0,28},{5,1},{9... | collective-permute-start | bytes 909320 | tf_op jit(solution)/shard_map/ppermute | solution.py:564
  36.7 1.6 %collective-permute-start.14 = (f32[16,128]{1,0:T(8,128)S(1)}, f32[16,128]{1,0:T(8,128)S(1)}, u32[]{:S(2)}, u32[]{:S(2)}) collective-permute-start(f32[16,128]{1,0:T(8,128)S(1)} %get-tuple-element.47.refs_5_), channel_id=1, source_target_pairs={{0,2},{1,3},{2,0},{3,1},{4,6},{5,7},{6,4},{7,5},{8,10},{9,11},{10,... | collective-permute-start | bytes 24584 | tf_op jit(solution)/shard_map/ppermute | solution.py:567
  38.3 0.9 %collective-permute-start.13 = (f32[16,128]{1,0:T(8,128)S(1)}, f32[16,128]{1,0:T(8,128)S(1)}, u32[]{:S(2)}, u32[]{:S(2)}) collective-permute-start(f32[16,128]{1,0:T(8,128)S(1)} %get-tuple-element.47.refs_5_), channel_id=1, source_target_pairs={{0,3},{1,2},{2,1},{3,0},{4,7},{5,6},{6,5},{7,4},{8,11},{9,10},{10,... | collective-permute-start | bytes 24584 | tf_op jit(solution)/shard_map/ppermute | solution.py:567
  39.2 1.1 %advect.6.refs_1_ = f32[4608,128]{1,0:T(8,128)S(1)} custom-call(f32[4608,128]{1,0:T(8,128)S(1)} %get-tuple-element.43.state.refs_0_, f32[24,8,128]{2,1,0:T(8,128)S(1)} %get-tuple-element.30.xw.refs_7_, f32[12,8,128]{2,1,0:T(8,128)S(1)} %get-tuple-element.31.yw.refs_8_), custom_call_target="tpu_custom_call" | custom-call | flops 7077888 | bytes 4718592 | tf_op jit(solution)/shard_map/advect/pallas_call | solution.py:568
  40.3 1.3 %collective-permute-done.14.refs_11_ = f32[16,128]{1,0:T(8,128)S(1)} collective-permute-done((f32[16,128]{1,0:T(8,128)S(1)}, f32[16,128]{1,0:T(8,128)S(1)}, u32[]{:S(2)}, u32[]{:S(2)}) %collective-permute-start.14) | collective-permute-done | bytes 8224 | tf_op jit(solution)/shard_map/ppermute | solution.py:567
  41.6 2.1 %collective-permute-done.13.refs_10_ = f32[16,128]{1,0:T(8,128)S(1)} collective-permute-done((f32[16,128]{1,0:T(8,128)S(1)}, f32[16,128]{1,0:T(8,128)S(1)}, u32[]{:S(2)}, u32[]{:S(2)}) %collective-permute-start.13) | collective-permute-done | bytes 8224 | tf_op jit(solution)/shard_map/ppermute | solution.py:567
  43.7 0.0 collective-permute-done.10.refs_2_
  43.7 0.6 %collective-permute-done.11.refs_3_ = f32[592,128]{1,0:T(8,128)S(1)} collective-permute-done((f32[592,128]{1,0:T(8,128)S(1)}, f32[592,128]{1,0:T(8,128)S(1)}, u32[]{:S(2)}, u32[]{:S(2)}) %collective-permute-start.11) | collective-permute-done | bytes 303136 | tf_op jit(solution)/shard_map/ppermute | solution.py:563
  44.4 0.0 collective-permute-done.12.refs_4_
  44.4 2.4 %step.5 = (f32[4608,128]{1,0:T(8,128)S(1)}, f32[74,8,128]{2,1,0:T(8,128)S(1)}, f32[16,128]{1,0:T(8,128)S(1)}, f32[592,128]{1,0:T(8,128)S(1)}, f32[592,128]{1,0:T(8,128)S(1)}) custom-call(f32[4608,128]{1,0:T(8,128)S(1)} %get-tuple-element.43.state.refs_0_, f32[4608,128]{1,0:T(8,128)S(1)} %advect.6.refs_1_, f32[74,8,128]{2,1,0:T(8,128)S(1)} %collective-permute-done.10.refs_2_, ...), custom_call_target="tpu_custom_call" | custom-call | flops 23592960 | bytes 4718592 | tf_op jit(solution)/shard_map/step/pallas_call | solution.py:584
  46.7 0.1 collective-permute-start.15
  46.8 0.4 collective-permute-start.16
  47.2 2.3 %collective-permute-start.17 = (f32[592,128]{1,0:T(8,128)S(1)}, f32[592,128]{1,0:T(8,128)S(1)}, u32[]{:S(2)}, u32[]{:S(2)}) collective-permute-start(f32[592,128]{1,0:T(8,128)S(1)} %get-tuple-element.51), channel_id=1, source_target_pairs={{4,0},{8,4},{12,8},{16,12},{20,16},{24,20},{28,24},{0,28},{5,1},{9... | collective-permute-start | bytes 909320 | tf_op jit(solution)/shard_map/ppermute | solution.py:564
  49.5 2.1 %collective-permute-start.19 = (f32[16,128]{1,0:T(8,128)S(1)}, f32[16,128]{1,0:T(8,128)S(1)}, u32[]{:S(2)}, u32[]{:S(2)}) collective-permute-start(f32[16,128]{1,0:T(8,128)S(1)} %get-tuple-element.52.refs_5_), channel_id=1, source_target_pairs={{0,2},{1,3},{2,0},{3,1},{4,6},{5,7},{6,4},{7,5},{8,10},{9,11},{10,... | collective-permute-start | bytes 24584 | tf_op jit(solution)/shard_map/ppermute | solution.py:567
  51.6 2.2 %collective-permute-start.18 = (f32[16,128]{1,0:T(8,128)S(1)}, f32[16,128]{1,0:T(8,128)S(1)}, u32[]{:S(2)}, u32[]{:S(2)}) collective-permute-start(f32[16,128]{1,0:T(8,128)S(1)} %get-tuple-element.52.refs_5_), channel_id=1, source_target_pairs={{0,3},{1,2},{2,1},{3,0},{4,7},{5,6},{6,5},{7,4},{8,11},{9,10},{10,... | collective-permute-start | bytes 24584 | tf_op jit(solution)/shard_map/ppermute | solution.py:567
  53.8 1.1 %advect.7.refs_1_ = f32[4608,128]{1,0:T(8,128)S(1)} custom-call(f32[4608,128]{1,0:T(8,128)S(1)} %get-tuple-element.48.state.refs_0_, f32[24,8,128]{2,1,0:T(8,128)S(1)} %get-tuple-element.30.xw.refs_7_, f32[12,8,128]{2,1,0:T(8,128)S(1)} %get-tuple-element.31.yw.refs_8_), custom_call_target="tpu_custom_call" | custom-call | flops 7077888 | bytes 4718592 | tf_op jit(solution)/shard_map/advect/pallas_call | solution.py:568
  55.0 0.0 collective-permute-done.19.refs_11_
  55.0 2.1 %collective-permute-done.18.refs_10_ = f32[16,128]{1,0:T(8,128)S(1)} collective-permute-done((f32[16,128]{1,0:T(8,128)S(1)}, f32[16,128]{1,0:T(8,128)S(1)}, u32[]{:S(2)}, u32[]{:S(2)}) %collective-permute-start.18) | collective-permute-done | bytes 8224 | tf_op jit(solution)/shard_map/ppermute | solution.py:567
  57.1 0.0 collective-permute-done.15.refs_2_
  57.1 0.0 collective-permute-done.16.refs_3_
  57.1 0.0 collective-permute-done.17.refs_4_
  57.1 3.8 %last.1 = f32[2,24,96,128]{3,2,1,0:T(8,128)} custom-call(f32[4608,128]{1,0:T(8,128)S(1)} %get-tuple-element.48.state.refs_0_, f32[4608,128]{1,0:T(8,128)S(1)} %advect.7.refs_1_, f32[74,8,128]{2,1,0:T(8,128)S(1)} %collective-permute-done.15.refs_2_, f32[592,128]{1,0:T(8,128)S(1)} %collective-permute-done.16.refs_3_, ...), custom_call_target="tpu_custom_call" | custom-call | flops 23592960 | bytes 4718592 | tf_op jit(solution)/shard_map/last/pallas_call | solution.py:584
Async XLA Ops:
  0.0 12.3 %copy-start.3 = (s32[3]{0:T(128)S(1)}, s32[3]{0:T(128)}, u32[]{:S(2)}) copy-start(s32[3]{0:T(128)} %acc_ref.1) | copy-start | bytes 40
  0.0 12.3 %copy-start.2 = (f32[2]{0:T(128)S(1)}, f32[2]{0:T(128)}, u32[]{:S(2)}) copy-start(f32[2]{0:T(128)} %temps_ref.1) | copy-start | bytes 28
  0.0 12.3 %copy-start.1 = (s32[2,8]{1,0:T(2,128)S(1)}, s32[2,8]{1,0:T(2,128)}, u32[]{:S(2)}) copy-start(s32[2,8]{1,0:T(2,128)} %index_ref.1) | copy-start | bytes 196
  0.0 12.3 %copy-start = (s32[2,8]{1,0:T(2,128)S(1)}, s32[2,8]{1,0:T(2,128)}, u32[]{:S(2)}) copy-start(s32[2,8]{1,0:T(2,128)} %type_ref.1) | copy-start | bytes 196
  3.9 13.8 %collective-permute-start = (f32[74,8,128]{2,1,0:T(8,128)S(1)}, f32[74,8,128]{2,1,0:T(8,128)S(1)}, u32[]{:S(2)}, u32[]{:S(2)}) collective-permute-start(f32[74,8,128]{2,1,0:T(8,128)S(1)} %get-tuple-element.32), channel_id=1, source_target_pairs={{0,1},{1,0},{2,3},{3,2},{4,5},{5,4},{6,7},{7,6},{8,9},{9,8},{10,11... | collective-permute-start | bytes 909320 | tf_op jit(solution)/shard_map/ppermute | solution.py:562
  7.0 10.7 %collective-permute-start.1 = (f32[592,128]{1,0:T(8,128)S(1)}, f32[592,128]{1,0:T(8,128)S(1)}, u32[]{:S(2)}, u32[]{:S(2)}) collective-permute-start(f32[592,128]{1,0:T(8,128)S(1)} %get-tuple-element.33), channel_id=1, source_target_pairs={{0,4},{4,8},{8,12},{12,16},{16,20},{20,24},{24,28},{28,0},{1,5},{5... | collective-permute-start | bytes 909320 | tf_op jit(solution)/shard_map/ppermute | solution.py:563
  7.0 10.7 %collective-permute-start.2 = (f32[592,128]{1,0:T(8,128)S(1)}, f32[592,128]{1,0:T(8,128)S(1)}, u32[]{:S(2)}, u32[]{:S(2)}) collective-permute-start(f32[592,128]{1,0:T(8,128)S(1)} %get-tuple-element.34), channel_id=1, source_target_pairs={{4,0},{8,4},{12,8},{16,12},{20,16},{24,20},{28,24},{0,28},{5,1},{9... | collective-permute-start | bytes 909320 | tf_op jit(solution)/shard_map/ppermute | solution.py:564
  9.7 4.7 %collective-permute-start.4 = (f32[16,128]{1,0:T(8,128)S(1)}, f32[16,128]{1,0:T(8,128)S(1)}, u32[]{:S(2)}, u32[]{:S(2)}) collective-permute-start(f32[16,128]{1,0:T(8,128)S(1)} %get-tuple-element.35.refs_5_), channel_id=1, source_target_pairs={{0,2},{1,3},{2,0},{3,1},{4,6},{5,7},{6,4},{7,5},{8,10},{9,11},{10,... | collective-permute-start | bytes 24584 | tf_op jit(solution)/shard_map/ppermute | solution.py:567
  12.3 5.4 %collective-permute-start.3 = (f32[16,128]{1,0:T(8,128)S(1)}, f32[16,128]{1,0:T(8,128)S(1)}, u32[]{:S(2)}, u32[]{:S(2)}) collective-permute-start(f32[16,128]{1,0:T(8,128)S(1)} %get-tuple-element.35.refs_5_), channel_id=1, source_target_pairs={{0,3},{1,2},{2,1},{3,0},{4,7},{5,6},{6,5},{7,4},{8,11},{9,10},{10,... | collective-permute-start | bytes 24584 | tf_op jit(solution)/shard_map/ppermute | solution.py:567
  20.1 9.6 %collective-permute-start.5 = (f32[74,8,128]{2,1,0:T(8,128)S(1)}, f32[74,8,128]{2,1,0:T(8,128)S(1)}, u32[]{:S(2)}, u32[]{:S(2)}) collective-permute-start(f32[74,8,128]{2,1,0:T(8,128)S(1)} %get-tuple-element.39), channel_id=1, source_target_pairs={{0,1},{1,0},{2,3},{3,2},{4,5},{5,4},{6,7},{7,6},{8,9},{9,8},{10,11... | collective-permute-start | bytes 909320 | tf_op jit(solution)/shard_map/ppermute | solution.py:562
  20.2 9.5 %collective-permute-start.6 = (f32[592,128]{1,0:T(8,128)S(1)}, f32[592,128]{1,0:T(8,128)S(1)}, u32[]{:S(2)}, u32[]{:S(2)}) collective-permute-start(f32[592,128]{1,0:T(8,128)S(1)} %get-tuple-element.40), channel_id=1, source_target_pairs={{0,4},{4,8},{8,12},{12,16},{16,20},{20,24},{24,28},{28,0},{1,5},{5... | collective-permute-start | bytes 909320 | tf_op jit(solution)/shard_map/ppermute | solution.py:563
  20.2 9.5 %collective-permute-start.7 = (f32[592,128]{1,0:T(8,128)S(1)}, f32[592,128]{1,0:T(8,128)S(1)}, u32[]{:S(2)}, u32[]{:S(2)}) collective-permute-start(f32[592,128]{1,0:T(8,128)S(1)} %get-tuple-element.41), channel_id=1, source_target_pairs={{4,0},{8,4},{12,8},{16,12},{20,16},{24,20},{28,24},{0,28},{5,1},{9... | collective-permute-start | bytes 909320 | tf_op jit(solution)/shard_map/ppermute | solution.py:564
  22.9 5.5 %collective-permute-start.9 = (f32[16,128]{1,0:T(8,128)S(1)}, f32[16,128]{1,0:T(8,128)S(1)}, u32[]{:S(2)}, u32[]{:S(2)}) collective-permute-start(f32[16,128]{1,0:T(8,128)S(1)} %get-tuple-element.42.refs_5_), channel_id=1, source_target_pairs={{0,2},{1,3},{2,0},{3,1},{4,6},{5,7},{6,4},{7,5},{8,10},{9,11},{10,... | collective-permute-start | bytes 24584 | tf_op jit(solution)/shard_map/ppermute | solution.py:567
  24.0 5.7 %collective-permute-start.8 = (f32[16,128]{1,0:T(8,128)S(1)}, f32[16,128]{1,0:T(8,128)S(1)}, u32[]{:S(2)}, u32[]{:S(2)}) collective-permute-start(f32[16,128]{1,0:T(8,128)S(1)} %get-tuple-element.42.refs_5_), channel_id=1, source_target_pairs={{0,3},{1,2},{2,1},{3,0},{4,7},{5,6},{6,5},{7,4},{8,11},{9,10},{10,... | collective-permute-start | bytes 24584 | tf_op jit(solution)/shard_map/ppermute | solution.py:567
  32.1 11.7 %collective-permute-start.10 = (f32[74,8,128]{2,1,0:T(8,128)S(1)}, f32[74,8,128]{2,1,0:T(8,128)S(1)}, u32[]{:S(2)}, u32[]{:S(2)}) collective-permute-start(f32[74,8,128]{2,1,0:T(8,128)S(1)} %get-tuple-element.44), channel_id=1, source_target_pairs={{0,1},{1,0},{2,3},{3,2},{4,5},{5,4},{6,7},{7,6},{8,9},{9,8},{10,11... | collective-permute-start | bytes 909320 | tf_op jit(solution)/shard_map/ppermute | solution.py:562
  34.0 10.3 %collective-permute-start.11 = (f32[592,128]{1,0:T(8,128)S(1)}, f32[592,128]{1,0:T(8,128)S(1)}, u32[]{:S(2)}, u32[]{:S(2)}) collective-permute-start(f32[592,128]{1,0:T(8,128)S(1)} %get-tuple-element.45), channel_id=1, source_target_pairs={{0,4},{4,8},{8,12},{12,16},{16,20},{20,24},{24,28},{28,0},{1,5},{5... | collective-permute-start | bytes 909320 | tf_op jit(solution)/shard_map/ppermute | solution.py:563
  34.5 9.9 %collective-permute-start.12 = (f32[592,128]{1,0:T(8,128)S(1)}, f32[592,128]{1,0:T(8,128)S(1)}, u32[]{:S(2)}, u32[]{:S(2)}) collective-permute-start(f32[592,128]{1,0:T(8,128)S(1)} %get-tuple-element.46), channel_id=1, source_target_pairs={{4,0},{8,4},{12,8},{16,12},{20,16},{24,20},{28,24},{0,28},{5,1},{9... | collective-permute-start | bytes 909320 | tf_op jit(solution)/shard_map/ppermute | solution.py:564
  36.7 4.9 %collective-permute-start.14 = (f32[16,128]{1,0:T(8,128)S(1)}, f32[16,128]{1,0:T(8,128)S(1)}, u32[]{:S(2)}, u32[]{:S(2)}) collective-permute-start(f32[16,128]{1,0:T(8,128)S(1)} %get-tuple-element.47.refs_5_), channel_id=1, source_target_pairs={{0,2},{1,3},{2,0},{3,1},{4,6},{5,7},{6,4},{7,5},{8,10},{9,11},{10,... | collective-permute-start | bytes 24584 | tf_op jit(solution)/shard_map/ppermute | solution.py:567
  38.3 5.4 %collective-permute-start.13 = (f32[16,128]{1,0:T(8,128)S(1)}, f32[16,128]{1,0:T(8,128)S(1)}, u32[]{:S(2)}, u32[]{:S(2)}) collective-permute-start(f32[16,128]{1,0:T(8,128)S(1)} %get-tuple-element.47.refs_5_), channel_id=1, source_target_pairs={{0,3},{1,2},{2,1},{3,0},{4,7},{5,6},{6,5},{7,4},{8,11},{9,10},{10,... | collective-permute-start | bytes 24584 | tf_op jit(solution)/shard_map/ppermute | solution.py:567
  46.7 10.3 %collective-permute-start.15 = (f32[74,8,128]{2,1,0:T(8,128)S(1)}, f32[74,8,128]{2,1,0:T(8,128)S(1)}, u32[]{:S(2)}, u32[]{:S(2)}) collective-permute-start(f32[74,8,128]{2,1,0:T(8,128)S(1)} %get-tuple-element.49), channel_id=1, source_target_pairs={{0,1},{1,0},{2,3},{3,2},{4,5},{5,4},{6,7},{7,6},{8,9},{9,8},{10,11... | collective-permute-start | bytes 909320 | tf_op jit(solution)/shard_map/ppermute | solution.py:562
  46.8 10.3 %collective-permute-start.16 = (f32[592,128]{1,0:T(8,128)S(1)}, f32[592,128]{1,0:T(8,128)S(1)}, u32[]{:S(2)}, u32[]{:S(2)}) collective-permute-start(f32[592,128]{1,0:T(8,128)S(1)} %get-tuple-element.50), channel_id=1, source_target_pairs={{0,4},{4,8},{8,12},{12,16},{16,20},{20,24},{24,28},{28,0},{1,5},{5... | collective-permute-start | bytes 909320 | tf_op jit(solution)/shard_map/ppermute | solution.py:563
  47.2 9.9 %collective-permute-start.17 = (f32[592,128]{1,0:T(8,128)S(1)}, f32[592,128]{1,0:T(8,128)S(1)}, u32[]{:S(2)}, u32[]{:S(2)}) collective-permute-start(f32[592,128]{1,0:T(8,128)S(1)} %get-tuple-element.51), channel_id=1, source_target_pairs={{4,0},{8,4},{12,8},{16,12},{20,16},{24,20},{28,24},{0,28},{5,1},{9... | collective-permute-start | bytes 909320 | tf_op jit(solution)/shard_map/ppermute | solution.py:564
  49.5 5.5 %collective-permute-start.19 = (f32[16,128]{1,0:T(8,128)S(1)}, f32[16,128]{1,0:T(8,128)S(1)}, u32[]{:S(2)}, u32[]{:S(2)}) collective-permute-start(f32[16,128]{1,0:T(8,128)S(1)} %get-tuple-element.52.refs_5_), channel_id=1, source_target_pairs={{0,2},{1,3},{2,0},{3,1},{4,6},{5,7},{6,4},{7,5},{8,10},{9,11},{10,... | collective-permute-start | bytes 24584 | tf_op jit(solution)/shard_map/ppermute | solution.py:567
  51.6 5.4 %collective-permute-start.18 = (f32[16,128]{1,0:T(8,128)S(1)}, f32[16,128]{1,0:T(8,128)S(1)}, u32[]{:S(2)}, u32[]{:S(2)}) collective-permute-start(f32[16,128]{1,0:T(8,128)S(1)} %get-tuple-element.52.refs_5_), channel_id=1, source_target_pairs={{0,3},{1,2},{2,1},{3,0},{4,7},{5,6},{6,5},{7,4},{8,11},{9,10},{10,... | collective-permute-start | bytes 24584 | tf_op jit(solution)/shard_map/ppermute | solution.py:567

commit v5 on v2

--- a/solution.py
+++ b/solution.py
@@ -239,7 +239,7 @@
                         parts.append(jnp.zeros((PART_X, sz.cells), jnp.float32))
                 turned = jnp.concatenate(parts, axis=0).T
                 t = xg * sz.kg + kg
-                slot = xg % 2
+                slot = xg % 6
                 for x in range(SUB):
                     for part in range(0, Y, SUB):
                         piece = turned[x * Y + part : x * Y + part + SUB, :]
@@ -427,7 +427,7 @@
         for kg in range(sz.kg):
             for xg in range(sz.xg):
                 t = xg * sz.kg + kg
-                slot = xg % 2
+                slot = xg % 6
                 base = sz.base(f, t)
                 for step in range(Y):
                     y = real_row(parity, step)
@@ -469,7 +469,7 @@
     final_shape = jax.ShapeDtypeStruct(distribution.shape, jnp.float32)
     bytes_moved = 2 * distribution.size * 4
     sums_scratch = pltpu.VMEM((FIELDS, sz.cells, LANES), jnp.float32)
-    turn_scratch = pltpu.VMEM((2, sz.cells, LANES), jnp.float32)
+    turn_scratch = pltpu.VMEM((6, sz.cells, LANES), jnp.float32)
     step_scratch = [pltpu.VMEM((FIELDS, sz.cells, LANES), jnp.float32)]
     first_vmem = ALL_VMEM - 26 * distribution.size
     stage = [

time: 60.4 us -> 60.2 us (level)
  no operation moved by 1% of the time
where the time goes in v5:
time: 60.2 us; the launch traced here: 60.1 us
  starting transfers between devices  29.6 us (49%)
  Pallas kernels  19.4 us (32%)
  waiting for transfers between devices  10.9 us (18%)
    ppermute x8, starting transfers between devices, on_device(): lax.ppermute(packet, 'vert', [(s, s ^ mask) for s in range(vert)])  13.7 us
    pallas_call x4, Pallas kernels, on_device(): pl.pallas_call(functools.partial(step_kernel, sz, last), out_shape=(final...  10.4 us
    ppermute x8, waiting for transfers between devices, on_device(): lax.ppermute(packet, 'vert', [(s, s ^ mask) for s in range(vert)])  10.3 us
    ppermute x4, starting transfers between devices, on_device(): left_in = lax.ppermute(left, 'gx', back)  9.85 us
    ppermute x4, starting transfers between devices, on_device(): mirror_in = lax.ppermute(mirror, 'vert', [(s, s ^ 1) for s in range(vert)])  5.23 us
    pallas_call x4, Pallas kernels, on_device(): pl.pallas_call(functools.partial(advect_kernel, sz), out_shape=jax.ShapeD...  4.73 us
    pallas_call x1, Pallas kernels, on_device(): pl.pallas_call(functools.partial(first_kernel, sz), out_shape=shapes(sz),...  3.55 us
  transfers between devices with their start and end apart: 20, of which 6 were waited for; matrix products, arithmetic and copies ran while one was open for 0% of the time, Pallas kernels for 9%

profile of v5, /device:TPU:0, one launch (start us, length us, event | category | flops | bytes accessed | tf_op | source)
XLA Modules:
  0.0 60.1 jit_solution(107171622996367063)
XLA Ops:
  0.0 0.0 copy-start.3
  0.0 0.0 copy-start.2
  0.0 0.0 copy-start.1
  0.0 0.0 copy-start
  0.0 3.5 %first.1 = (f32[4608,128]{1,0:T(8,128)S(1)}, f32[74,8,128]{2,1,0:T(8,128)S(1)}, f32[16,128]{1,0:T(8,128)S(1)}, f32[592,128]{1,0:T(8,128)S(1)}, f32[592,128]{1,0:T(8,128)S(1)}) custom-call(f32[2,24,96,128]{3,2,1,0:T(8,128)} %argument.1), custom_call_target="tpu_custom_call" | custom-call | flops 5898240 | bytes 4718592 | tf_op jit(solution)/shard_map/first/pallas_call | solution.py:479
  3.6 3.1 %collective-permute-start = (f32[74,8,128]{2,1,0:T(8,128)S(1)}, f32[74,8,128]{2,1,0:T(8,128)S(1)}, u32[]{:S(2)}, u32[]{:S(2)}) collective-permute-start(f32[74,8,128]{2,1,0:T(8,128)S(1)} %get-tuple-element.32), channel_id=1, source_target_pairs={{0,1},{1,0},{2,3},{3,2},{4,5},{5,4},{6,7},{7,6},{8,9},{9,8},{10,11... | collective-permute-start | bytes 909320 | tf_op jit(solution)/shard_map/ppermute | solution.py:506
  6.7 0.0 collective-permute-start.1
  6.7 2.6 %collective-permute-start.2 = (f32[592,128]{1,0:T(8,128)S(1)}, f32[592,128]{1,0:T(8,128)S(1)}, u32[]{:S(2)}, u32[]{:S(2)}) collective-permute-start(f32[592,128]{1,0:T(8,128)S(1)} %get-tuple-element.34), channel_id=1, source_target_pairs={{4,0},{8,4},{12,8},{16,12},{20,16},{24,20},{28,24},{0,28},{5,1},{9... | collective-permute-start | bytes 909320 | tf_op jit(solution)/shard_map/ppermute | solution.py:508
  9.3 2.6 %collective-permute-start.4 = (f32[16,128]{1,0:T(8,128)S(1)}, f32[16,128]{1,0:T(8,128)S(1)}, u32[]{:S(2)}, u32[]{:S(2)}) collective-permute-start(f32[16,128]{1,0:T(8,128)S(1)} %get-tuple-element.35.refs_5_), channel_id=1, source_target_pairs={{0,2},{1,3},{2,0},{3,1},{4,6},{5,7},{6,4},{7,5},{8,10},{9,11},{10,... | collective-permute-start | bytes 24584 | tf_op jit(solution)/shard_map/ppermute | solution.py:511
  11.9 0.0 collective-permute-start.3
  11.9 0.0 copy-done.3
  11.9 0.0 copy-done.2
  11.9 0.0 copy-done.1
  11.9 0.0 copy-done
  11.9 0.7 %walls.1 = (f32[1,8,128]{2,1,0:T(8,128)S(1)}, f32[24,8,128]{2,1,0:T(8,128)S(1)}, f32[12,8,128]{2,1,0:T(8,128)S(1)}, f32[36,8,128]{2,1,0:T(8,128)S(1)}) custom-call(s32[2,8]{1,0:T(2,128)S(1)} %copy-done, s32[2,8]{1,0:T(2,128)S(1)} %copy-done.1, f32[2]{0:T(128)S(1)} %copy-done.2, s32[3]{0:T(128)S(1)} %copy-done.3), custom_call_target="tpu_custom_call" | custom-call | tf_op jit(solution)/shard_map/walls/pallas_call | solution.py:491
  12.6 1.3 %advect.4.refs_1_ = f32[4608,128]{1,0:T(8,128)S(1)} custom-call(f32[4608,128]{1,0:T(8,128)S(1)} %get-tuple-element.29.state.refs_0_, f32[24,8,128]{2,1,0:T(8,128)S(1)} %get-tuple-element.30.xw.refs_7_, f32[12,8,128]{2,1,0:T(8,128)S(1)} %get-tuple-element.31.yw.refs_8_), custom_call_target="tpu_custom_call" | custom-call | flops 7077888 | bytes 4718592 | tf_op jit(solution)/shard_map/advect/pallas_call | solution.py:512
  13.9 0.0 collective-permute-done.4.refs_11_
  14.0 3.4 %collective-permute-done.3.refs_10_ = f32[16,128]{1,0:T(8,128)S(1)} collective-permute-done((f32[16,128]{1,0:T(8,128)S(1)}, f32[16,128]{1,0:T(8,128)S(1)}, u32[]{:S(2)}, u32[]{:S(2)}) %collective-permute-start.3) | collective-permute-done | bytes 8224 | tf_op jit(solution)/shard_map/ppermute | solution.py:511
  17.3 0.0 collective-permute-done.refs_2_
  17.4 0.0 collective-permute-done.1.refs_3_
  17.4 0.0 collective-permute-done.2.refs_4_
  17.4 2.4 %step.3 = (f32[4608,128]{1,0:T(8,128)S(1)}, f32[74,8,128]{2,1,0:T(8,128)S(1)}, f32[16,128]{1,0:T(8,128)S(1)}, f32[592,128]{1,0:T(8,128)S(1)}, f32[592,128]{1,0:T(8,128)S(1)}) custom-call(f32[4608,128]{1,0:T(8,128)S(1)} %get-tuple-element.29.state.refs_0_, f32[4608,128]{1,0:T(8,128)S(1)} %advect.4.refs_1_, f32[74,8,128]{2,1,0:T(8,128)S(1)} %collective-permute-done.refs_2_, ...), custom_call_target="tpu_custom_call" | custom-call | flops 23592960 | bytes 4718592 | tf_op jit(solution)/shard_map/step/pallas_call | solution.py:527
  19.7 0.1 collective-permute-start.5
  19.8 0.1 collective-permute-start.6
  19.9 2.6 %collective-permute-start.7 = (f32[592,128]{1,0:T(8,128)S(1)}, f32[592,128]{1,0:T(8,128)S(1)}, u32[]{:S(2)}, u32[]{:S(2)}) collective-permute-start(f32[592,128]{1,0:T(8,128)S(1)} %get-tuple-element.41), channel_id=1, source_target_pairs={{4,0},{8,4},{12,8},{16,12},{20,16},{24,20},{28,24},{0,28},{5,1},{9... | collective-permute-start | bytes 909320 | tf_op jit(solution)/shard_map/ppermute | solution.py:508
  22.5 1.1 %collective-permute-start.9 = (f32[16,128]{1,0:T(8,128)S(1)}, f32[16,128]{1,0:T(8,128)S(1)}, u32[]{:S(2)}, u32[]{:S(2)}) collective-permute-start(f32[16,128]{1,0:T(8,128)S(1)} %get-tuple-element.42.refs_5_), channel_id=1, source_target_pairs={{0,2},{1,3},{2,0},{3,1},{4,6},{5,7},{6,4},{7,5},{8,10},{9,11},{10,... | collective-permute-start | bytes 24584 | tf_op jit(solution)/shard_map/ppermute | solution.py:511
  23.6 3.2 %collective-permute-start.8 = (f32[16,128]{1,0:T(8,128)S(1)}, f32[16,128]{1,0:T(8,128)S(1)}, u32[]{:S(2)}, u32[]{:S(2)}) collective-permute-start(f32[16,128]{1,0:T(8,128)S(1)} %get-tuple-element.42.refs_5_), channel_id=1, source_target_pairs={{0,3},{1,2},{2,1},{3,0},{4,7},{5,6},{6,5},{7,4},{8,11},{9,10},{10,... | collective-permute-start | bytes 24584 | tf_op jit(solution)/shard_map/ppermute | solution.py:511
  26.8 1.1 %advect.5.refs_1_ = f32[4608,128]{1,0:T(8,128)S(1)} custom-call(f32[4608,128]{1,0:T(8,128)S(1)} %get-tuple-element.38.state.refs_0_, f32[24,8,128]{2,1,0:T(8,128)S(1)} %get-tuple-element.30.xw.refs_7_, f32[12,8,128]{2,1,0:T(8,128)S(1)} %get-tuple-element.31.yw.refs_8_), custom_call_target="tpu_custom_call" | custom-call | flops 7077888 | bytes 4718592 | tf_op jit(solution)/shard_map/advect/pallas_call | solution.py:512
  28.0 0.0 collective-permute-done.9.refs_11_
  28.0 1.3 %collective-permute-done.8.refs_10_ = f32[16,128]{1,0:T(8,128)S(1)} collective-permute-done((f32[16,128]{1,0:T(8,128)S(1)}, f32[16,128]{1,0:T(8,128)S(1)}, u32[]{:S(2)}, u32[]{:S(2)}) %collective-permute-start.8) | collective-permute-done | bytes 8224 | tf_op jit(solution)/shard_map/ppermute | solution.py:511
  29.3 0.0 collective-permute-done.5.refs_2_
  29.3 0.0 collective-permute-done.6.refs_3_
  29.3 0.0 collective-permute-done.7.refs_4_
  29.3 2.4 %step.4 = (f32[4608,128]{1,0:T(8,128)S(1)}, f32[74,8,128]{2,1,0:T(8,128)S(1)}, f32[16,128]{1,0:T(8,128)S(1)}, f32[592,128]{1,0:T(8,128)S(1)}, f32[592,128]{1,0:T(8,128)S(1)}) custom-call(f32[4608,128]{1,0:T(8,128)S(1)} %get-tuple-element.38.state.refs_0_, f32[4608,128]{1,0:T(8,128)S(1)} %advect.5.refs_1_, f32[74,8,128]{2,1,0:T(8,128)S(1)} %collective-permute-done.5.refs_2_, ...), custom_call_target="tpu_custom_call" | custom-call | flops 23592960 | bytes 4718592 | tf_op jit(solution)/shard_map/step/pallas_call | solution.py:527
  31.7 2.0 %collective-permute-start.10 = (f32[74,8,128]{2,1,0:T(8,128)S(1)}, f32[74,8,128]{2,1,0:T(8,128)S(1)}, u32[]{:S(2)}, u32[]{:S(2)}) collective-permute-start(f32[74,8,128]{2,1,0:T(8,128)S(1)} %get-tuple-element.44), channel_id=1, source_target_pairs={{0,1},{1,0},{2,3},{3,2},{4,5},{5,4},{6,7},{7,6},{8,9},{9,8},{10,11... | collective-permute-start | bytes 909320 | tf_op jit(solution)/shard_map/ppermute | solution.py:506
  33.7 0.4 collective-permute-start.11
  34.1 2.2 %collective-permute-start.12 = (f32[592,128]{1,0:T(8,128)S(1)}, f32[592,128]{1,0:T(8,128)S(1)}, u32[]{:S(2)}, u32[]{:S(2)}) collective-permute-start(f32[592,128]{1,0:T(8,128)S(1)} %get-tuple-element.46), channel_id=1, source_target_pairs={{4,0},{8,4},{12,8},{16,12},{20,16},{24,20},{28,24},{0,28},{5,1},{9... | collective-permute-start | bytes 909320 | tf_op jit(solution)/shard_map/ppermute | solution.py:508
  36.3 1.6 %collective-permute-start.14 = (f32[16,128]{1,0:T(8,128)S(1)}, f32[16,128]{1,0:T(8,128)S(1)}, u32[]{:S(2)}, u32[]{:S(2)}) collective-permute-start(f32[16,128]{1,0:T(8,128)S(1)} %get-tuple-element.47.refs_5_), channel_id=1, source_target_pairs={{0,2},{1,3},{2,0},{3,1},{4,6},{5,7},{6,4},{7,5},{8,10},{9,11},{10,... | collective-permute-start | bytes 24584 | tf_op jit(solution)/shard_map/ppermute | solution.py:511
  37.9 0.9 %collective-permute-start.13 = (f32[16,128]{1,0:T(8,128)S(1)}, f32[16,128]{1,0:T(8,128)S(1)}, u32[]{:S(2)}, u32[]{:S(2)}) collective-permute-start(f32[16,128]{1,0:T(8,128)S(1)} %get-tuple-element.47.refs_5_), channel_id=1, source_target_pairs={{0,3},{1,2},{2,1},{3,0},{4,7},{5,6},{6,5},{7,4},{8,11},{9,10},{10,... | collective-permute-start | bytes 24584 | tf_op jit(solution)/shard_map/ppermute | solution.py:511
  38.8 1.1 %advect.6.refs_1_ = f32[4608,128]{1,0:T(8,128)S(1)} custom-call(f32[4608,128]{1,0:T(8,128)S(1)} %get-tuple-element.43.state.refs_0_, f32[24,8,128]{2,1,0:T(8,128)S(1)} %get-tuple-element.30.xw.refs_7_, f32[12,8,128]{2,1,0:T(8,128)S(1)} %get-tuple-element.31.yw.refs_8_), custom_call_target="tpu_custom_call" | custom-call | flops 7077888 | bytes 4718592 | tf_op jit(solution)/shard_map/advect/pallas_call | solution.py:512
  40.0 1.3 %collective-permute-done.14.refs_11_ = f32[16,128]{1,0:T(8,128)S(1)} collective-permute-done((f32[16,128]{1,0:T(8,128)S(1)}, f32[16,128]{1,0:T(8,128)S(1)}, u32[]{:S(2)}, u32[]{:S(2)}) %collective-permute-start.14) | collective-permute-done | bytes 8224 | tf_op jit(solution)/shard_map/ppermute | solution.py:511
  41.2 2.1 %collective-permute-done.13.refs_10_ = f32[16,128]{1,0:T(8,128)S(1)} collective-permute-done((f32[16,128]{1,0:T(8,128)S(1)}, f32[16,128]{1,0:T(8,128)S(1)}, u32[]{:S(2)}, u32[]{:S(2)}) %collective-permute-start.13) | collective-permute-done | bytes 8224 | tf_op jit(solution)/shard_map/ppermute | solution.py:511
  43.4 0.0 collective-permute-done.10.refs_2_
  43.4 0.6 %collective-permute-done.11.refs_3_ = f32[592,128]{1,0:T(8,128)S(1)} collective-permute-done((f32[592,128]{1,0:T(8,128)S(1)}, f32[592,128]{1,0:T(8,128)S(1)}, u32[]{:S(2)}, u32[]{:S(2)}) %collective-permute-start.11) | collective-permute-done | bytes 303136 | tf_op jit(solution)/shard_map/ppermute | solution.py:507
  44.0 0.0 collective-permute-done.12.refs_4_
  44.0 2.4 %step.5 = (f32[4608,128]{1,0:T(8,128)S(1)}, f32[74,8,128]{2,1,0:T(8,128)S(1)}, f32[16,128]{1,0:T(8,128)S(1)}, f32[592,128]{1,0:T(8,128)S(1)}, f32[592,128]{1,0:T(8,128)S(1)}) custom-call(f32[4608,128]{1,0:T(8,128)S(1)} %get-tuple-element.43.state.refs_0_, f32[4608,128]{1,0:T(8,128)S(1)} %advect.6.refs_1_, f32[74,8,128]{2,1,0:T(8,128)S(1)} %collective-permute-done.10.refs_2_, ...), custom_call_target="tpu_custom_call" | custom-call | flops 23592960 | bytes 4718592 | tf_op jit(solution)/shard_map/step/pallas_call | solution.py:527
  46.4 0.1 collective-permute-start.15
  46.5 0.4 collective-permute-start.16
  46.8 2.3 %collective-permute-start.17 = (f32[592,128]{1,0:T(8,128)S(1)}, f32[592,128]{1,0:T(8,128)S(1)}, u32[]{:S(2)}, u32[]{:S(2)}) collective-permute-start(f32[592,128]{1,0:T(8,128)S(1)} %get-tuple-element.51), channel_id=1, source_target_pairs={{4,0},{8,4},{12,8},{16,12},{20,16},{24,20},{28,24},{0,28},{5,1},{9... | collective-permute-start | bytes 909320 | tf_op jit(solution)/shard_map/ppermute | solution.py:508
  49.1 2.1 %collective-permute-start.19 = (f32[16,128]{1,0:T(8,128)S(1)}, f32[16,128]{1,0:T(8,128)S(1)}, u32[]{:S(2)}, u32[]{:S(2)}) collective-permute-start(f32[16,128]{1,0:T(8,128)S(1)} %get-tuple-element.52.refs_5_), channel_id=1, source_target_pairs={{0,2},{1,3},{2,0},{3,1},{4,6},{5,7},{6,4},{7,5},{8,10},{9,11},{10,... | collective-permute-start | bytes 24584 | tf_op jit(solution)/shard_map/ppermute | solution.py:511
  51.3 2.2 %collective-permute-start.18 = (f32[16,128]{1,0:T(8,128)S(1)}, f32[16,128]{1,0:T(8,128)S(1)}, u32[]{:S(2)}, u32[]{:S(2)}) collective-permute-start(f32[16,128]{1,0:T(8,128)S(1)} %get-tuple-element.52.refs_5_), channel_id=1, source_target_pairs={{0,3},{1,2},{2,1},{3,0},{4,7},{5,6},{6,5},{7,4},{8,11},{9,10},{10,... | collective-permute-start | bytes 24584 | tf_op jit(solution)/shard_map/ppermute | solution.py:511
  53.5 1.1 %advect.7.refs_1_ = f32[4608,128]{1,0:T(8,128)S(1)} custom-call(f32[4608,128]{1,0:T(8,128)S(1)} %get-tuple-element.48.state.refs_0_, f32[24,8,128]{2,1,0:T(8,128)S(1)} %get-tuple-element.30.xw.refs_7_, f32[12,8,128]{2,1,0:T(8,128)S(1)} %get-tuple-element.31.yw.refs_8_), custom_call_target="tpu_custom_call" | custom-call | flops 7077888 | bytes 4718592 | tf_op jit(solution)/shard_map/advect/pallas_call | solution.py:512
  54.6 0.0 collective-permute-done.19.refs_11_
  54.6 2.1 %collective-permute-done.18.refs_10_ = f32[16,128]{1,0:T(8,128)S(1)} collective-permute-done((f32[16,128]{1,0:T(8,128)S(1)}, f32[16,128]{1,0:T(8,128)S(1)}, u32[]{:S(2)}, u32[]{:S(2)}) %collective-permute-start.18) | collective-permute-done | bytes 8224 | tf_op jit(solution)/shard_map/ppermute | solution.py:511
  56.7 0.0 collective-permute-done.15.refs_2_
  56.7 0.0 collective-permute-done.16.refs_3_
  56.7 0.0 collective-permute-done.17.refs_4_
  56.7 3.4 %last.1 = f32[2,24,96,128]{3,2,1,0:T(8,128)} custom-call(f32[4608,128]{1,0:T(8,128)S(1)} %get-tuple-element.48.state.refs_0_, f32[4608,128]{1,0:T(8,128)S(1)} %advect.7.refs_1_, f32[74,8,128]{2,1,0:T(8,128)S(1)} %collective-permute-done.15.refs_2_, f32[592,128]{1,0:T(8,128)S(1)} %collective-permute-done.16.refs_3_, ...), custom_call_target="tpu_custom_call" | custom-call | flops 23592960 | bytes 4718592 | tf_op jit(solution)/shard_map/last/pallas_call | solution.py:527
Async XLA Ops:
  0.0 11.9 %copy-start.3 = (s32[3]{0:T(128)S(1)}, s32[3]{0:T(128)}, u32[]{:S(2)}) copy-start(s32[3]{0:T(128)} %acc_ref.1) | copy-start | bytes 40
  0.0 11.9 %copy-start.2 = (f32[2]{0:T(128)S(1)}, f32[2]{0:T(128)}, u32[]{:S(2)}) copy-start(f32[2]{0:T(128)} %temps_ref.1) | copy-start | bytes 28
  0.0 11.9 %copy-start.1 = (s32[2,8]{1,0:T(2,128)S(1)}, s32[2,8]{1,0:T(2,128)}, u32[]{:S(2)}) copy-start(s32[2,8]{1,0:T(2,128)} %index_ref.1) | copy-start | bytes 196
  0.0 11.9 %copy-start = (s32[2,8]{1,0:T(2,128)S(1)}, s32[2,8]{1,0:T(2,128)}, u32[]{:S(2)}) copy-start(s32[2,8]{1,0:T(2,128)} %type_ref.1) | copy-start | bytes 196
  3.6 13.8 %collective-permute-start = (f32[74,8,128]{2,1,0:T(8,128)S(1)}, f32[74,8,128]{2,1,0:T(8,128)S(1)}, u32[]{:S(2)}, u32[]{:S(2)}) collective-permute-start(f32[74,8,128]{2,1,0:T(8,128)S(1)} %get-tuple-element.32), channel_id=1, source_target_pairs={{0,1},{1,0},{2,3},{3,2},{4,5},{5,4},{6,7},{7,6},{8,9},{9,8},{10,11... | collective-permute-start | bytes 909320 | tf_op jit(solution)/shard_map/ppermute | solution.py:506
  6.7 10.7 %collective-permute-start.1 = (f32[592,128]{1,0:T(8,128)S(1)}, f32[592,128]{1,0:T(8,128)S(1)}, u32[]{:S(2)}, u32[]{:S(2)}) collective-permute-start(f32[592,128]{1,0:T(8,128)S(1)} %get-tuple-element.33), channel_id=1, source_target_pairs={{0,4},{4,8},{8,12},{12,16},{16,20},{20,24},{24,28},{28,0},{1,5},{5... | collective-permute-start | bytes 909320 | tf_op jit(solution)/shard_map/ppermute | solution.py:507
  6.7 10.7 %collective-permute-start.2 = (f32[592,128]{1,0:T(8,128)S(1)}, f32[592,128]{1,0:T(8,128)S(1)}, u32[]{:S(2)}, u32[]{:S(2)}) collective-permute-start(f32[592,128]{1,0:T(8,128)S(1)} %get-tuple-element.34), channel_id=1, source_target_pairs={{4,0},{8,4},{12,8},{16,12},{20,16},{24,20},{28,24},{0,28},{5,1},{9... | collective-permute-start | bytes 909320 | tf_op jit(solution)/shard_map/ppermute | solution.py:508
  9.3 4.7 %collective-permute-start.4 = (f32[16,128]{1,0:T(8,128)S(1)}, f32[16,128]{1,0:T(8,128)S(1)}, u32[]{:S(2)}, u32[]{:S(2)}) collective-permute-start(f32[16,128]{1,0:T(8,128)S(1)} %get-tuple-element.35.refs_5_), channel_id=1, source_target_pairs={{0,2},{1,3},{2,0},{3,1},{4,6},{5,7},{6,4},{7,5},{8,10},{9,11},{10,... | collective-permute-start | bytes 24584 | tf_op jit(solution)/shard_map/ppermute | solution.py:511
  11.9 5.4 %collective-permute-start.3 = (f32[16,128]{1,0:T(8,128)S(1)}, f32[16,128]{1,0:T(8,128)S(1)}, u32[]{:S(2)}, u32[]{:S(2)}) collective-permute-start(f32[16,128]{1,0:T(8,128)S(1)} %get-tuple-element.35.refs_5_), channel_id=1, source_target_pairs={{0,3},{1,2},{2,1},{3,0},{4,7},{5,6},{6,5},{7,4},{8,11},{9,10},{10,... | collective-permute-start | bytes 24584 | tf_op jit(solution)/shard_map/ppermute | solution.py:511
  19.7 9.6 %collective-permute-start.5 = (f32[74,8,128]{2,1,0:T(8,128)S(1)}, f32[74,8,128]{2,1,0:T(8,128)S(1)}, u32[]{:S(2)}, u32[]{:S(2)}) collective-permute-start(f32[74,8,128]{2,1,0:T(8,128)S(1)} %get-tuple-element.39), channel_id=1, source_target_pairs={{0,1},{1,0},{2,3},{3,2},{4,5},{5,4},{6,7},{7,6},{8,9},{9,8},{10,11... | collective-permute-start | bytes 909320 | tf_op jit(solution)/shard_map/ppermute | solution.py:506
  19.8 9.5 %collective-permute-start.6 = (f32[592,128]{1,0:T(8,128)S(1)}, f32[592,128]{1,0:T(8,128)S(1)}, u32[]{:S(2)}, u32[]{:S(2)}) collective-permute-start(f32[592,128]{1,0:T(8,128)S(1)} %get-tuple-element.40), channel_id=1, source_target_pairs={{0,4},{4,8},{8,12},{12,16},{16,20},{20,24},{24,28},{28,0},{1,5},{5... | collective-permute-start | bytes 909320 | tf_op jit(solution)/shard_map/ppermute | solution.py:507
  19.9 9.5 %collective-permute-start.7 = (f32[592,128]{1,0:T(8,128)S(1)}, f32[592,128]{1,0:T(8,128)S(1)}, u32[]{:S(2)}, u32[]{:S(2)}) collective-permute-start(f32[592,128]{1,0:T(8,128)S(1)} %get-tuple-element.41), channel_id=1, source_target_pairs={{4,0},{8,4},{12,8},{16,12},{20,16},{24,20},{28,24},{0,28},{5,1},{9... | collective-permute-start | bytes 909320 | tf_op jit(solution)/shard_map/ppermute | solution.py:508
  22.5 5.5 %collective-permute-start.9 = (f32[16,128]{1,0:T(8,128)S(1)}, f32[16,128]{1,0:T(8,128)S(1)}, u32[]{:S(2)}, u32[]{:S(2)}) collective-permute-start(f32[16,128]{1,0:T(8,128)S(1)} %get-tuple-element.42.refs_5_), channel_id=1, source_target_pairs={{0,2},{1,3},{2,0},{3,1},{4,6},{5,7},{6,4},{7,5},{8,10},{9,11},{10,... | collective-permute-start | bytes 24584 | tf_op jit(solution)/shard_map/ppermute | solution.py:511
  23.6 5.7 %collective-permute-start.8 = (f32[16,128]{1,0:T(8,128)S(1)}, f32[16,128]{1,0:T(8,128)S(1)}, u32[]{:S(2)}, u32[]{:S(2)}) collective-permute-start(f32[16,128]{1,0:T(8,128)S(1)} %get-tuple-element.42.refs_5_), channel_id=1, source_target_pairs={{0,3},{1,2},{2,1},{3,0},{4,7},{5,6},{6,5},{7,4},{8,11},{9,10},{10,... | collective-permute-start | bytes 24584 | tf_op jit(solution)/shard_map/ppermute | solution.py:511
  31.7 11.7 %collective-permute-start.10 = (f32[74,8,128]{2,1,0:T(8,128)S(1)}, f32[74,8,128]{2,1,0:T(8,128)S(1)}, u32[]{:S(2)}, u32[]{:S(2)}) collective-permute-start(f32[74,8,128]{2,1,0:T(8,128)S(1)} %get-tuple-element.44), channel_id=1, source_target_pairs={{0,1},{1,0},{2,3},{3,2},{4,5},{5,4},{6,7},{7,6},{8,9},{9,8},{10,11... | collective-permute-start | bytes 909320 | tf_op jit(solution)/shard_map/ppermute | solution.py:506
  33.7 10.3 %collective-permute-start.11 = (f32[592,128]{1,0:T(8,128)S(1)}, f32[592,128]{1,0:T(8,128)S(1)}, u32[]{:S(2)}, u32[]{:S(2)}) collective-permute-start(f32[592,128]{1,0:T(8,128)S(1)} %get-tuple-element.45), channel_id=1, source_target_pairs={{0,4},{4,8},{8,12},{12,16},{16,20},{20,24},{24,28},{28,0},{1,5},{5... | collective-permute-start | bytes 909320 | tf_op jit(solution)/shard_map/ppermute | solution.py:507
  34.1 9.9 %collective-permute-start.12 = (f32[592,128]{1,0:T(8,128)S(1)}, f32[592,128]{1,0:T(8,128)S(1)}, u32[]{:S(2)}, u32[]{:S(2)}) collective-permute-start(f32[592,128]{1,0:T(8,128)S(1)} %get-tuple-element.46), channel_id=1, source_target_pairs={{4,0},{8,4},{12,8},{16,12},{20,16},{24,20},{28,24},{0,28},{5,1},{9... | collective-permute-start | bytes 909320 | tf_op jit(solution)/shard_map/ppermute | solution.py:508
  36.3 4.9 %collective-permute-start.14 = (f32[16,128]{1,0:T(8,128)S(1)}, f32[16,128]{1,0:T(8,128)S(1)}, u32[]{:S(2)}, u32[]{:S(2)}) collective-permute-start(f32[16,128]{1,0:T(8,128)S(1)} %get-tuple-element.47.refs_5_), channel_id=1, source_target_pairs={{0,2},{1,3},{2,0},{3,1},{4,6},{5,7},{6,4},{7,5},{8,10},{9,11},{10,... | collective-permute-start | bytes 24584 | tf_op jit(solution)/shard_map/ppermute | solution.py:511
  37.9 5.4 %collective-permute-start.13 = (f32[16,128]{1,0:T(8,128)S(1)}, f32[16,128]{1,0:T(8,128)S(1)}, u32[]{:S(2)}, u32[]{:S(2)}) collective-permute-start(f32[16,128]{1,0:T(8,128)S(1)} %get-tuple-element.47.refs_5_), channel_id=1, source_target_pairs={{0,3},{1,2},{2,1},{3,0},{4,7},{5,6},{6,5},{7,4},{8,11},{9,10},{10,... | collective-permute-start | bytes 24584 | tf_op jit(solution)/shard_map/ppermute | solution.py:511
  46.4 10.3 %collective-permute-start.15 = (f32[74,8,128]{2,1,0:T(8,128)S(1)}, f32[74,8,128]{2,1,0:T(8,128)S(1)}, u32[]{:S(2)}, u32[]{:S(2)}) collective-permute-start(f32[74,8,128]{2,1,0:T(8,128)S(1)} %get-tuple-element.49), channel_id=1, source_target_pairs={{0,1},{1,0},{2,3},{3,2},{4,5},{5,4},{6,7},{7,6},{8,9},{9,8},{10,11... | collective-permute-start | bytes 909320 | tf_op jit(solution)/shard_map/ppermute | solution.py:506
  46.5 10.3 %collective-permute-start.16 = (f32[592,128]{1,0:T(8,128)S(1)}, f32[592,128]{1,0:T(8,128)S(1)}, u32[]{:S(2)}, u32[]{:S(2)}) collective-permute-start(f32[592,128]{1,0:T(8,128)S(1)} %get-tuple-element.50), channel_id=1, source_target_pairs={{0,4},{4,8},{8,12},{12,16},{16,20},{20,24},{24,28},{28,0},{1,5},{5... | collective-permute-start | bytes 909320 | tf_op jit(solution)/shard_map/ppermute | solution.py:507
  46.8 9.9 %collective-permute-start.17 = (f32[592,128]{1,0:T(8,128)S(1)}, f32[592,128]{1,0:T(8,128)S(1)}, u32[]{:S(2)}, u32[]{:S(2)}) collective-permute-start(f32[592,128]{1,0:T(8,128)S(1)} %get-tuple-element.51), channel_id=1, source_target_pairs={{4,0},{8,4},{12,8},{16,12},{20,16},{24,20},{28,24},{0,28},{5,1},{9... | collective-permute-start | bytes 909320 | tf_op jit(solution)/shard_map/ppermute | solution.py:508
  49.1 5.5 %collective-permute-start.19 = (f32[16,128]{1,0:T(8,128)S(1)}, f32[16,128]{1,0:T(8,128)S(1)}, u32[]{:S(2)}, u32[]{:S(2)}) collective-permute-start(f32[16,128]{1,0:T(8,128)S(1)} %get-tuple-element.52.refs_5_), channel_id=1, source_target_pairs={{0,2},{1,3},{2,0},{3,1},{4,6},{5,7},{6,4},{7,5},{8,10},{9,11},{10,... | collective-permute-start | bytes 24584 | tf_op jit(solution)/shard_map/ppermute | solution.py:511
  51.3 5.4 %collective-permute-start.18 = (f32[16,128]{1,0:T(8,128)S(1)}, f32[16,128]{1,0:T(8,128)S(1)}, u32[]{:S(2)}, u32[]{:S(2)}) collective-permute-start(f32[16,128]{1,0:T(8,128)S(1)} %get-tuple-element.52.refs_5_), channel_id=1, source_target_pairs={{0,3},{1,2},{2,1},{3,0},{4,7},{5,6},{6,5},{7,4},{8,11},{9,10},{10,... | collective-permute-start | bytes 24584 | tf_op jit(solution)/shard_map/ppermute | solution.py:511
